TPU v7x, 32 devices: a whole 2x2x4 slice. The times are simulated.
32 devices in a mesh: pipe: 4 (over x, core), ctx: 8 (over z, y).
Axes of the slice: x: 2, y: 2, z: 4, core: 2. Of those that a mesh axis runs over, the one named last changes fastest.
Arguments:
- features: bfloat16 [4, 1024, 4096], P('pipe', 'ctx'), may hold values from -6 to 6
- state_maps: bfloat16 [4, 1024, 256], P('pipe', 'ctx'), may hold values from -6 to 6
- step_raw: bfloat16 [4, 1024, 64], P('pipe', 'ctx'), may hold values from -6 to 6
- conv_weight: float32 [4, 4, 4352], P('pipe'), may hold values from -3 to 3
- conv_bias: float32 [4, 4352], P('pipe'), may hold values from -3 to 3
- decay_log: float32 [4, 64], P('pipe'), may hold values from -12 to 0
- step_bias: float32 [4, 64], P('pipe'), may hold values from -4 to -2
- skip_gain: float32 [4, 64], P('pipe'), may hold values from 0.5 to 1.5
- output_grads: bfloat16 [4, 1024, 4096], P('pipe', 'ctx'), may hold values from -6 to 6
Outputs:
- feature_grads: bfloat16 [4, 1024, 4096], P('pipe', 'ctx')
- map_grads: bfloat16 [4, 1024, 256], P('pipe', 'ctx')
- step_grads: bfloat16 [4, 1024, 64], P('pipe', 'ctx')
All inputs are finite; a program needn't handle non-finite values.
Results may differ from a plain program's by a relative error of at most 0.001.
Values may be sent and summed in bfloat16 or wider, within the bound.
No kernel may reach another device: no remote copies, remote signals or barrier semaphores. Data moves between devices by JAX's collectives and lax.ppermute only.
A program may use at most 128 MiB of HBM per device.

v0:
```python
import jax
import jax.numpy as jnp
from jax import lax
from jax.sharding import PartitionSpec as P

BLOCK = 128


def shifted(block, axis, distance):
    devices = range(lax.axis_size(axis))
    route = [((i - distance) % len(devices), i) for i in devices]
    return lax.ppermute(block, axis, route)


def conv_silu(padded, weight, bias):
    taps = weight.shape[0]
    length = padded.shape[0] - taps + 1
    total = jnp.broadcast_to(bias[None, :], (length, bias.shape[0]))
    for offset in range(taps):
        first = taps - 1 - offset
        total = total + weight[offset][None, :] * padded[first : first + length]
    return jax.nn.silu(total)


def ssd_forward(x_conv, steps, rates, b_rows, c_rows, skips, initial, block):
    length, heads, head_dim = x_conv.shape
    blocks = length // block
    highest = lax.Precision.HIGHEST
    log_decay = (steps * rates[None, :]).reshape(blocks, block, heads)
    cumulative = jnp.cumsum(log_decay, axis=1)
    scaled = (x_conv * steps[:, :, None]).reshape(blocks, block, heads, head_dim)
    b_block = b_rows.reshape(blocks, block, -1)
    c_block = c_rows.reshape(blocks, block, -1)
    scores = jnp.einsum("cqn,ckn->cqk", c_block, b_block, precision=highest)
    causal = (jnp.arange(block)[:, None] >= jnp.arange(block)[None, :])[None, :, :, None]
    spread = cumulative[:, :, None, :] - cumulative[:, None, :, :]
    within = jnp.where(causal, jnp.exp(jnp.where(causal, spread, 0.0)), 0.0)
    mixing = scores[:, :, :, None] * within
    y_within = jnp.einsum("cqkh,ckhp->cqhp", mixing, scaled, precision=highest)
    to_end = jnp.exp(cumulative[:, -1:, :] - cumulative)
    weighted = scaled * to_end[:, :, :, None]
    states = jnp.einsum("ckn,ckhp->chpn", b_block, weighted, precision=highest)
    totals = cumulative[:, -1, :]
    running = jnp.cumsum(totals, axis=0)
    before_sum = running - totals
    earlier = (jnp.arange(blocks)[None, :] < jnp.arange(blocks)[:, None])[:, :, None]
    carry_decay = jnp.where(
        earlier, jnp.exp(jnp.where(earlier, before_sum[:, None, :] - running[None, :, :], 0.0)), 0.0
    )
    entering = jnp.einsum("cdh,dhpn->chpn", carry_decay, states, precision=highest)
    entering = entering + jnp.exp(before_sum)[:, :, None, None] * initial[None]
    y_across = jnp.einsum("cqn,chpn->cqhp", c_block, entering, precision=highest)
    y_across = y_across * jnp.exp(cumulative)[:, :, :, None]
    outputs = (y_within + y_across).reshape(length, heads, head_dim) + skips[None, :, None] * x_conv
    last_sum = running[-1]
    final = jnp.exp(last_sum)[:, None, None] * initial
    final = final + jnp.einsum(
        "dh,dhpn->hpn", jnp.exp(last_sum[None, :] - running), states, precision=highest
    )
    return (outputs, final, jnp.exp(last_sum))


def per_device(
    features,
    state_maps,
    step_raw,
    conv_weight,
    conv_bias,
    decay_log,
    step_bias,
    skip_gain,
    output_grads,
):
    incoming = shifted(output_grads, "pipe", -1)
    weight = conv_weight[0]
    bias = conv_bias[0]
    inner = features.shape[2]
    state = state_maps.shape[2] // 2
    heads = decay_log.shape[1]
    head_dim = inner // heads
    taps = weight.shape[0]
    rates = -jnp.exp(decay_log[0])
    offsets = step_bias[0]
    skips = skip_gain[0]
    moved_f, moved_grad, moved_step = (
        lax.all_to_all(features, "ctx", split_axis=2, concat_axis=1, tiled=True),
        lax.all_to_all(incoming, "ctx", split_axis=2, concat_axis=1, tiled=True),
        lax.all_to_all(step_raw, "ctx", split_axis=2, concat_axis=1, tiled=True),
    )
    whole_maps = lax.all_gather(state_maps, "ctx", axis=1, tiled=True)
    local_heads = heads // lax.axis_size("ctx")
    width = local_heads * head_dim
    rank = lax.axis_index("ctx")
    head_start = rank * local_heads
    weight_local = jnp.concatenate(
        [lax.dynamic_slice_in_dim(weight[:, :inner], rank * width, width, 1), weight[:, inner:]],
        axis=1,
    )
    bias_local = jnp.concatenate(
        [lax.dynamic_slice_in_dim(bias[:inner], rank * width, width, 0), bias[inner:]], axis=0
    )
    rates_local = lax.dynamic_slice_in_dim(rates, head_start, local_heads, 0)
    offsets_local = lax.dynamic_slice_in_dim(offsets, head_start, local_heads, 0)
    skips_local = lax.dynamic_slice_in_dim(skips, head_start, local_heads, 0)
    length = moved_f.shape[1]

    def forward(feature_rows, map_rows, step_rows):
        joined = jnp.concatenate([feature_rows, map_rows], axis=1)
        padded = jnp.concatenate(
            [jnp.zeros((taps - 1, joined.shape[1]), jnp.float32), joined], axis=0
        )
        conv_out = conv_silu(padded, weight_local, bias_local)
        x_conv = conv_out[:, :width].reshape(length, local_heads, head_dim)
        steps = jax.nn.softplus(step_rows + offsets_local[None, :])
        initial = jnp.zeros((local_heads, head_dim, state), jnp.float32)
        outputs, final, decay = ssd_forward(
            x_conv,
            steps,
            rates_local,
            conv_out[:, width : width + state],
            conv_out[:, width + state :],
            skips_local,
            initial,
            BLOCK,
        )
        return outputs

    primal, pull = jax.vjp(
        forward,
        moved_f[0].astype(jnp.float32),
        whole_maps[0].astype(jnp.float32),
        moved_step[0].astype(jnp.float32),
    )
    grad_feature, grad_map, grad_step = pull(
        moved_grad[0].astype(jnp.float32).reshape(length, local_heads, head_dim)
    )
    feature_grads, step_grads = (
        lax.all_to_all(
            grad_feature.astype(jnp.bfloat16)[None], "ctx", split_axis=1, concat_axis=2, tiled=True
        ),
        lax.all_to_all(
            grad_step.astype(jnp.bfloat16)[None], "ctx", split_axis=1, concat_axis=2, tiled=True
        ),
    )
    map_total = lax.psum_scatter(grad_map[None], "ctx", scatter_dimension=1, tiled=True)
    return (feature_grads, map_total.astype(jnp.bfloat16), step_grads)


def solution(mesh):
    return jax.shard_map(
        per_device,
        mesh=mesh,
        in_specs=(
            P("pipe", "ctx", None),
            P("pipe", "ctx", None),
            P("pipe", "ctx", None),
            P("pipe", None, None),
            P("pipe", None),
            P("pipe", None),
            P("pipe", None),
            P("pipe", None),
            P("pipe", "ctx", None),
        ),
        out_specs=(P("pipe", "ctx", None), P("pipe", "ctx", None), P("pipe", "ctx", None)),
        check_vma=False,
    )
```

profile of v0, /device:TPU:0, one launch (start us, length us, event | category | flops | bytes accessed | tf_op | source)
XLA Modules:
  0.0 375.5 jit_solution(7831362978823182095)
XLA Ops:
  9.8 7.3 %all-to-all-start.1 = ((bf16[8,2,512]{2,1,0:T(2,128)(2,1)}), bf16[8,2,512]{2,1,0:T(2,128)(2,1)S(1)}, u32[]{:S(2)}, u32[]{:S(2)}) async-start(bf16[8,2,512]{2,1,0:T(2,128)(2,1)} %reshape.371), calls=%async_computation.1 | async-start | bytes 32768 | tf_op jit(solution)/shard_map/all_to_all | solution.py:88
  19.2 5.0 %copy.211 = bf16[1,128,4096]{1,0,2:T(2,128)(2,1)S(1)} copy(bf16[1,128,4096]{2,1,0:T(8,128)(2,1)} %param.9) | data formatting | bytes 2097152 | tf_op args[0]
  24.3 22.4 %reduce.8 = bf16[4096,128]{1,0:T(8,128)(2,1)S(1)} reduce(bf16[4096,1,128]{2,1,0:T(2,128)(2,1)S(1)} %bitcast.212, bf16[]{:T(256)} %broadcast.167), dimensions={1}, to_apply=%bitcast.159.reduce_sub_computation | reduce | bytes 2097154
  47.8 5.7 %all-to-all-start.2 = ((bf16[8,2,32768]{2,1,0:T(2,128)(2,1)}), bf16[8,2,32768]{2,1,0:T(2,128)(2,1)}, u32[]{:S(2)}, u32[]{:S(2)}) async-start(bf16[8,2,32768]{2,1,0:T(2,128)(2,1)} %reshape.369), calls=%async_computation.2 | async-start | bytes 2097152 | tf_op jit(solution)/shard_map/all_to_all | solution.py:86
  54.7 48.6 %all_gather.3 = bf16[1,1024,256]{2,1,0:T(8,128)(2,1)} all-gather(bf16[1,128,256]{2,1,0:T(8,128)(2,1)S(1)} %copy-done.28), channel_id=1, replica_groups=mesh['pipe'=4,'ctx'=8] {'ctx'}, dimensions={1}, use_global_device_ids=true | all-gather | bytes 589824 | tf_op jit(solution)/shard_map/all_gather | solution.py:90
  103.7 23.3 %fusion.146 = f32[8,128,8]{2,0,1:T(8,128)S(1)} fusion(f32[8,128,8]{2,0,1:T(8,128)S(1)} %copy.209), kind=kOutput, calls=%fused_computation.165 | output fusion | flops 1040384 | bytes 65536 | tf_op jit(solution)/shard_map/jvp(jit(cumsum))/reduce_window_sum | solution.py:30
  127.7 5.0 %copy.207 = bf16[1,128,4096]{1,0,2:T(2,128)(2,1)S(1)} copy(bf16[1,128,4096]{2,1,0:T(8,128)(2,1)} %collective-permute-done) | data formatting | bytes 2097152 | tf_op jit(solution)/shard_map/ppermute | solution.py:12
  132.7 23.4 %reduce.9 = bf16[4096,128]{1,0:T(8,128)(2,1)} reduce(bf16[4096,1,128]{2,1,0:T(2,128)(2,1)S(1)} %bitcast.210, bf16[]{:T(256)} %broadcast.167), dimensions={1}, to_apply=%bitcast.157.reduce_sub_computation | reduce | bytes 2097154
  158.3 3.6 all-to-all-start
  164.2 4.3 %reshape.370 = bf16[4096,1,128]{2,1,0:T(2,128)(2,1)S(1)} reshape(bf16[8,2,32768]{2,1,0:T(2,128)(2,1)} %all-to-all-done.2) | data formatting | bytes 2097152
  187.8 3.6 reshape.368
  198.8 3.7 multiply_reduce_fusion
  210.1 4.3 %fusion.51 = f32[8,128,128]{2,1,0:T(8,128)S(1)} fusion(f32[8,8,64,128]{3,0,2,1:T(8,128)S(1)} %copy-done.6, f32[8,128,8,64]{1,3,2,0:T(8,128)S(1)} %copy.214, f32[8,128,8]{1,2,0:T(8,128)S(1)} %copy.215, f32[8,128,8]{1,2,0:T(8,128)S(1)} %get-tuple-element.34), kind=kOutput, calls=%fused_computation.65 | convolution fusion | flops 806354944 | bytes 4784128 | tf_op jit(solution)/shard_map/transpose(jvp(ckn,ckhp->chpn))/dot_general | solution.py:42
  214.4 6.7 %fusion.143 = (f32[8,8]{0,1:T(8,128)S(1)}, f32[8,8]{0,1:T(8,128)S(1)}) fusion(f32[8,8]{0,1:T(8,128)S(1)} %copy.217, f32[8,8]{0,1:T(8,128)S(1)} %copy.216, f32[8,8,64,128]{3,2,1,0:T(8,128)S(1)} %fusion.38, f32[8,64,128,8]{2,1,0,3:T(8,128)S(1)} %bitcast.197, pred[8,8]{1,0:T(8,128)(4,1)S(1)} %iota_compare_fusion.1), kind=kOutput, calls=%fused_computation.160 | convolution fusion | flops 50335104 | bytes 4195392 | tf_op jit(solution)/shard_map/transpose(jvp(cdh,dhpn->chpn))/dot_general | solution.py:50
  226.7 6.5 %fusion.14 = (f32[8,128,8]{1,2,0:T(8,128)S(1)}, f32[8,128,8]{1,2,0:T(8,128)S(1)}, f32[8,128,128]{1,2,0:T(8,128)S(1)}) fusion(f32[8,128,128]{1,2,0:T(8,128)S(1)} %copy-done.27, f32[8,128,8]{1,2,0:T(8,128)S(1)} %copy.221, pred[128,128]{0,1:T(8,128)(4,1)S(1)} %iota_compare_fusion, bf16[8,8,64,128]{3,2,1,0:T(8,128)(2,1)S(1)} %bitcast.192, ...), kind=kOutput, calls=%fused_computation.22 | convolution fusion | flops 817217536 | bytes 4341760 | tf_op jit(solution)/shard_map/transpose(jvp(cqkh,ckhp->cqhp))/dot_general | solution.py:39
  233.2 4.9 %bitcast_add_fusion = f32[8,128,8,64]{1,3,2,0:T(8,128)S(1)} fusion(f32[8,128,8,64]{1,3,2,0:T(8,128)S(1)} %copy-done.24, bf16[8,8,64,128]{3,2,1,0:T(8,128)(2,1)S(1)} %bitcast.193, f32[8,128,128]{1,2,0:T(8,128)S(1)} %copy-done.27, f32[8,128,8]{1,2,0:T(8,128)S(1)} %copy.221, pred[128,128]{0,1:T(8,128)(4,1)S(1)} %iota_compare_fusion, f32[8,128,8]{1,2,0:T(8,128)S(1)} %copy.215), kind=kOutput, calls=%fused_computation.27 | convolution fusion | flops 810549248 | bytes 5849088 | tf_op jit(solution)/shard_map/transpose(jvp(cqkh,ckhp->cqhp))/dot_general | solution.py:39
  239.2 4.5 %fusion.59 = f32[8,128,128]{2,1,0:T(8,128)} fusion(f32[8,128,128]{2,1,0:T(8,128)S(1)} %fusion.147, f32[8,8,64,128]{3,0,2,1:T(8,128)S(1)} %bitcast_add_fusion.1, bf16[8,128,8,64]{1,3,2,0:T(8,128)(2,1)S(1)} %bitcast.194, f32[8,128,8]{1,2,0:T(8,128)S(1)} %copy.210), kind=kOutput, calls=%fused_computation.68 | convolution fusion | flops 806486016 | bytes 4227072 | tf_op jit(solution)/shard_map/transpose(jvp(cqn,chpn->cqhp))/dot_general | solution.py:52
  263.6 6.2 %pad_add_fusion = bf16[1027,768]{1,0:T(8,128)(2,1)} fusion(f32[1024,768]{1,0:T(8,128)} %copy-done.4, f32[1024,768]{1,0:T(8,128)} %copy-done.3, f32[1024,768]{1,0:T(8,128)} %copy-done.2, f32[1024,768]{1,0:T(8,128)S(1)} %get-tuple-element.31), kind=kLoop, calls=%fused_computation.11 | loop fusion | flops 3154944 | bytes 14160384 | tf_op jit(solution)/shard_map/transpose(jvp())/add_any | solution.py:21
  273.8 3.8 %fusion.97 = f32[8,128,8]{2,0,1:T(8,128)} fusion(f32[8,128,8]{2,0,1:T(8,128)} %copy.247, f32[8,128,8]{2,0,1:T(8,128)} %copy.246, f32[8,1,8]{2,0,1:T(8,128)S(1)} %bitcast.229, f32[8,1,8]{2,0,1:T(8,128)S(1)} %negate_add_fusion, f32[8,128,8]{2,0,1:T(8,128)} %copy.239, f32[8,128,8]{2,0,1:T(8,128)S(1)} %copy-done.21, f32[8,128,8]{2,0,1:T(8,128)} %get-tuple-element.30, ...), kind=kOutput, calls=%fused_computation.83 | output fusion | flops 1114112 | bytes 229888 | tf_op jit(solution)/shard_map/transpose(jvp(jit(cumsum)))/reduce_window_sum | solution.py:30
  284.5 5.9 %all-to-all-start.4 = ((bf16[8,2,512]{2,1,0:T(2,128)(2,1)}), bf16[8,2,512]{2,1,0:T(2,128)(2,1)S(1)}, u32[]{:S(2)}, u32[]{:S(2)}) async-start(bf16[8,2,512]{2,1,0:T(2,128)(2,1)} %reshape.375), calls=%async_computation.5 | async-start | bytes 32768 | tf_op jit(solution)/shard_map/all_to_all | solution.py:141
  293.0 7.3 %reduce.11 = bf16[1024,512]{1,0:T(8,128)(2,1)S(1)} reduce(bf16[1024,1,512]{2,1,0:T(2,128)(2,1)S(1)} %bitcast.209, bf16[]{:T(256)} %broadcast.167), dimensions={1}, to_apply=%bitcast.188.reduce_sub_computation | reduce | bytes 2097154
  301.9 6.0 %all-to-all-start.3 = ((bf16[8,2,32768]{2,1,0:T(2,128)(2,1)}), bf16[8,2,32768]{2,1,0:T(2,128)(2,1)S(1)}, u32[]{:S(2)}, u32[]{:S(2)}) async-start(bf16[8,2,32768]{2,1,0:T(2,128)(2,1)} %reshape.373), calls=%async_computation.3 | async-start | bytes 2097152 | tf_op jit(solution)/shard_map/all_to_all | solution.py:138
  309.5 26.6 %all-to-all-done.3 = bf16[8,2,32768]{2,1,0:T(2,128)(2,1)S(1)} async-done(((bf16[8,2,32768]{2,1,0:T(2,128)(2,1)}), bf16[8,2,32768]{2,1,0:T(2,128)(2,1)S(1)}, u32[]{:S(2)}, u32[]{:S(2)}) %all-to-all-start.3) | async-done | bytes 1048608 | tf_op jit(solution)/shard_map/all_to_all | solution.py:138
  339.4 27.2 %reduce-scatter.2.cloned.1.call-done = f32[1,128,256]{2,1,0:T(8,128)} async-done(((f32[1,1024,256]{2,1,0:T(8,128)}), f32[1,128,256]{2,1,0:T(8,128)}) %reduce-scatter.2.cloned.1.call-update) | async-done | bytes 131088 | tf_op jit(solution)/shard_map/reduce_scatter | solution.py:145
  (161 shorter events, 94.3 us)
Async XLA Ops:
  7.2 46.4 %copy-start = (f32[1,64]{1,0:T(1,128)S(1)}, f32[1,64]{1,0:T(1,128)}, u32[]{:S(2)}) copy-start(f32[1,64]{1,0:T(1,128)} %param.16) | copy-start | bytes 772
  9.8 38.0 %all-to-all-start.1 = ((bf16[8,2,512]{2,1,0:T(2,128)(2,1)}), bf16[8,2,512]{2,1,0:T(2,128)(2,1)S(1)}, u32[]{:S(2)}, u32[]{:S(2)}) async-start(bf16[8,2,512]{2,1,0:T(2,128)(2,1)} %reshape.371), calls=%async_computation.1 | async-start | bytes 32768 | tf_op jit(solution)/shard_map/all_to_all | solution.py:88
  17.1 110.6 %collective-permute-start = (bf16[1,128,4096]{2,1,0:T(8,128)(2,1)}, bf16[1,128,4096]{2,1,0:T(8,128)(2,1)}, u32[]{:S(2)}, u32[]{:S(2)}) collective-permute-start(bf16[1,128,4096]{2,1,0:T(8,128)(2,1)} %param.17), channel_id=1, source_target_pairs={{8,0},{16,8},{24,16},{0,24},{9,1},{17,9},{25,17},{1,25},{10,2},{18... | collective-permute-start | bytes 3145736 | tf_op jit(solution)/shard_map/ppermute | solution.py:12
  46.7 7.8 %copy-start.29 = (f32[1,64]{1,0:T(1,128)S(1)}, f32[1,64]{1,0:T(1,128)}, u32[]{:S(2)}) copy-start(f32[1,64]{1,0:T(1,128)} %param.15) | copy-start | bytes 772
  46.7 7.9 %slice-start = ((f32[1,4352]{1,0:T(1,128)}), f32[1,4096]{1,0:T(1,128)S(1)}, s32[]{:S(2)}) async-start(f32[1,4352]{1,0:T(1,128)} %param.13), calls=%async_computation.7 | async-start | bytes 32768 | tf_op jit(solution)/shard_map/slice | solution.py:100
  46.7 7.9 %slice-start.1 = ((f32[1,4352]{1,0:T(1,128)}), f32[1,256]{1,0:T(1,128)S(1)}, s32[]{:S(2)}) async-start(f32[1,4352]{1,0:T(1,128)} %param.13), calls=%async_computation.8 | async-start | bytes 2048 | tf_op jit(solution)/shard_map/slice | solution.py:100
  46.7 7.9 %copy-start.28 = (bf16[1,128,256]{2,1,0:T(8,128)(2,1)S(1)}, bf16[1,128,256]{2,1,0:T(8,128)(2,1)}, u32[]{:S(2)}) copy-start(bf16[1,128,256]{2,1,0:T(8,128)(2,1)} %param.10) | copy-start | bytes 196612
  47.8 110.5 %all-to-all-start.2 = ((bf16[8,2,32768]{2,1,0:T(2,128)(2,1)}), bf16[8,2,32768]{2,1,0:T(2,128)(2,1)}, u32[]{:S(2)}, u32[]{:S(2)}) async-start(bf16[8,2,32768]{2,1,0:T(2,128)(2,1)} %reshape.369), calls=%async_computation.2 | async-start | bytes 2097152 | tf_op jit(solution)/shard_map/all_to_all | solution.py:86
  127.0 34.9 %copy-start.9 = (f32[8,128,8]{2,0,1:T(8,128)}, f32[8,128,8]{2,0,1:T(8,128)S(1)}, u32[]{:S(2)}) copy-start(f32[8,128,8]{2,0,1:T(8,128)S(1)} %fusion.146) | copy-start | bytes 98308
  158.3 29.5 %all-to-all-start = ((bf16[8,2,32768]{2,1,0:T(2,128)(2,1)}), bf16[8,2,32768]{2,1,0:T(2,128)(2,1)S(1)}, u32[]{:S(2)}, u32[]{:S(2)}) async-start(bf16[8,2,32768]{2,1,0:T(2,128)(2,1)} %reshape.367), calls=%async_computation | async-start | bytes 2097152 | tf_op jit(solution)/shard_map/all_to_all | solution.py:87
  198.8 3.7 copy-start.5
  210.1 4.3 %copy-start.8 = (f32[8,8,64,128]{3,2,1,0:T(8,128)S(1)}, f32[8,8,64,128]{3,2,1,0:T(8,128)}, u32[]{:S(2)}) copy-start(f32[8,8,64,128]{3,2,1,0:T(8,128)} %copy-done.7) | copy-start | bytes 6291460
  226.7 6.5 %copy-start.24 = (f32[8,128,8,64]{1,3,2,0:T(8,128)S(1)}, f32[8,128,8,64]{1,3,2,0:T(8,128)}, u32[]{:S(2)}) copy-start(f32[8,128,8,64]{1,3,2,0:T(8,128)} %get-tuple-element.43) | copy-start | bytes 6291460
  233.2 5.0 %copy-start.16 = (f32[1024,128]{1,0:T(8,128)S(1)}, f32[1024,128]{1,0:T(8,128)}, u32[]{:S(2)}) copy-start(f32[1024,128]{1,0:T(8,128)} %copy-done.14) | copy-start | bytes 1572868
  238.2 7.1 %copy-start.19 = (f32[8,128,8,64]{1,3,2,0:T(8,128)}, f32[8,128,8,64]{1,3,2,0:T(8,128)S(1)}, u32[]{:S(2)}) copy-start(f32[8,128,8,64]{1,3,2,0:T(8,128)S(1)} %bitcast_add_fusion) | copy-start | bytes 6291460
  258.7 3.6 copy-start.4
  269.8 4.0 %copy-start.10 = (f32[8,128,8]{2,0,1:T(8,128)S(1)}, f32[8,128,8]{2,0,1:T(8,128)}, u32[]{:S(2)}) copy-start(f32[8,128,8]{2,0,1:T(8,128)} %copy-done.9) | copy-start | bytes 98308
  269.8 4.0 %copy-start.21 = (f32[8,128,8]{2,0,1:T(8,128)S(1)}, f32[8,128,8]{2,0,1:T(8,128)}, u32[]{:S(2)}) copy-start(f32[8,128,8]{2,0,1:T(8,128)} %copy.245) | copy-start | bytes 98308
  273.8 5.0 %copy-start.20 = (f32[8,128,8,64]{1,3,2,0:T(8,128)S(1)}, f32[8,128,8,64]{1,3,2,0:T(8,128)}, u32[]{:S(2)}) copy-start(f32[8,128,8,64]{1,3,2,0:T(8,128)} %copy-done.19) | copy-start | bytes 6291460
  280.8 10.3 %copy-start.22 = (bf16[1027,768]{1,0:T(8,128)(2,1)S(1)}, bf16[1027,768]{1,0:T(8,128)(2,1)}, u32[]{:S(2)}) copy-start(bf16[1027,768]{1,0:T(8,128)(2,1)} %pad_add_fusion) | copy-start | bytes 4732420
  284.5 17.5 %all-to-all-start.4 = ((bf16[8,2,512]{2,1,0:T(2,128)(2,1)}), bf16[8,2,512]{2,1,0:T(2,128)(2,1)S(1)}, u32[]{:S(2)}, u32[]{:S(2)}) async-start(bf16[8,2,512]{2,1,0:T(2,128)(2,1)} %reshape.375), calls=%async_computation.5 | async-start | bytes 32768 | tf_op jit(solution)/shard_map/all_to_all | solution.py:141
  290.4 76.2 %reduce-scatter.2.cloned.1.call-start = ((), (), s32[]{:S(2)}) async-start(), calls=%async_computation.6 | async-start | bytes 1179648 | tf_op jit(solution)/shard_map/reduce_scatter | solution.py:145
  301.9 34.2 %all-to-all-start.3 = ((bf16[8,2,32768]{2,1,0:T(2,128)(2,1)}), bf16[8,2,32768]{2,1,0:T(2,128)(2,1)S(1)}, u32[]{:S(2)}, u32[]{:S(2)}) async-start(bf16[8,2,32768]{2,1,0:T(2,128)(2,1)} %reshape.373), calls=%async_computation.3 | async-start | bytes 2097152 | tf_op jit(solution)/shard_map/all_to_all | solution.py:138
  337.4 30.8 %copy-start.1 = (f32[1,64]{1,0:T(1,128)S(1)}, f32[1,64]{1,0:T(1,128)}, u32[]{:S(2)}) copy-start(f32[1,64]{1,0:T(1,128)} %param.16) | copy-start | bytes 772
  (15 other events, 36.5 us)
Sparse Core Ops, SparseCore 0:
  294.6 71.9 reduce-scatter.1
where the time goes:
time: 381 us; the launch traced here: 375 us
  other arithmetic  107 us (28%)
  local copies, waits for them, and re-layouts  71.7 us (19%)
  waiting for transfers between devices  54.3 us (14%)
  matrix products  49.4 us (13%)
  blocking collectives  48.6 us (13%)
  starting transfers between devices  29.4 us (8%)
  between operations  15.1 us (4%)
    unnamed x5, other arithmetic  56.2 us
    all_gather x1, blocking collectives, per_device(): whole_maps = lax.all_gather(state_maps, 'ctx', axis=1, tiled=True)  48.6 us
    unnamed x77, local copies, waits for them, and re-layouts  33.3 us
    reduce_scatter x1, waiting for transfers between devices, per_device(): lax.psum_scatter(grad_map[None], 'ctx', scatter_dimension=1, tiled=True)  27.2 us
    another operation x2, other arithmetic, ssd_forward(): cumulative = jnp.cumsum(log_decay, axis=1)  27.1 us
    all_to_all x1, waiting for transfers between devices, per_device(): lax.all_to_all(grad_feature.astype(jnp.bfloat16)[None], 'ctx', split_axis...  26.6 us
    dot_general x3, matrix products, ssd_forward(): jnp.einsum('cdh,dhpn->chpn', carry_decay, states, precision=highest)  13.1 us
    dot_general x2, matrix products, ssd_forward(): y_within = jnp.einsum('cqkh,ckhp->cqhp', mixing, scaled, precision=highest)  11.4 us
  transfers between devices with their start and end apart: 7, of which 2 were waited for; matrix products, arithmetic and copies ran while one was open for 33% of the time, Pallas kernels for 0%

commit v1 on v0

v1 whole, which is shorter than its diff:
```python
import functools

import jax
import jax.numpy as jnp
from jax import lax
from jax.experimental import pallas as pl
from jax.experimental.pallas import tpu as pltpu
from jax.sharding import PartitionSpec as P

BLOCK = 128
LANES = 128
HEAD = 64
PAD = 8
F32 = jnp.float32
BF16 = jnp.bfloat16
NEG = -1e30
NN = (((1,), (0,)), ((), ()))
NT = (((1,), (1,)), ((), ()))
TN = (((0,), (0,)), ((), ()))


def mm(a, b, dims=NN):
    return lax.dot_general(a, b, dims, preferred_element_type=F32)


def split(a):
    high = a.astype(BF16)
    return high, (a - high.astype(F32)).astype(BF16)


def mm3(a, b, dims=NN):
    (ah, al), (bh, bl) = a, b
    return mm(ah, bh, dims) + (mm(ah, bl, dims) + mm(al, bh, dims))


def iota(shape, axis):
    return lax.broadcasted_iota(jnp.int32, shape, axis)


def expand(values, pair):
    rows = values.shape[0]
    first = jnp.broadcast_to(values[:, 2 * pair : 2 * pair + 1], (rows, LANES))
    second = jnp.broadcast_to(values[:, 2 * pair + 1 : 2 * pair + 2], (rows, LANES))
    return jnp.where(iota((rows, LANES), 1) < HEAD, first, second)


def head_sum(tile, pair):
    onto = (iota((LANES, LANES), 1) == 2 * pair + iota((LANES, LANES), 0) // HEAD).astype(F32).astype(BF16)
    high, low = split(tile)
    return mm(high, onto) + mm(low, onto)


def lanes(pair):
    return slice(pair * LANES, (pair + 1) * LANES)


class Plan:
    def __init__(self, devices, inner, state, heads):
        self.half = devices // 2
        self.inner = inner
        self.state = state
        self.heads = heads // self.half
        self.width = inner // self.half
        self.pairs = self.width // LANES
        self.blocks = self.half
        self.tokens = self.half * BLOCK
        self.conv = self.width + 2 * state
        self.pay = self.conv + LANES
        self.out = self.width + LANES
        self.edge = PAD * self.width // (2 * state)


def place(plan):
    rank = lax.axis_index("ctx")
    return lax.rem(rank, plan.half), lax.div(rank, plan.half)


def call(kernel, plan, out_shape, scratch=(), flops=0):
    return pl.pallas_call(
        functools.partial(kernel, plan),
        out_shape=out_shape,
        scratch_shapes=list(scratch),
        compiler_params=pltpu.CompilerParams(vmem_limit_bytes=56 * 1024 * 1024),
        cost_estimate=pl.CostEstimate(flops=flops, transcendentals=0, bytes_accessed=4 << 20),
    )


def struct(*shape, dtype=F32):
    return jax.ShapeDtypeStruct(shape, dtype)


def pack_kernel(plan, f_ref, m_ref, s_ref, o_ref, *outs):
    own, _ = place(plan)
    half, width = plan.half, plan.width
    pays, edges, grads = outs[:half], outs[half : 2 * half], outs[2 * half :]
    for k in range(half):
        start = pl.multiple_of(jnp.bitwise_xor(own, k) * width, LANES)
        pays[k][:, :width] = f_ref[:, pl.ds(start, width)]
        pays[k][:, width : plan.conv] = m_ref[...]
        pays[k][:, plan.conv :] = jnp.zeros((BLOCK, LANES), BF16)
        pays[k][:, plan.conv : plan.conv + s_ref.shape[1]] = s_ref[...]
        grads[k][...] = o_ref[:, pl.ds(start, width)]
        edges[k][:, :width] = f_ref[BLOCK - 16 :, k * width : (k + 1) * width]
        edges[k][:, width:] = m_ref[BLOCK - 16 :, :]


def forward_kernel(plan, *refs):
    half, width, conv, pairs = plan.half, plan.width, plan.conv, plan.pairs
    pays, edges = refs[:half], refs[half : 2 * half]
    (cw_ref, cb_ref, dl_ref, sb_ref, x_ref, ds_ref, st_ref, sg_ref, cum_ref, el_ref,
     raw, sraw, prm) = refs[2 * half :]
    own, _ = place(plan)
    halo = edges[0][...].astype(F32)
    for k in range(1, half):
        halo = halo + edges[k][...].astype(F32)
    raw[0:PAD, :] = halo[16 - PAD :, :]
    for k in range(half):
        block = jnp.bitwise_xor(own, k) * BLOCK
        raw[pl.ds(pl.multiple_of(block + PAD, 8), BLOCK), :] = pays[k][:, :conv].astype(F32)
        sraw[pl.ds(pl.multiple_of(block, 8), BLOCK), :] = pays[k][:, conv:].astype(F32)
    heads_all = dl_ref.shape[1]
    prm[...] = jnp.zeros_like(prm)
    prm[0:1, 0:heads_all] = -jnp.exp(dl_ref[...])
    prm[1:2, 0:heads_all] = sb_ref[...]
    shift = lax.rem(LANES - own * plan.heads, LANES)
    local = pltpu.roll(prm[...], shift, 1)
    rates, offsets = local[0:1, :], local[1:2, :]
    lower = (iota((BLOCK, BLOCK), 0) >= iota((BLOCK, BLOCK), 1)).astype(F32)
    el_ref[0:BLOCK, :] = jnp.zeros((BLOCK, width), F32)
    tile = 256 if width % 256 == 0 else LANES

    def body(b, carry):
        row = pl.multiple_of(b * BLOCK, BLOCK)
        rows = pl.ds(row, BLOCK)
        for c in range(0, conv, tile):
            window = raw[pl.ds(row, BLOCK + PAD), c : c + tile]
            if c < width:
                cols = pl.ds(pl.multiple_of(own * width + c, LANES), tile)
            else:
                cols = slice(plan.inner + c - width, plan.inner + c - width + tile)
            weight = cw_ref[:, cols]
            v = jnp.broadcast_to(cb_ref[:, cols], (BLOCK, tile))
            for k in range(weight.shape[0]):
                v = v + weight[k : k + 1, :] * window[PAD - k : PAD - k + BLOCK, :]
            s = 1.0 / (1.0 + jnp.exp(-v))
            x_ref[rows, c : c + tile] = v * s
            ds_ref[rows, c : c + tile] = s * (1.0 + v * (1.0 - s))
        a = pltpu.roll(sraw[rows, :], shift, 1) + offsets
        e = jnp.exp(-jnp.abs(a))
        u = 1.0 + e
        d = u - 1.0
        step = jnp.maximum(a, 0.0) + jnp.where(d == 0.0, e, jnp.log(u) * (e / jnp.where(d == 0.0, 1.0, d)))
        st_ref[rows, :] = step
        sg_ref[rows, :] = jnp.where(a >= 0.0, 1.0, e) / u
        cum = lax.dot_general(lower, step * rates, NN, precision=lax.Precision.HIGHEST, preferred_element_type=F32)
        cum_ref[rows, :] = cum
        total = cum[BLOCK - 1 :, :]
        weighted = jnp.exp(total - cum) * step
        decay = jnp.exp(total)
        b_maps = x_ref[rows, width : width + plan.state]
        bt = split(b_maps.T)
        nxt = pl.ds(pl.multiple_of(row + BLOCK, BLOCK), BLOCK)
        for i in range(pairs):
            wx = split(x_ref[rows, lanes(i)] * expand(weighted, i))
            el_ref[nxt, lanes(i)] = el_ref[rows, lanes(i)] * expand(decay, i) + mm3(bt, wx)
        return carry

    lax.fori_loop(0, plan.blocks, body, 0)


def gradient_kernel(plan, *refs):
    half, width, pairs, blocks = plan.half, plan.width, plan.pairs, plan.blocks
    grads = refs[:half]
    x_ref, cum_ref, el_ref, gy_ref, gl_ref, send_ref = refs[half:]
    own, late = place(plan)
    for k in range(half):
        block = pl.multiple_of(jnp.bitwise_xor(own, k) * BLOCK, BLOCK)
        gy_ref[pl.ds(block, BLOCK), :] = grads[k][...]
    gl_ref[blocks * BLOCK :, :] = jnp.zeros((BLOCK, width), F32)

    def body(t, carry):
        row = pl.multiple_of((blocks - 1 - t) * BLOCK, BLOCK)
        rows = pl.ds(row, BLOCK)
        nxt = pl.ds(pl.multiple_of(row + BLOCK, BLOCK), BLOCK)
        cum = cum_ref[rows, :]
        grown, decay = jnp.exp(cum), jnp.exp(cum[BLOCK - 1 :, :])
        ct = split(x_ref[rows, width + plan.state :].T)
        for i in range(pairs):
            ge = split(gy_ref[rows, lanes(i)].astype(F32) * expand(grown, i))
            gl_ref[rows, lanes(i)] = gl_ref[nxt, lanes(i)] * expand(decay, i) + mm3(ct, ge)
        return carry

    lax.fori_loop(0, blocks, body, 0)

    @pl.when(late == 0)
    def _():
        send_ref[...] = el_ref[blocks * BLOCK :, :]

    @pl.when(late != 0)
    def _():
        send_ref[...] = gl_ref[0:BLOCK, :]


def within_kernel(plan, x_ref, st_ref, cum_ref, gy_ref, yw_ref, dw_ref, dsc_ref):
    width, pairs = plan.width, plan.pairs
    causal = iota((BLOCK, BLOCK), 0) >= iota((BLOCK, BLOCK), 1)
    left = iota((BLOCK, LANES), 1) < HEAD

    def body(b, carry):
        rows = pl.ds(pl.multiple_of(b * BLOCK, BLOCK), BLOCK)
        cum = cum_ref[rows, :]
        cum_t = cum.T
        step = st_ref[rows, :]
        b_maps = split(x_ref[rows, width : width + plan.state])
        c_maps = split(x_ref[rows, width + plan.state :])
        scores = mm3(c_maps, b_maps, NT)
        total = jnp.zeros((BLOCK, BLOCK), F32)
        zero = jnp.zeros((BLOCK, LANES), BF16)
        for i in range(pairs):
            xs = x_ref[rows, lanes(i)] * expand(step, i)
            xh, xl = split(xs)
            gy = gy_ref[rows, lanes(i)]
            g0, g1 = jnp.where(left, gy, zero), jnp.where(left, zero, gy)
            decays, mh, ml = [], [], []
            for h in (2 * i, 2 * i + 1):
                spread = jnp.broadcast_to(cum[:, h : h + 1], (BLOCK, BLOCK)) - cum_t[h : h + 1, :]
                decay = jnp.exp(jnp.where(causal, spread, NEG))
                high, low = split(scores * decay)
                decays.append(decay)
                mh.append(high)
                ml.append(low)
            both = jnp.concatenate(
                [
                    jnp.concatenate([jnp.where(left, xh, zero), jnp.where(left, xl, zero)], axis=1),
                    jnp.concatenate([jnp.where(left, zero, xh), jnp.where(left, zero, xl)], axis=1),
                ],
                axis=0,
            )
            high = mm(jnp.concatenate(mh, axis=1), both)
            low = mm(jnp.concatenate(ml, axis=1), both[:, :LANES])
            yw_ref[rows, lanes(i)] = high[:, :LANES] + (high[:, LANES:] + low)
            gs = jnp.concatenate([g0, g1], axis=0)
            dw_ref[rows, lanes(i)] = mm(jnp.concatenate(mh, axis=0), gs, TN) + mm(jnp.concatenate(ml, axis=0), gs, TN)
            dm = mm(jnp.concatenate([gs, gs], axis=1), jnp.concatenate([xh, xl], axis=1), NT)
            total = total + dm[:BLOCK] * decays[0] + dm[BLOCK:] * decays[1]
        dsc_ref[rows, :] = total
        return carry

    lax.fori_loop(0, plan.blocks, body, 0)


def final_kernel(plan, *refs):
    half, width, conv, pairs, blocks, state = plan.half, plan.width, plan.conv, plan.pairs, plan.blocks, plan.state
    (got_ref, x_ref, ds_ref, st_ref, sg_ref, cum_ref, el_ref, gl_ref, gy_ref, yw_ref, dw_ref, dsc_ref,
     cw_ref, dl_ref, sk_ref) = refs[:15]
    outs, maps, halos = refs[15 : 15 + half], refs[15 + half : 15 + 2 * half], refs[15 + 2 * half]
    prm, dz, nxt_dz, carry_ref, o_sc, m_sc, e_sc, lc_sc = refs[16 + 2 * half :]
    own, late = place(plan)
    is_late = late.astype(F32)
    heads_all = dl_ref.shape[1]
    prm[...] = jnp.zeros_like(prm)
    prm[0:1, 0:heads_all] = -jnp.exp(dl_ref[...])
    prm[1:2, 0:heads_all] = sk_ref[...]
    shift = lax.rem(LANES - own * plan.heads, LANES)
    local = pltpu.roll(prm[...], shift, 1)
    rates, skips = local[0:1, :], local[1:2, :]
    upper = (iota((BLOCK, BLOCK), 0) <= iota((BLOCK, BLOCK), 1)).astype(F32)
    nxt_dz[...] = jnp.zeros_like(nxt_dz)
    lc_sc[...] = jnp.zeros_like(lc_sc)
    for b in range(1, blocks):
        lc_sc[b : b + 1, :] = lc_sc[b - 1 : b, :] + cum_ref[b * BLOCK - 1 : b * BLOCK, :]
    whole = lc_sc[blocks - 1 : blocks, :] + cum_ref[blocks * BLOCK - 1 :, :]
    ends = jnp.zeros((8, LANES), F32)
    for i in range(pairs):
        product = jnp.sum(got_ref[:, lanes(i)] * el_ref[blocks * BLOCK :, lanes(i)], axis=0, keepdims=True)
        ends = ends + head_sum(jnp.broadcast_to(product, (8, LANES)), i)
    carry_ref[...] = ends * (1.0 - is_late)

    def body(t, carry):
        b = blocks - 1 - t
        row = pl.multiple_of(b * BLOCK, BLOCK)
        rows = pl.ds(row, BLOCK)
        nxt = pl.ds(pl.multiple_of(row + BLOCK, BLOCK), BLOCK)
        cum, step = cum_ref[rows, :], st_ref[rows, :]
        total = cum[BLOCK - 1 :, :]
        grown, shrunk = jnp.exp(cum), jnp.exp(total - cum)
        before = lc_sc[pl.ds(b, 1), :]
        from_first = jnp.exp(before) * is_late
        to_last = jnp.exp(whole - before - total) * (1.0 - is_late)
        b_f32, c_f32 = x_ref[rows, width : width + state], x_ref[rows, width + state : conv]
        b_maps, c_maps = split(b_f32), split(c_f32)
        dsc = split(dsc_ref[rows, :])
        d_c = mm3(dsc, b_maps)
        d_b = mm3(dsc, c_maps, TN)
        sums = jnp.zeros((BLOCK, LANES), F32)
        direct = jnp.zeros((BLOCK, LANES), F32)
        for i in range(pairs):
            got = got_ref[:, lanes(i)]
            entering = split(el_ref[rows, lanes(i)] + got * expand(from_first, i))
            leaving = split(gl_ref[nxt, lanes(i)] + got * expand(to_last, i))
            x = x_ref[rows, lanes(i)]
            step_x, shrunk_x, grown_x = expand(step, i), expand(shrunk, i), expand(grown, i)
            xs = x * step_x
            gy = gy_ref[rows, lanes(i)].astype(F32)
            y = yw_ref[rows, lanes(i)] + grown_x * mm3(c_maps, entering)
            dxs = dw_ref[rows, lanes(i)] + shrunk_x * mm3(b_maps, leaving)
            d_c = d_c + mm3(split(gy * grown_x), entering, NT)
            d_b = d_b + mm3(split(xs * shrunk_x), leaving, NT)
            sums = sums + head_sum(gy * y - xs * dxs, i)
            direct = direct + head_sum(dxs * x, i)
            dz[0:BLOCK, lanes(i)] = (dxs * step_x + expand(skips, i) * gy) * ds_ref[rows, lanes(i)]
        dz[0:BLOCK, width : width + state] = d_b * ds_ref[rows, width : width + state]
        dz[0:BLOCK, width + state :] = d_c * ds_ref[rows, width + state :]
        dz[BLOCK:, :] = nxt_dz[...]
        d_log = lax.dot_general(upper, sums, NN, precision=lax.Precision.HIGHEST, preferred_element_type=F32)
        d_log = d_log + carry_ref[0:1, :]
        carry_ref[...] = jnp.broadcast_to(d_log[0:1, :], (8, LANES))
        d_step = (d_log * rates + direct) * sg_ref[rows, :]
        valid = iota((BLOCK, LANES), 1) < plan.heads
        o_sc[rows, width:] = jnp.where(valid, d_step, 0.0).astype(BF16)
        for c in range(0, conv, LANES):
            window = dz[:, c : c + LANES]
            if c < width:
                cols = pl.ds(pl.multiple_of(own * width + c, LANES), LANES)
            else:
                cols = slice(plan.inner + c - width, plan.inner + c - width + LANES)
            weight = cw_ref[:, cols]
            grad = weight[0:1, :] * window[0:BLOCK, :]
            for k in range(1, weight.shape[0]):
                grad = grad + weight[k : k + 1, :] * window[k : k + BLOCK, :]
            if c < width:
                o_sc[rows, c : c + LANES] = grad.astype(BF16)
                e_sc[pl.ds(pl.multiple_of(b * PAD, PAD), PAD), c : c + LANES] = grad[BLOCK - PAD :, :]
            else:
                m_sc[rows, c - width : c - width + LANES] = grad

            @pl.when(b == 0)
            def _():
                padded = jnp.concatenate([jnp.zeros((PAD, LANES), F32), window[0:PAD, :]], axis=0)
                spill = jnp.zeros((PAD, LANES), F32)
                for k in range(1, weight.shape[0]):
                    spill = spill + weight[k : k + 1, :] * padded[k : k + PAD, :]
                halos[:, c : c + LANES] = spill

        nxt_dz[...] = dz[0:PAD, :]
        return carry

    lax.fori_loop(0, blocks, body, 0)
    for k in range(half):
        b = jnp.bitwise_xor(own, k)
        rows = pl.ds(pl.multiple_of(b * BLOCK, BLOCK), BLOCK)
        outs[k][...] = o_sc[rows, :]
        maps[k][0:BLOCK, :] = m_sc[rows, :]
        step = 2 * state
        for part in range(width // step):
            maps[k][BLOCK + part * PAD : BLOCK + (part + 1) * PAD, :] = e_sc[
                pl.ds(pl.multiple_of(b * PAD, PAD), PAD), part * step : (part + 1) * step
            ]


def owner_kernel(plan, *refs):
    half, width, state = plan.half, plan.width, plan.state
    outs, maps, halos = refs[:half], refs[half : 2 * half], refs[2 * half : 3 * half]
    f_ref, m_ref, s_ref, edge = refs[3 * half :]
    own, _ = place(plan)
    total = maps[0][0:BLOCK, :]
    spill = halos[0][:, width:]
    steps = jnp.zeros((BLOCK, LANES), F32)
    span = 2 * state
    for k in range(half):
        part = jnp.bitwise_xor(own, k)
        start = pl.multiple_of(part * width, LANES)
        f_ref[:, pl.ds(start, width)] = outs[k][:, :width]
        for piece in range(width // span):
            edge[:, pl.ds(pl.multiple_of(start + piece * span, LANES), span)] = maps[k][
                BLOCK + piece * PAD : BLOCK + (piece + 1) * PAD, :
            ]
        steps = steps + pltpu.roll(outs[k][:, width:].astype(F32), part * plan.heads, 1)
        if k:
            total = total + maps[k][0:BLOCK, :]
            spill = spill + halos[k][:, width:]
    for k in range(half):
        cols = slice(k * width, (k + 1) * width)
        fixed = edge[:, cols] + halos[k][:, :width]
        tail = f_ref[BLOCK - 16 :, cols].astype(F32)
        f_ref[BLOCK - 16 :, cols] = jnp.concatenate([tail[:PAD], fixed], axis=0).astype(BF16)
    m_ref[0 : BLOCK - 16, :] = total[0 : BLOCK - 16].astype(BF16)
    m_ref[BLOCK - 16 :, :] = jnp.concatenate(
        [total[BLOCK - 16 : BLOCK - PAD], total[BLOCK - PAD :] + spill], axis=0
    ).astype(BF16)
    s_ref[...] = steps[:, : s_ref.shape[1]].astype(BF16)


def per_device(sections, devices, features, state_maps, step_raw, conv_weight, conv_bias, decay_log, step_bias, skip_gain, output_grads):
    state = state_maps.shape[2] // 2
    heads = decay_log.shape[1]
    plan = Plan(devices, features.shape[2], state, heads)
    half, width, conv, tokens = plan.half, plan.width, plan.conv, plan.tokens
    weight = conv_weight[0]

    def partner(array, k):
        return lax.ppermute(array, "ctx", [(i, i ^ k) for i in range(devices)])

    packed = call(
        pack_kernel,
        plan,
        [struct(BLOCK, plan.pay, dtype=BF16)] * half
        + [struct(16, conv, dtype=BF16)] * half
        + [struct(BLOCK, width, dtype=BF16)] * half,
    )(features[0], state_maps[0], step_raw[0], output_grads[0])
    pays, edges, grads = packed[:half], packed[half : 2 * half], packed[2 * half :]
    edges = [lax.ppermute(e, "ctx", [(half - 1, half + k)]) for k, e in enumerate(edges)]
    pays = [pays[0]] + [partner(pays[k], k) for k in range(1, half)]

    def shifted(array, k):
        route = [
            (((p + 1) % sections) * devices + i, p * devices + (i ^ k))
            for p in range(sections)
            for i in range(devices)
        ]
        return lax.ppermute(array, ("pipe", "ctx"), route)

    grads = [shifted(g, k) for k, g in enumerate(grads)]
    big = 2 * tokens * state * width
    x_conv, dsilu, steps, sigmoids, cums, states = call(
        forward_kernel,
        plan,
        [struct(tokens, conv), struct(tokens, conv), struct(tokens, LANES), struct(tokens, LANES),
         struct(tokens, LANES), struct(tokens + BLOCK, width)],
        [pltpu.VMEM((tokens + PAD, conv), F32), pltpu.VMEM((tokens, LANES), F32), pltpu.VMEM((8, LANES), F32)],
        flops=6 * big,
    )(*pays, *edges, weight, conv_bias, decay_log, step_bias)
    gy, back, send = call(
        gradient_kernel,
        plan,
        [struct(tokens, width, dtype=BF16), struct(tokens + BLOCK, width), struct(BLOCK, width)],
        flops=3 * big,
    )(*grads, x_conv, cums, states)
    got = partner(send, half)
    y_within, d_within, d_scores = call(
        within_kernel,
        plan,
        [struct(tokens, width), struct(tokens, width), struct(tokens, BLOCK)],
        flops=50 * big,
    )(x_conv, steps, cums, gy)
    results = call(
        final_kernel,
        plan,
        [struct(BLOCK, plan.out, dtype=BF16)] * half
        + [struct(BLOCK + plan.edge, 2 * state)] * half
        + [struct(PAD, conv)],
        [pltpu.VMEM((8, LANES), F32), pltpu.VMEM((BLOCK + PAD, conv), F32), pltpu.VMEM((PAD, conv), F32),
         pltpu.VMEM((8, LANES), F32), pltpu.VMEM((tokens, plan.out), BF16), pltpu.VMEM((tokens, 2 * state), F32),
         pltpu.VMEM((PAD * plan.blocks, width), F32), pltpu.VMEM((max(8, plan.blocks), LANES), F32)],
        flops=12 * big,
    )(got, x_conv, dsilu, steps, sigmoids, cums, states, back, gy, y_within, d_within, d_scores,
      weight, decay_log, skip_gain)
    outs, maps, halo = results[:half], results[half : 2 * half], results[2 * half]
    outs = [outs[0]] + [partner(outs[k], k) for k in range(1, half)]
    maps = [maps[0]] + [partner(maps[k], k) for k in range(1, half)]
    halos = [lax.ppermute(halo, "ctx", [(half + k, half - 1)]) for k in range(half)]
    feature_grads, map_grads, step_grads = call(
        owner_kernel,
        plan,
        [struct(BLOCK, plan.inner, dtype=BF16), struct(BLOCK, 2 * state, dtype=BF16), struct(BLOCK, heads, dtype=BF16)],
        [pltpu.VMEM((PAD, plan.inner), F32)],
    )(*outs, *maps, *halos)
    return (feature_grads[None], map_grads[None], step_grads[None])


def solution(mesh):
    return jax.shard_map(
        functools.partial(per_device, mesh.shape["pipe"], mesh.shape["ctx"]),
        mesh=mesh,
        in_specs=(
            P("pipe", "ctx", None),
            P("pipe", "ctx", None),
            P("pipe", "ctx", None),
            P("pipe", None, None),
            P("pipe", None),
            P("pipe", None),
            P("pipe", None),
            P("pipe", None),
            P("pipe", "ctx", None),
        ),
        out_specs=(P("pipe", "ctx", None), P("pipe", "ctx", None), P("pipe", "ctx", None)),
        check_vma=False,
    )
```

time: 381 us -> 140 us (0.37); the launches traced: 375 us -> 139 us
  other arithmetic: 107 us -> 0 us
  local copies, waits for them, and re-layouts: 71.7 us -> 6.26 us
  Pallas kernels: 0 us -> 54 us
  matrix products: 49.4 us -> 0 us
  blocking collectives: 48.6 us -> 0 us
  waiting for transfers between devices: 54.3 us -> 19.3 us
  starting transfers between devices: 29.4 us -> 58.6 us
  between operations: 15.1 us -> 0.98 us
    ppermute x1 -> x22, starting transfers between devices: 0.65 us -> 58.6 us  [the longest x10 37.2 us: partner(): return lax.ppermute(array, 'ctx', [(i, i ^ k) for i in range(devices)])]
    unnamed x5 -> x0, other arithmetic: 56.2 us -> none
    pallas_call x0 -> x6, Pallas kernels: none -> 54 us  [the longest x1 19.9 us: per_device(): call(final_kernel, plan, [struct(BLOCK, plan.out, dtype=BF16)] * half + [...]
    dot_general x14 -> x0, matrix products: 49.4 us -> none  [the longest x3 13.1 us: ssd_forward(): jnp.einsum('cdh,dhpn->chpn', carry_decay, states, precision=highest)]
    all_gather x1 -> x0, blocking collectives: 48.6 us -> none  [per_device(): whole_maps = lax.all_gather(state_maps, 'ctx', axis=1, tiled=True)]
    all_to_all x5 -> x0, starting transfers between devices: 28.5 us -> none  [the longest x1 7.28 us: per_device(): lax.all_to_all(step_raw, 'ctx', split_axis=2, concat_axis=1, tiled=True)]
    reduce_scatter x1 -> x0, waiting for transfers between devices: 27.2 us -> none  [per_device(): lax.psum_scatter(grad_map[None], 'ctx', scatter_dimension=1, tiled=True)]
    another operation x4 -> x0, other arithmetic: 27.1 us -> none  [the longest x2 27.1 us: ssd_forward(): cumulative = jnp.cumsum(log_decay, axis=1)]
  transfers between devices with their start and end apart: 7 -> 22, of which waited for: 2 -> 3; matrix products, arithmetic and copies ran while one was open for 33% -> 0% of each run, Pallas kernels for 0% -> 15%
where the time goes in v1:
time: 140 us; the launch traced here: 139 us
  starting transfers between devices  58.6 us (42%)
  Pallas kernels  54 us (39%)
  waiting for transfers between devices  19.3 us (14%)
  local copies, waits for them, and re-layouts  6.26 us (4%)
    ppermute x10, starting transfers between devices, partner(): return lax.ppermute(array, 'ctx', [(i, i ^ k) for i in range(devices)])  37.2 us
    pallas_call x1, Pallas kernels, per_device(): call(final_kernel, plan, [struct(BLOCK, plan.out, dtype=BF16)] * half + [...  19.9 us
    ppermute x10, waiting for transfers between devices, partner(): return lax.ppermute(array, 'ctx', [(i, i ^ k) for i in range(devices)])  19.2 us
    ppermute x4, starting transfers between devices, shifted(): return lax.ppermute(array, ('pipe', 'ctx'), route)  16.1 us
    pallas_call x1, Pallas kernels, per_device(): call(within_kernel, plan, [struct(tokens, width), struct(tokens, width),...  11.1 us
    pallas_call x1, Pallas kernels, per_device(): call(forward_kernel, plan, [struct(tokens, conv), struct(tokens, conv), s...  9.47 us
    pallas_call x1, Pallas kernels, per_device(): call(gradient_kernel, plan, [struct(tokens, width, dtype=BF16), struct(to...  7.79 us
    unnamed x46, local copies, waits for them, and re-layouts  6.26 us
  transfers between devices with their start and end apart: 22, of which 3 were waited for; matrix products, arithmetic and copies ran while one was open for 0% of the time, Pallas kernels for 15%

profile of v1, /device:TPU:0, one launch (start us, length us, event | category | flops | bytes accessed | tf_op | source)
XLA Modules:
  0.0 139.1 jit_solution(17691698854299518387)
XLA Ops:
  0.6 1.4 %copy.12 = bf16[1,128,64]{2,1,0:T(8,128)(2,1)} copy(bf16[1,128,64]{1,2,0:T(8,128)(2,1)} %param.11) | data formatting | bytes 32768 | tf_op args[2]
  2.1 3.2 %shard_map.112 = (bf16[128,1408]{1,0:T(8,128)(2,1)}, bf16[128,1408]{1,0:T(8,128)(2,1)}, bf16[128,1408]{1,0:T(8,128)(2,1)}, bf16[128,1408]{1,0:T(8,128)(2,1)}, bf...) custom-call(bf16[128,4096]{1,0:T(8,128)(2,1)} %bitcast.8, ...), custom_call_target="tpu_custom_call" | custom-call | bytes 4194304 | tf_op jit(solution)/shard_map/pallas_call | solution.py:404
  5.2 3.0 %collective-permute-start.4 = (bf16[128,1408]{1,0:T(8,128)(2,1)}, bf16[128,1408]{1,0:T(8,128)(2,1)S(1)}, u32[]{:S(2)}, u32[]{:S(2)}) collective-permute-start(bf16[128,1408]{1,0:T(8,128)(2,1)} %get-tuple-element.44), channel_id=1, source_target_pairs={{0,1},{1,0},{2,3},{3,2},{4,5},{5,4},{6,7},{7,6},{8,9},{9,8},{10,11... | collective-permute-start | bytes 1081352 | tf_op jit(solution)/shard_map/ppermute | solution.py:402
  8.2 1.6 %collective-permute-start.5 = (bf16[128,1408]{1,0:T(8,128)(2,1)}, bf16[128,1408]{1,0:T(8,128)(2,1)S(1)}, u32[]{:S(2)}, u32[]{:S(2)}) collective-permute-start(bf16[128,1408]{1,0:T(8,128)(2,1)} %get-tuple-element.45), channel_id=1, source_target_pairs={{0,2},{1,3},{2,0},{3,1},{4,6},{5,7},{6,4},{7,5},{8,10},{9,11},{10,... | collective-permute-start | bytes 1081352 | tf_op jit(solution)/shard_map/ppermute | solution.py:402
  10.5 0.7 collective-permute-start.8
  11.1 0.7 collective-permute-start.9
  13.1 2.5 %collective-permute-start.1 = (bf16[128,1024]{1,0:T(8,128)(2,1)}, bf16[128,1024]{1,0:T(8,128)(2,1)S(1)}, u32[]{:S(2)}, u32[]{:S(2)}) collective-permute-start(bf16[128,1024]{1,0:T(8,128)(2,1)} %get-tuple-element.40), channel_id=1, source_target_pairs={{8,1},{9,0},{10,3},{11,2},{12,5},{13,4},{14,7},{15,6},{16,9},{17,8... | collective-permute-start | bytes 786440 | tf_op jit(solution)/shard_map/ppermute | solution.py:421
  15.5 2.2 %collective-permute-done.4.refs_1_ = bf16[128,1408]{1,0:T(8,128)(2,1)S(1)} collective-permute-done((bf16[128,1408]{1,0:T(8,128)(2,1)}, bf16[128,1408]{1,0:T(8,128)(2,1)S(1)}, u32[]{:S(2)}, u32[]{:S(2)}) %collective-permute-start.4) | collective-permute-done | bytes 360480 | tf_op jit(solution)/shard_map/ppermute | solution.py:402
  17.7 6.2 %collective-permute-start.2 = (bf16[128,1024]{1,0:T(8,128)(2,1)}, bf16[128,1024]{1,0:T(8,128)(2,1)S(1)}, u32[]{:S(2)}, u32[]{:S(2)}) collective-permute-start(bf16[128,1024]{1,0:T(8,128)(2,1)} %get-tuple-element.41), channel_id=1, source_target_pairs={{8,2},{9,3},{10,0},{11,1},{12,6},{13,7},{14,4},{15,5},{16,10},{17,... | collective-permute-start | bytes 786440 | tf_op jit(solution)/shard_map/ppermute | solution.py:421
  23.9 6.9 %collective-permute-start.3 = (bf16[128,1024]{1,0:T(8,128)(2,1)}, bf16[128,1024]{1,0:T(8,128)(2,1)S(1)}, u32[]{:S(2)}, u32[]{:S(2)}) collective-permute-start(bf16[128,1024]{1,0:T(8,128)(2,1)} %get-tuple-element.42), channel_id=1, source_target_pairs={{8,3},{9,2},{10,1},{11,0},{12,7},{13,6},{14,5},{15,4},{16,11},{17,... | collective-permute-start | bytes 786440 | tf_op jit(solution)/shard_map/ppermute | solution.py:421
  30.8 0.7 copy-done.17
  31.5 9.5 %shard_map.113 = (f32[512,1280]{1,0:T(8,128)}, f32[512,1280]{1,0:T(8,128)}, f32[512,128]{1,0:T(8,128)}, f32[512,128]{1,0:T(8,128)}, f32[512,128]{1,0:T(8,128)}, /*index=5*/f32[640,1024]{1,0:T(8,128)}) custom-call(bf16[128,1408]{1,0:T(8,128)(2,1)} %get-tuple-element.43.refs_0_, bf16[128,1408]{1,0:T(8,128)(2,1)} %copy-done.15, bf16[128,1408]{1,0:T(8,128)(2,1)} %copy-done.16, ...), custom_call_target="tpu_custom_call" | custom-call | flops 805306368 | bytes 4194304 | tf_op jit(solution)/shard_map/pallas_call | solution.py:425
  42.0 7.8 %shard_map.114 = (bf16[512,1024]{1,0:T(8,128)(2,1)}, f32[640,1024]{1,0:T(8,128)}, f32[128,1024]{1,0:T(8,128)}) custom-call(bf16[128,1024]{1,0:T(8,128)(2,1)} %copy-done.4, bf16[128,1024]{1,0:T(8,128)(2,1)} %copy-done.5, bf16[128,1024]{1,0:T(8,128)(2,1)} %copy-done.6, bf16[128,1024]{1,0:T(8,128)(2,1)} %copy-done.7, ...), custom_call_target="tpu_custom_call" | custom-call | flops 402653184 | bytes 4194304 | tf_op jit(solution)/shard_map/pallas_call | solution.py:433
  49.8 11.1 %shard_map.115 = (f32[512,1024]{1,0:T(8,128)}, f32[512,1024]{1,0:T(8,128)}, f32[512,128]{1,0:T(8,128)}) custom-call(f32[512,1280]{1,0:T(8,128)} %get-tuple-element.51.refs_4_.x_ref.refs_1_, f32[512,128]{1,0:T(8,128)} %get-tuple-element.56.st_ref.refs_3_, f32[512,128]{1,0:T(8,128)} %get-tuple-element.52.refs_5_.cum_ref, ...), custom_call_target="tpu_custom_call" | custom-call | flops 6710886400 | bytes 4194304 | tf_op jit(solution)/shard_map/pallas_call | solution.py:440
  60.9 11.9 %collective-permute-done.11.refs_0_ = f32[128,1024]{1,0:T(8,128)S(1)} collective-permute-done((f32[128,1024]{1,0:T(8,128)}, f32[128,1024]{1,0:T(8,128)S(1)}, u32[]{:S(2)}, u32[]{:S(2)}) %collective-permute-start.11) | collective-permute-done | bytes 524320 | tf_op jit(solution)/shard_map/ppermute | solution.py:402
  72.8 0.8 copy-done
  73.6 19.9 %shard_map.116 = (bf16[128,1152]{1,0:T(8,128)(2,1)}, bf16[128,1152]{1,0:T(8,128)(2,1)}, bf16[128,1152]{1,0:T(8,128)(2,1)}, bf16[128,1152]{1,0:T(8,128)(2,1)}, f3...) custom-call(f32[128,1024]{1,0:T(8,128)} %copy-done, ...), custom_call_target="tpu_custom_call" | custom-call | flops 1610612736 | bytes 4194304 | tf_op jit(solution)/shard_map/pallas_call | solution.py:446
  94.1 2.4 %collective-permute-start.15 = (f32[160,256]{1,0:T(8,128)}, f32[160,256]{1,0:T(8,128)S(1)}, u32[]{:S(2)}, u32[]{:S(2)}) collective-permute-start(f32[160,256]{1,0:T(8,128)} %get-tuple-element.68), channel_id=1, source_target_pairs={{0,1},{1,0},{2,3},{3,2},{4,5},{5,4},{6,7},{7,6},{8,9},{9,8},{10,11... | collective-permute-start | bytes 491528 | tf_op jit(solution)/shard_map/ppermute | solution.py:402
  97.1 2.9 %collective-permute-start.14 = (bf16[128,1152]{1,0:T(8,128)(2,1)}, bf16[128,1152]{1,0:T(8,128)(2,1)S(1)}, u32[]{:S(2)}, u32[]{:S(2)}) collective-permute-start(bf16[128,1152]{1,0:T(8,128)(2,1)} %get-tuple-element.66), channel_id=1, source_target_pairs={{0,3},{1,2},{2,1},{3,0},{4,7},{5,6},{6,5},{7,4},{8,11},{9,10},{10,... | collective-permute-start | bytes 884744 | tf_op jit(solution)/shard_map/ppermute | solution.py:402
  101.5 0.7 collective-permute-start.18
  102.7 26.2 %collective-permute-start.17 = (f32[160,256]{1,0:T(8,128)}, f32[160,256]{1,0:T(8,128)S(1)}, u32[]{:S(2)}, u32[]{:S(2)}) collective-permute-start(f32[160,256]{1,0:T(8,128)} %get-tuple-element.70), channel_id=1, source_target_pairs={{0,3},{1,2},{2,1},{3,0},{4,7},{5,6},{6,5},{7,4},{8,11},{9,10},{10,... | collective-permute-start | bytes 491528 | tf_op jit(solution)/shard_map/ppermute | solution.py:402
  128.9 5.2 %collective-permute-done.17.refs_7_ = f32[160,256]{1,0:T(8,128)S(1)} collective-permute-done((f32[160,256]{1,0:T(8,128)}, f32[160,256]{1,0:T(8,128)S(1)}, u32[]{:S(2)}, u32[]{:S(2)}) %collective-permute-start.17) | collective-permute-done | bytes 163872 | tf_op jit(solution)/shard_map/ppermute | solution.py:402
  135.1 2.6 %shard_map.117 = (bf16[128,4096]{1,0:T(8,128)(2,1)}, bf16[128,256]{1,0:T(8,128)(2,1)}, bf16[128,64]{1,0:T(8,128)(2,1)}) custom-call(bf16[128,1152]{1,0:T(8,128)(2,1)} %get-tuple-element.63.refs_0_, bf16[128,1152]{1,0:T(8,128)(2,1)} %copy-done.1, bf16[128,1152]{1,0:T(8,128)(2,1)} %copy-done.2, bf16[128,1152]{1,0:T(8,128)(2,1)} %copy-done.3, ...), custom_call_target="tpu_custom_call" | custom-call | bytes 4194304 | tf_op jit(solution)/shard_map/pallas_call | solution.py:462
  137.6 1.4 %copy.13 = bf16[1,128,64]{1,2,0:T(8,128)(2,1)} copy(bf16[1,128,64]{2,1,0:T(8,128)(2,1)} %bitcast.14) | data formatting | bytes 32768
  (72 shorter events, 6.8 us)
Async XLA Ops:
  5.2 12.5 %collective-permute-start.4 = (bf16[128,1408]{1,0:T(8,128)(2,1)}, bf16[128,1408]{1,0:T(8,128)(2,1)S(1)}, u32[]{:S(2)}, u32[]{:S(2)}) collective-permute-start(bf16[128,1408]{1,0:T(8,128)(2,1)} %get-tuple-element.44), channel_id=1, source_target_pairs={{0,1},{1,0},{2,3},{3,2},{4,5},{5,4},{6,7},{7,6},{8,9},{9,8},{10,11... | collective-permute-start | bytes 1081352 | tf_op jit(solution)/shard_map/ppermute | solution.py:402
  8.2 15.7 %collective-permute-start.5 = (bf16[128,1408]{1,0:T(8,128)(2,1)}, bf16[128,1408]{1,0:T(8,128)(2,1)S(1)}, u32[]{:S(2)}, u32[]{:S(2)}) collective-permute-start(bf16[128,1408]{1,0:T(8,128)(2,1)} %get-tuple-element.45), channel_id=1, source_target_pairs={{0,2},{1,3},{2,0},{3,1},{4,6},{5,7},{6,4},{7,5},{8,10},{9,11},{10,... | collective-permute-start | bytes 1081352 | tf_op jit(solution)/shard_map/ppermute | solution.py:402
  9.8 21.0 %collective-permute-start.6 = (bf16[128,1408]{1,0:T(8,128)(2,1)}, bf16[128,1408]{1,0:T(8,128)(2,1)S(1)}, u32[]{:S(2)}, u32[]{:S(2)}) collective-permute-start(bf16[128,1408]{1,0:T(8,128)(2,1)} %get-tuple-element.46), channel_id=1, source_target_pairs={{0,3},{1,2},{2,1},{3,0},{4,7},{5,6},{6,5},{7,4},{8,11},{9,10},{10,... | collective-permute-start | bytes 1081352 | tf_op jit(solution)/shard_map/ppermute | solution.py:402
  9.8 1.3 collective-permute-start.7
  10.5 1.4 collective-permute-start.8
  11.1 1.4 collective-permute-start.9
  11.8 1.2 collective-permute-start.10
  12.5 28.5 %collective-permute-start = (bf16[128,1024]{1,0:T(8,128)(2,1)}, bf16[128,1024]{1,0:T(8,128)(2,1)S(1)}, u32[]{:S(2)}, u32[]{:S(2)}) collective-permute-start(bf16[128,1024]{1,0:T(8,128)(2,1)} %get-tuple-element.39), channel_id=1, source_target_pairs={{8,0},{9,1},{10,2},{11,3},{12,4},{13,5},{14,6},{15,7},{16,8},{17,9... | collective-permute-start | bytes 786440 | tf_op jit(solution)/shard_map/ppermute | solution.py:421
  13.1 28.0 %collective-permute-start.1 = (bf16[128,1024]{1,0:T(8,128)(2,1)}, bf16[128,1024]{1,0:T(8,128)(2,1)S(1)}, u32[]{:S(2)}, u32[]{:S(2)}) collective-permute-start(bf16[128,1024]{1,0:T(8,128)(2,1)} %get-tuple-element.40), channel_id=1, source_target_pairs={{8,1},{9,0},{10,3},{11,2},{12,5},{13,4},{14,7},{15,6},{16,9},{17,8... | collective-permute-start | bytes 786440 | tf_op jit(solution)/shard_map/ppermute | solution.py:421
  17.7 23.3 %collective-permute-start.2 = (bf16[128,1024]{1,0:T(8,128)(2,1)}, bf16[128,1024]{1,0:T(8,128)(2,1)S(1)}, u32[]{:S(2)}, u32[]{:S(2)}) collective-permute-start(bf16[128,1024]{1,0:T(8,128)(2,1)} %get-tuple-element.41), channel_id=1, source_target_pairs={{8,2},{9,3},{10,0},{11,1},{12,6},{13,7},{14,4},{15,5},{16,10},{17,... | collective-permute-start | bytes 786440 | tf_op jit(solution)/shard_map/ppermute | solution.py:421
  23.9 17.2 %collective-permute-start.3 = (bf16[128,1024]{1,0:T(8,128)(2,1)}, bf16[128,1024]{1,0:T(8,128)(2,1)S(1)}, u32[]{:S(2)}, u32[]{:S(2)}) collective-permute-start(bf16[128,1024]{1,0:T(8,128)(2,1)} %get-tuple-element.42), channel_id=1, source_target_pairs={{8,3},{9,2},{10,1},{11,0},{12,7},{13,6},{14,5},{15,4},{16,11},{17,... | collective-permute-start | bytes 786440 | tf_op jit(solution)/shard_map/ppermute | solution.py:421
  49.8 23.0 %collective-permute-start.11 = (f32[128,1024]{1,0:T(8,128)}, f32[128,1024]{1,0:T(8,128)S(1)}, u32[]{:S(2)}, u32[]{:S(2)}) collective-permute-start(f32[128,1024]{1,0:T(8,128)} %get-tuple-element.54), channel_id=1, source_target_pairs={{0,4},{1,5},{2,6},{3,7},{4,0},{5,1},{6,2},{7,3},{8,12},{9,13},{10,... | collective-permute-start | bytes 1572872 | tf_op jit(solution)/shard_map/ppermute | solution.py:402
  93.5 6.6 %collective-permute-start.21 = (f32[8,1280]{1,0:T(8,128)}, f32[8,1280]{1,0:T(8,128)S(1)}, u32[]{:S(2)}, u32[]{:S(2)}) collective-permute-start(f32[8,1280]{1,0:T(8,128)} %get-tuple-element.71), channel_id=1, source_target_pairs={{7,3},{15,11},{23,19},{31,27}} | collective-permute-start | bytes 122888 | tf_op jit(solution)/shard_map/ppermute | solution.py:461
  94.1 8.6 %collective-permute-start.15 = (f32[160,256]{1,0:T(8,128)}, f32[160,256]{1,0:T(8,128)S(1)}, u32[]{:S(2)}, u32[]{:S(2)}) collective-permute-start(f32[160,256]{1,0:T(8,128)} %get-tuple-element.68), channel_id=1, source_target_pairs={{0,1},{1,0},{2,3},{3,2},{4,5},{5,4},{6,7},{7,6},{8,9},{9,8},{10,11... | collective-permute-start | bytes 491528 | tf_op jit(solution)/shard_map/ppermute | solution.py:402
  96.6 37.5 %collective-permute-start.12 = (bf16[128,1152]{1,0:T(8,128)(2,1)}, bf16[128,1152]{1,0:T(8,128)(2,1)S(1)}, u32[]{:S(2)}, u32[]{:S(2)}) collective-permute-start(bf16[128,1152]{1,0:T(8,128)(2,1)} %get-tuple-element.64), channel_id=1, source_target_pairs={{0,1},{1,0},{2,3},{3,2},{4,5},{5,4},{6,7},{7,6},{8,9},{9,8},{10,11... | collective-permute-start | bytes 884744 | tf_op jit(solution)/shard_map/ppermute | solution.py:402
  96.7 37.4 %collective-permute-start.13 = (bf16[128,1152]{1,0:T(8,128)(2,1)}, bf16[128,1152]{1,0:T(8,128)(2,1)S(1)}, u32[]{:S(2)}, u32[]{:S(2)}) collective-permute-start(bf16[128,1152]{1,0:T(8,128)(2,1)} %get-tuple-element.65), channel_id=1, source_target_pairs={{0,2},{1,3},{2,0},{3,1},{4,6},{5,7},{6,4},{7,5},{8,10},{9,11},{10,... | collective-permute-start | bytes 884744 | tf_op jit(solution)/shard_map/ppermute | solution.py:402
  97.1 37.0 %collective-permute-start.14 = (bf16[128,1152]{1,0:T(8,128)(2,1)}, bf16[128,1152]{1,0:T(8,128)(2,1)S(1)}, u32[]{:S(2)}, u32[]{:S(2)}) collective-permute-start(bf16[128,1152]{1,0:T(8,128)(2,1)} %get-tuple-element.66), channel_id=1, source_target_pairs={{0,3},{1,2},{2,1},{3,0},{4,7},{5,6},{6,5},{7,4},{8,11},{9,10},{10,... | collective-permute-start | bytes 884744 | tf_op jit(solution)/shard_map/ppermute | solution.py:402
  100.1 34.1 %copy-start.11 = (f32[8,1280]{1,0:T(8,128)}, f32[8,1280]{1,0:T(8,128)S(1)}, u32[]{:S(2)}) copy-start(f32[8,1280]{1,0:T(8,128)S(1)} %collective-permute-done.21.refs_11_) | copy-start | bytes 122884
  100.1 0.7 collective-permute-start.20
  100.7 33.4 %copy-start.12 = (f32[8,1280]{1,0:T(8,128)}, f32[8,1280]{1,0:T(8,128)S(1)}, u32[]{:S(2)}) copy-start(f32[8,1280]{1,0:T(8,128)S(1)} %collective-permute-done.20.refs_10_) | copy-start | bytes 122884
  100.8 0.7 collective-permute-start.19
  101.5 0.7 collective-permute-start.18
  102.1 26.8 %collective-permute-start.16 = (f32[160,256]{1,0:T(8,128)}, f32[160,256]{1,0:T(8,128)S(1)}, u32[]{:S(2)}, u32[]{:S(2)}) collective-permute-start(f32[160,256]{1,0:T(8,128)} %get-tuple-element.69), channel_id=1, source_target_pairs={{0,2},{1,3},{2,0},{3,1},{4,6},{5,7},{6,4},{7,5},{8,10},{9,11},{10,... | collective-permute-start | bytes 491528 | tf_op jit(solution)/shard_map/ppermute | solution.py:402
  102.7 31.4 %collective-permute-start.17 = (f32[160,256]{1,0:T(8,128)}, f32[160,256]{1,0:T(8,128)S(1)}, u32[]{:S(2)}, u32[]{:S(2)}) collective-permute-start(f32[160,256]{1,0:T(8,128)} %get-tuple-element.70), channel_id=1, source_target_pairs={{0,3},{1,2},{2,1},{3,0},{4,7},{5,6},{6,5},{7,4},{8,11},{9,10},{10,... | collective-permute-start | bytes 491528 | tf_op jit(solution)/shard_map/ppermute | solution.py:402
  (20 other events, 204.4 us)

commit v2 on v1

--- a/solution.py
+++ b/solution.py
@@ -67,7 +67,6 @@
         self.conv = self.width + 2 * state
         self.pay = self.conv + LANES
         self.out = self.width + LANES
-        self.edge = PAD * self.width // (2 * state)
 
 
 def place(plan):
@@ -80,25 +79,38 @@
         functools.partial(kernel, plan),
         out_shape=out_shape,
         scratch_shapes=list(scratch),
-        compiler_params=pltpu.CompilerParams(vmem_limit_bytes=56 * 1024 * 1024),
+        compiler_params=pltpu.CompilerParams(vmem_limit_bytes=32 * 1024 * 1024),
         cost_estimate=pl.CostEstimate(flops=flops, transcendentals=0, bytes_accessed=4 << 20),
     )
 
 
 def struct(*shape, dtype=F32):
     return jax.ShapeDtypeStruct(shape, dtype)
+
+
+def near(*shape, dtype=F32):
+    return pltpu.VMEM(shape, dtype)
+
+
+def head_rows(plan, prm, refs, own):
+    prm[...] = jnp.zeros_like(prm)
+    for row, values in enumerate(refs):
+        prm[row : row + 1, 0 : values.shape[1]] = values
+    local = pltpu.roll(prm[...], lax.rem(LANES - own * plan.heads, LANES), 1)
+    return [local[row : row + 1, :] for row in range(len(refs))]
 
 
 def pack_kernel(plan, f_ref, m_ref, s_ref, o_ref, *outs):
     own, _ = place(plan)
     half, width = plan.half, plan.width
+    steps = s_ref[...].astype(F32).T.astype(BF16)
     pays, edges, grads = outs[:half], outs[half : 2 * half], outs[2 * half :]
     for k in range(half):
         start = pl.multiple_of(jnp.bitwise_xor(own, k) * width, LANES)
         pays[k][:, :width] = f_ref[:, pl.ds(start, width)]
         pays[k][:, width : plan.conv] = m_ref[...]
         pays[k][:, plan.conv :] = jnp.zeros((BLOCK, LANES), BF16)
-        pays[k][:, plan.conv : plan.conv + s_ref.shape[1]] = s_ref[...]
+        pays[k][:, plan.conv : plan.conv + s_ref.shape[0]] = steps
         grads[k][...] = o_ref[:, pl.ds(start, width)]
         edges[k][:, :width] = f_ref[BLOCK - 16 :, k * width : (k + 1) * width]
         edges[k][:, width:] = m_ref[BLOCK - 16 :, :]
@@ -118,13 +130,8 @@
         block = jnp.bitwise_xor(own, k) * BLOCK
         raw[pl.ds(pl.multiple_of(block + PAD, 8), BLOCK), :] = pays[k][:, :conv].astype(F32)
         sraw[pl.ds(pl.multiple_of(block, 8), BLOCK), :] = pays[k][:, conv:].astype(F32)
-    heads_all = dl_ref.shape[1]
-    prm[...] = jnp.zeros_like(prm)
-    prm[0:1, 0:heads_all] = -jnp.exp(dl_ref[...])
-    prm[1:2, 0:heads_all] = sb_ref[...]
+    rates, offsets = head_rows(plan, prm, [-jnp.exp(dl_ref[...]), sb_ref[...]], own)
     shift = lax.rem(LANES - own * plan.heads, LANES)
-    local = pltpu.roll(prm[...], shift, 1)
-    rates, offsets = local[0:1, :], local[1:2, :]
     lower = (iota((BLOCK, BLOCK), 0) >= iota((BLOCK, BLOCK), 1)).astype(F32)
     el_ref[0:BLOCK, :] = jnp.zeros((BLOCK, width), F32)
     tile = 256 if width % 256 == 0 else LANES
@@ -201,8 +208,10 @@
         send_ref[...] = gl_ref[0:BLOCK, :]
 
 
-def within_kernel(plan, x_ref, st_ref, cum_ref, gy_ref, yw_ref, dw_ref, dsc_ref):
-    width, pairs = plan.width, plan.pairs
+def within_kernel(plan, x_ref, ds_ref, st_ref, cum_ref, gy_ref, gl_ref, sk_ref, yw_ref, dw_ref, dsc_ref, edge_ref, prm):
+    width, pairs, state = plan.width, plan.pairs, plan.state
+    own, _ = place(plan)
+    (skips,) = head_rows(plan, prm, [sk_ref[...]], own)
     causal = iota((BLOCK, BLOCK), 0) >= iota((BLOCK, BLOCK), 1)
     left = iota((BLOCK, LANES), 1) < HEAD
 
@@ -247,25 +256,49 @@
         return carry
 
     lax.fori_loop(0, plan.blocks, body, 0)
+    top = slice(0, 16)
+    cum, step = cum_ref[top, :], st_ref[top, :]
+    shrunk, grown = jnp.exp(cum_ref[BLOCK - 1 : BLOCK, :] - cum), jnp.exp(cum)
+    dsc = split(dsc_ref[0:BLOCK, :])
+    first_b = split(x_ref[top, width : width + state])
+    d_b = mm3(tuple(part.T for part in split(dsc_ref[0:BLOCK, :])), split(x_ref[0:BLOCK, width + state :]))[top]
+    d_c = mm3(dsc, split(x_ref[0:BLOCK, width : width + state]))[top]
+    edge_ref[...] = jnp.zeros_like(edge_ref)
+    for i in range(pairs):
+        leaving = split(gl_ref[BLOCK : 2 * BLOCK, lanes(i)])
+        xs = x_ref[top, lanes(i)] * expand(step, i)
+        gy = gy_ref[top, lanes(i)].astype(F32)
+        shrunk_x = expand(shrunk, i)
+        dxs = dw_ref[top, lanes(i)] + shrunk_x * mm3(first_b, leaving)
+        d_b = d_b + mm3(split(xs * shrunk_x), leaving, NT)
+        dzx = (dxs * expand(step, i) + expand(skips, i) * gy) * ds_ref[top, lanes(i)]
+        edge_ref[0:PAD, lanes(i)] = dzx[0:PAD]
+        edge_ref[PAD : 2 * PAD, lanes(i)] = (gy * expand(grown, i))[0:PAD]
+    edge_ref[2 * PAD : 3 * PAD, 0:state] = (d_b * ds_ref[top, width : width + state])[0:PAD]
+    edge_ref[2 * PAD : 3 * PAD, state : 2 * state] = d_c[0:PAD]
+    edge_ref[3 * PAD : 4 * PAD, 0:state] = ds_ref[0:PAD, width + state :]
 
 
 def final_kernel(plan, *refs):
     half, width, conv, pairs, blocks, state = plan.half, plan.width, plan.conv, plan.pairs, plan.blocks, plan.state
-    (got_ref, x_ref, ds_ref, st_ref, sg_ref, cum_ref, el_ref, gl_ref, gy_ref, yw_ref, dw_ref, dsc_ref,
-     cw_ref, dl_ref, sk_ref) = refs[:15]
-    outs, maps, halos = refs[15 : 15 + half], refs[15 + half : 15 + 2 * half], refs[15 + 2 * half]
-    prm, dz, nxt_dz, carry_ref, o_sc, m_sc, e_sc, lc_sc = refs[16 + 2 * half :]
+    (got_ref, edge_ref, x_ref, ds_ref, st_ref, sg_ref, cum_ref, el_ref, gl_ref, gy_ref, yw_ref, dw_ref, dsc_ref,
+     cw_ref, dl_ref, sk_ref) = refs[:16]
+    outs, maps = refs[16 : 16 + half], refs[16 + half : 16 + 2 * half]
+    prm, dz, nxt_dz, carry_ref, o_sc, m_sc, lc_sc = refs[16 + 2 * half :]
     own, late = place(plan)
     is_late = late.astype(F32)
-    heads_all = dl_ref.shape[1]
-    prm[...] = jnp.zeros_like(prm)
-    prm[0:1, 0:heads_all] = -jnp.exp(dl_ref[...])
-    prm[1:2, 0:heads_all] = sk_ref[...]
-    shift = lax.rem(LANES - own * plan.heads, LANES)
-    local = pltpu.roll(prm[...], shift, 1)
-    rates, skips = local[0:1, :], local[1:2, :]
+    rates, skips = head_rows(plan, prm, [-jnp.exp(dl_ref[...]), sk_ref[...]], own)
     upper = (iota((BLOCK, BLOCK), 0) <= iota((BLOCK, BLOCK), 1)).astype(F32)
-    nxt_dz[...] = jnp.zeros_like(nxt_dz)
+    after_c = jnp.zeros((2 * PAD, state), F32)
+    for i in range(pairs):
+        leaving_s = split(el_ref[blocks * BLOCK :, lanes(i)])
+        after_c = after_c + mm3(split(edge_ref[PAD : 3 * PAD, lanes(i)]), leaving_s, NT)
+    after_c = (after_c[0:PAD] + edge_ref[2 * PAD : 3 * PAD, state : 2 * state]) * edge_ref[3 * PAD : 4 * PAD, 0:state]
+    early = iota((PAD, LANES), 0) * 0 + late == 0
+    for i in range(pairs):
+        nxt_dz[:, lanes(i)] = jnp.where(early, edge_ref[0:PAD, lanes(i)], 0.0)
+    nxt_dz[:, width : width + state] = jnp.where(early, edge_ref[2 * PAD : 3 * PAD, 0:state], 0.0)
+    nxt_dz[:, width + state :] = jnp.where(early, after_c, 0.0)
     lc_sc[...] = jnp.zeros_like(lc_sc)
     for b in range(1, blocks):
         lc_sc[b : b + 1, :] = lc_sc[b - 1 : b, :] + cum_ref[b * BLOCK - 1 : b * BLOCK, :]
@@ -330,17 +363,8 @@
                 grad = grad + weight[k : k + 1, :] * window[k : k + BLOCK, :]
             if c < width:
                 o_sc[rows, c : c + LANES] = grad.astype(BF16)
-                e_sc[pl.ds(pl.multiple_of(b * PAD, PAD), PAD), c : c + LANES] = grad[BLOCK - PAD :, :]
             else:
                 m_sc[rows, c - width : c - width + LANES] = grad
-
-            @pl.when(b == 0)
-            def _():
-                padded = jnp.concatenate([jnp.zeros((PAD, LANES), F32), window[0:PAD, :]], axis=0)
-                spill = jnp.zeros((PAD, LANES), F32)
-                for k in range(1, weight.shape[0]):
-                    spill = spill + weight[k : k + 1, :] * padded[k : k + PAD, :]
-                halos[:, c : c + LANES] = spill
 
         nxt_dz[...] = dz[0:PAD, :]
         return carry
@@ -350,45 +374,24 @@
         b = jnp.bitwise_xor(own, k)
         rows = pl.ds(pl.multiple_of(b * BLOCK, BLOCK), BLOCK)
         outs[k][...] = o_sc[rows, :]
-        maps[k][0:BLOCK, :] = m_sc[rows, :]
-        step = 2 * state
-        for part in range(width // step):
-            maps[k][BLOCK + part * PAD : BLOCK + (part + 1) * PAD, :] = e_sc[
-                pl.ds(pl.multiple_of(b * PAD, PAD), PAD), part * step : (part + 1) * step
-            ]
+        maps[k][...] = m_sc[rows, :]
 
 
 def owner_kernel(plan, *refs):
-    half, width, state = plan.half, plan.width, plan.state
-    outs, maps, halos = refs[:half], refs[half : 2 * half], refs[2 * half : 3 * half]
-    f_ref, m_ref, s_ref, edge = refs[3 * half :]
+    half, width = plan.half, plan.width
+    outs, maps = refs[:half], refs[half : 2 * half]
+    f_ref, m_ref, s_ref = refs[2 * half :]
     own, _ = place(plan)
-    total = maps[0][0:BLOCK, :]
-    spill = halos[0][:, width:]
+    total = maps[0][...]
     steps = jnp.zeros((BLOCK, LANES), F32)
-    span = 2 * state
     for k in range(half):
         part = jnp.bitwise_xor(own, k)
-        start = pl.multiple_of(part * width, LANES)
-        f_ref[:, pl.ds(start, width)] = outs[k][:, :width]
-        for piece in range(width // span):
-            edge[:, pl.ds(pl.multiple_of(start + piece * span, LANES), span)] = maps[k][
-                BLOCK + piece * PAD : BLOCK + (piece + 1) * PAD, :
-            ]
+        f_ref[:, pl.ds(pl.multiple_of(part * width, LANES), width)] = outs[k][:, :width]
         steps = steps + pltpu.roll(outs[k][:, width:].astype(F32), part * plan.heads, 1)
         if k:
-            total = total + maps[k][0:BLOCK, :]
-            spill = spill + halos[k][:, width:]
-    for k in range(half):
-        cols = slice(k * width, (k + 1) * width)
-        fixed = edge[:, cols] + halos[k][:, :width]
-        tail = f_ref[BLOCK - 16 :, cols].astype(F32)
-        f_ref[BLOCK - 16 :, cols] = jnp.concatenate([tail[:PAD], fixed], axis=0).astype(BF16)
-    m_ref[0 : BLOCK - 16, :] = total[0 : BLOCK - 16].astype(BF16)
-    m_ref[BLOCK - 16 :, :] = jnp.concatenate(
-        [total[BLOCK - 16 : BLOCK - PAD], total[BLOCK - PAD :] + spill], axis=0
-    ).astype(BF16)
-    s_ref[...] = steps[:, : s_ref.shape[1]].astype(BF16)
+            total = total + maps[k][...]
+    m_ref[...] = total.astype(BF16)
+    s_ref[...] = steps.T[: s_ref.shape[0]].astype(BF16)
 
 
 def per_device(sections, devices, features, state_maps, step_raw, conv_weight, conv_bias, decay_log, step_bias, skip_gain, output_grads):
@@ -407,7 +410,7 @@
         [struct(BLOCK, plan.pay, dtype=BF16)] * half
         + [struct(16, conv, dtype=BF16)] * half
         + [struct(BLOCK, width, dtype=BF16)] * half,
-    )(features[0], state_maps[0], step_raw[0], output_grads[0])
+    )(features[0], state_maps[0], step_raw[0].T, output_grads[0])
     pays, edges, grads = packed[:half], packed[half : 2 * half], packed[2 * half :]
     edges = [lax.ppermute(e, "ctx", [(half - 1, half + k)]) for k, e in enumerate(edges)]
     pays = [pays[0]] + [partner(pays[k], k) for k in range(1, half)]
@@ -425,47 +428,45 @@
     x_conv, dsilu, steps, sigmoids, cums, states = call(
         forward_kernel,
         plan,
-        [struct(tokens, conv), struct(tokens, conv), struct(tokens, LANES), struct(tokens, LANES),
-         struct(tokens, LANES), struct(tokens + BLOCK, width)],
+        [near(tokens, conv), near(tokens, conv), near(tokens, LANES), near(tokens, LANES),
+         near(tokens, LANES), near(tokens + BLOCK, width)],
         [pltpu.VMEM((tokens + PAD, conv), F32), pltpu.VMEM((tokens, LANES), F32), pltpu.VMEM((8, LANES), F32)],
         flops=6 * big,
     )(*pays, *edges, weight, conv_bias, decay_log, step_bias)
     gy, back, send = call(
         gradient_kernel,
         plan,
-        [struct(tokens, width, dtype=BF16), struct(tokens + BLOCK, width), struct(BLOCK, width)],
+        [near(tokens, width, dtype=BF16), near(tokens + BLOCK, width), struct(BLOCK, width)],
         flops=3 * big,
     )(*grads, x_conv, cums, states)
     got = partner(send, half)
-    y_within, d_within, d_scores = call(
+    y_within, d_within, d_scores, edge = call(
         within_kernel,
         plan,
-        [struct(tokens, width), struct(tokens, width), struct(tokens, BLOCK)],
+        [near(tokens, width), near(tokens, width), near(tokens, BLOCK), struct(4 * PAD, width)],
+        [pltpu.VMEM((8, LANES), F32)],
         flops=50 * big,
-    )(x_conv, steps, cums, gy)
+    )(x_conv, dsilu, steps, cums, gy, back, skip_gain)
+    edge = partner(edge, half)
     results = call(
         final_kernel,
         plan,
-        [struct(BLOCK, plan.out, dtype=BF16)] * half
-        + [struct(BLOCK + plan.edge, 2 * state)] * half
-        + [struct(PAD, conv)],
+        [struct(BLOCK, plan.out, dtype=BF16)] * half + [struct(BLOCK, 2 * state)] * half,
         [pltpu.VMEM((8, LANES), F32), pltpu.VMEM((BLOCK + PAD, conv), F32), pltpu.VMEM((PAD, conv), F32),
          pltpu.VMEM((8, LANES), F32), pltpu.VMEM((tokens, plan.out), BF16), pltpu.VMEM((tokens, 2 * state), F32),
-         pltpu.VMEM((PAD * plan.blocks, width), F32), pltpu.VMEM((max(8, plan.blocks), LANES), F32)],
+         pltpu.VMEM((max(8, plan.blocks), LANES), F32)],
         flops=12 * big,
-    )(got, x_conv, dsilu, steps, sigmoids, cums, states, back, gy, y_within, d_within, d_scores,
+    )(got, edge, x_conv, dsilu, steps, sigmoids, cums, states, back, gy, y_within, d_within, d_scores,
       weight, decay_log, skip_gain)
-    outs, maps, halo = results[:half], results[half : 2 * half], results[2 * half]
+    outs, maps = results[:half], results[half:]
     outs = [outs[0]] + [partner(outs[k], k) for k in range(1, half)]
     maps = [maps[0]] + [partner(maps[k], k) for k in range(1, half)]
-    halos = [lax.ppermute(halo, "ctx", [(half + k, half - 1)]) for k in range(half)]
     feature_grads, map_grads, step_grads = call(
         owner_kernel,
         plan,
-        [struct(BLOCK, plan.inner, dtype=BF16), struct(BLOCK, 2 * state, dtype=BF16), struct(BLOCK, heads, dtype=BF16)],
-        [pltpu.VMEM((PAD, plan.inner), F32)],
-    )(*outs, *maps, *halos)
-    return (feature_grads[None], map_grads[None], step_grads[None])
+        [struct(BLOCK, plan.inner, dtype=BF16), struct(BLOCK, 2 * state, dtype=BF16), struct(heads, BLOCK, dtype=BF16)],
+    )(*outs, *maps)
+    return (feature_grads[None], map_grads[None], step_grads.T[None])
 
 
 def solution(mesh):

time: 140 us -> 111 us (0.79)
  starting transfers between devices: 58.6 us -> 32.4 us
  Pallas kernels: 54 us -> 29.5 us
  waiting for transfers between devices: 19.3 us -> 40.7 us
    ppermute x10 -> x11, starting transfers between devices: 37.2 us -> 13.6 us  [partner(): return lax.ppermute(array, 'ctx', [(i, i ^ k) for i in range(devices)])]
    ppermute x10 -> x11, waiting for transfers between devices: 19.2 us -> 40.7 us  [partner(): return lax.ppermute(array, 'ctx', [(i, i ^ k) for i in range(devices)])]
    pallas_call x3, Pallas kernels: 28.4 us -> 15.7 us  [the longest x1 7.84 us: per_device(): call(within_kernel, plan, [near(tokens, width), near(tokens, width), near...]
    pallas_call x1, Pallas kernels: 19.9 us -> 12.5 us  [per_device(): call(final_kernel, plan, [struct(BLOCK, plan.out, dtype=BF16)] * half + [...]
    pallas_call x1, Pallas kernels: 3.18 us -> 0.2 us  [per_device(): call(pack_kernel, plan, [struct(BLOCK, plan.pay, dtype=BF16)] * half + [s...]
    ppermute x4 -> x0, starting transfers between devices: 2.63 us -> none  [per_device(): lax.ppermute(halo, 'ctx', [(half + k, half - 1)])]
    unnamed x46 -> x22, local copies, waits for them, and re-layouts: 6.26 us -> 6.92 us
  transfers between devices with their start and end apart: 22 -> 19, of which waited for: 3 -> 5; matrix products, arithmetic and copies ran while one was open for 0% -> 0% of each run, Pallas kernels for 15% -> 12%
where the time goes in v2:
time: 111 us; the launch traced here: 110 us
  waiting for transfers between devices  40.7 us (37%)
  starting transfers between devices  32.4 us (29%)
  Pallas kernels  29.5 us (27%)
  local copies, waits for them, and re-layouts  6.92 us (6%)
    ppermute x11, waiting for transfers between devices, partner(): return lax.ppermute(array, 'ctx', [(i, i ^ k) for i in range(devices)])  40.7 us
    ppermute x4, starting transfers between devices, shifted(): return lax.ppermute(array, ('pipe', 'ctx'), route)  16.1 us
    ppermute x11, starting transfers between devices, partner(): return lax.ppermute(array, 'ctx', [(i, i ^ k) for i in range(devices)])  13.6 us
    pallas_call x1, Pallas kernels, per_device(): call(final_kernel, plan, [struct(BLOCK, plan.out, dtype=BF16)] * half + [...  12.5 us
    pallas_call x1, Pallas kernels, per_device(): call(within_kernel, plan, [near(tokens, width), near(tokens, width), near...  7.84 us
    unnamed x22, local copies, waits for them, and re-layouts  6.92 us
    pallas_call x1, Pallas kernels, per_device(): call(forward_kernel, plan, [near(tokens, conv), near(tokens, conv), near(...  5.03 us
    pallas_call x1, Pallas kernels, per_device(): call(gradient_kernel, plan, [near(tokens, width, dtype=BF16), near(tokens...  2.82 us
  transfers between devices with their start and end apart: 19, of which 5 were waited for; matrix products, arithmetic and copies ran while one was open for 0% of the time, Pallas kernels for 12%

profile of v2, /device:TPU:0, one launch (start us, length us, event | category | flops | bytes accessed | tf_op | source)
XLA Modules:
  0.0 110.3 jit_solution(9225909767805955639)
XLA Ops:
  0.6 1.2 %copy-done = bf16[1,128,4096]{2,1,0:T(8,128)(2,1)S(1)} copy-done((bf16[1,128,4096]{2,1,0:T(8,128)(2,1)S(1)}, bf16[1,128,4096]{2,1,0:T(8,128)(2,1)}, u32[]{:S(2)}) %copy-start) | copy-done | bytes 1048600
  1.9 1.2 %copy-done.1 = bf16[1,128,4096]{2,1,0:T(8,128)(2,1)S(1)} copy-done((bf16[1,128,4096]{2,1,0:T(8,128)(2,1)S(1)}, bf16[1,128,4096]{2,1,0:T(8,128)(2,1)}, u32[]{:S(2)}) %copy-start.1) | copy-done | bytes 1048600
  3.1 0.8 copy-done.4
  4.8 3.0 %collective-permute-start.4 = (bf16[128,1408]{1,0:T(8,128)(2,1)S(1)}, bf16[128,1408]{1,0:T(8,128)(2,1)S(1)}, u32[]{:S(2)}, u32[]{:S(2)}) collective-permute-start(bf16[128,1408]{1,0:T(8,128)(2,1)S(1)} %get-tuple-element.44), channel_id=1, source_target_pairs={{0,1},{1,0},{2,3},{3,2},{4,5},{5,4},{6,7},{7,6},{8,9},{9,8},{10,11... | collective-permute-start | bytes 1081352 | tf_op jit(solution)/shard_map/ppermute | solution.py:405
  7.9 1.6 %collective-permute-start.5 = (bf16[128,1408]{1,0:T(8,128)(2,1)S(1)}, bf16[128,1408]{1,0:T(8,128)(2,1)S(1)}, u32[]{:S(2)}, u32[]{:S(2)}) collective-permute-start(bf16[128,1408]{1,0:T(8,128)(2,1)S(1)} %get-tuple-element.45), channel_id=1, source_target_pairs={{0,2},{1,3},{2,0},{3,1},{4,6},{5,7},{6,4},{7,5},{8,10},{9,11},{10,... | collective-permute-start | bytes 1081352 | tf_op jit(solution)/shard_map/ppermute | solution.py:405
  12.7 2.5 %collective-permute-start.1 = (bf16[128,1024]{1,0:T(8,128)(2,1)S(1)}, bf16[128,1024]{1,0:T(8,128)(2,1)S(1)}, u32[]{:S(2)}, u32[]{:S(2)}) collective-permute-start(bf16[128,1024]{1,0:T(8,128)(2,1)S(1)} %get-tuple-element.40), channel_id=1, source_target_pairs={{8,1},{9,0},{10,3},{11,2},{12,5},{13,4},{14,7},{15,6},{16,9},{17,8... | collective-permute-start | bytes 786440 | tf_op jit(solution)/shard_map/ppermute | solution.py:424
  15.2 2.1 %collective-permute-done.4.refs_1_ = bf16[128,1408]{1,0:T(8,128)(2,1)S(1)} collective-permute-done((bf16[128,1408]{1,0:T(8,128)(2,1)S(1)}, bf16[128,1408]{1,0:T(8,128)(2,1)S(1)}, u32[]{:S(2)}, u32[]{:S(2)}) %collective-permute-start.4) | collective-permute-done | bytes 360480 | tf_op jit(solution)/shard_map/ppermute | solution.py:405
  17.2 5.7 %collective-permute-start.2 = (bf16[128,1024]{1,0:T(8,128)(2,1)S(1)}, bf16[128,1024]{1,0:T(8,128)(2,1)S(1)}, u32[]{:S(2)}, u32[]{:S(2)}) collective-permute-start(bf16[128,1024]{1,0:T(8,128)(2,1)S(1)} %get-tuple-element.41), channel_id=1, source_target_pairs={{8,2},{9,3},{10,0},{11,1},{12,6},{13,7},{14,4},{15,5},{16,10},{17,... | collective-permute-start | bytes 786440 | tf_op jit(solution)/shard_map/ppermute | solution.py:424
  22.9 7.4 %collective-permute-start.3 = (bf16[128,1024]{1,0:T(8,128)(2,1)S(1)}, bf16[128,1024]{1,0:T(8,128)(2,1)S(1)}, u32[]{:S(2)}, u32[]{:S(2)}) collective-permute-start(bf16[128,1024]{1,0:T(8,128)(2,1)S(1)} %get-tuple-element.42), channel_id=1, source_target_pairs={{8,3},{9,2},{10,1},{11,0},{12,7},{13,6},{14,5},{15,4},{16,11},{17,... | collective-permute-start | bytes 786440 | tf_op jit(solution)/shard_map/ppermute | solution.py:424
  30.4 0.9 copy-done.2
  31.9 0.7 copy-done.9
  33.3 5.0 %shard_map.113 = (f32[512,1280]{1,0:T(8,128)S(1)}, f32[512,1280]{1,0:T(8,128)S(1)}, f32[512,128]{1,0:T(8,128)S(1)}, f32[512,128]{1,0:T(8,128)S(1)}, f32[512,128]{1,0:T(8,128)S(1)}, /*index=5*/f32[640,1024]{1,0:T(8,128)S(1)}) custom-call(bf16[128,1408]{1,0:T(8,128)(2,1)S(1)} %get-tuple-element.43.refs_0_, ...), custom_call_target="tpu_custom_call" | custom-call | flops 805306368 | bytes 4194304 | tf_op jit(solution)/shard_map/pallas_call | solution.py:428
  38.4 2.8 %shard_map.114 = (bf16[512,1024]{1,0:T(8,128)(2,1)S(1)}, f32[640,1024]{1,0:T(8,128)S(1)}, f32[128,1024]{1,0:T(8,128)S(1)}) custom-call(bf16[128,1024]{1,0:T(8,128)(2,1)S(1)} %collective-permute-done.refs_0_, bf16[128,1024]{1,0:T(8,128)(2,1)S(1)} %collective-permute-done.1.refs_1_, bf16[128,1024]{1,0:T(8,128)(2,1)S(1)} %collective-permute-done.2.refs_2_, ...), custom_call_target="tpu_custom_call" | custom-call | flops 402653184 | bytes 4194304 | tf_op jit(solution)/shard_map/pallas_call | solution.py:436
  41.3 7.8 %shard_map.115 = (f32[512,1024]{1,0:T(8,128)S(1)}, f32[512,1024]{1,0:T(8,128)S(1)}, f32[512,128]{1,0:T(8,128)S(1)}, f32[32,1024]{1,0:T(8,128)S(1)}) custom-call(f32[512,1280]{1,0:T(8,128)S(1)} %get-tuple-element.51.refs_4_.x_ref.refs_2_, f32[512,1280]{1,0:T(8,128)S(1)} %get-tuple-element.55.ds_ref.refs_3_, f32[512,128]{1,0:T(8,128)S(1)} %get-tuple-element.56.st_ref.refs_4_, ...), custom_call_target="tpu_custom_call" | custom-call | flops 6710886400 | bytes 4194304 | tf_op jit(solution)/shard_map/pallas_call | solution.py:443
  49.1 2.9 %collective-permute-start.12 = (f32[32,1024]{1,0:T(8,128)S(1)}, f32[32,1024]{1,0:T(8,128)S(1)}, u32[]{:S(2)}, u32[]{:S(2)}) collective-permute-start(f32[32,1024]{1,0:T(8,128)S(1)} %get-tuple-element.59), channel_id=1, source_target_pairs={{0,4},{1,5},{2,6},{3,7},{4,0},{5,1},{6,2},{7,3},{8,12},{9,13},{10,... | collective-permute-start | bytes 393224 | tf_op jit(solution)/shard_map/ppermute | solution.py:405
  52.0 19.8 %collective-permute-done.12.refs_1_ = f32[32,1024]{1,0:T(8,128)S(1)} collective-permute-done((f32[32,1024]{1,0:T(8,128)S(1)}, f32[32,1024]{1,0:T(8,128)S(1)}, u32[]{:S(2)}, u32[]{:S(2)}) %collective-permute-start.12) | collective-permute-done | bytes 131104 | tf_op jit(solution)/shard_map/ppermute | solution.py:405
  71.8 12.5 %shard_map.116 = (bf16[128,1152]{1,0:T(8,128)(2,1)S(1)}, bf16[128,1152]{1,0:T(8,128)(2,1)S(1)}, bf16[128,1152]{1,0:T(8,128)(2,1)S(1)}, bf16[128,1152]{1,0:T(8,12...) custom-call(f32[128,1024]{1,0:T(8,128)S(1)} %collective-permute-done, ...), custom_call_target="tpu_custom_call" | custom-call | flops 1610612736 | bytes 4194304 | tf_op jit(solution)/shard_map/pallas_call | solution.py:451
  84.3 2.5 %collective-permute-start.13 = (bf16[128,1152]{1,0:T(8,128)(2,1)S(1)}, bf16[128,1152]{1,0:T(8,128)(2,1)S(1)}, u32[]{:S(2)}, u32[]{:S(2)}) collective-permute-start(bf16[128,1152]{1,0:T(8,128)(2,1)S(1)} %get-tuple-element.65), channel_id=1, source_target_pairs={{0,1},{1,0},{2,3},{3,2},{4,5},{5,4},{6,7},{7,6},{8,9},{9,8},{10,11... | collective-permute-start | bytes 884744 | tf_op jit(solution)/shard_map/ppermute | solution.py:405
  86.8 1.5 %collective-permute-start.15 = (bf16[128,1152]{1,0:T(8,128)(2,1)S(1)}, bf16[128,1152]{1,0:T(8,128)(2,1)S(1)}, u32[]{:S(2)}, u32[]{:S(2)}) collective-permute-start(bf16[128,1152]{1,0:T(8,128)(2,1)S(1)} %get-tuple-element.67), channel_id=1, source_target_pairs={{0,3},{1,2},{2,1},{3,0},{4,7},{5,6},{6,5},{7,4},{8,11},{9,10},{10,... | collective-permute-start | bytes 884744 | tf_op jit(solution)/shard_map/ppermute | solution.py:405
  88.4 1.9 %collective-permute-start.16 = (f32[128,256]{1,0:T(8,128)S(1)}, f32[128,256]{1,0:T(8,128)S(1)}, u32[]{:S(2)}, u32[]{:S(2)}) collective-permute-start(f32[128,256]{1,0:T(8,128)S(1)} %get-tuple-element.69), channel_id=1, source_target_pairs={{0,1},{1,0},{2,3},{3,2},{4,5},{5,4},{6,7},{7,6},{8,9},{9,8},{10,11... | collective-permute-start | bytes 393224 | tf_op jit(solution)/shard_map/ppermute | solution.py:405
  90.3 12.9 %collective-permute-done.16.refs_5_ = f32[128,256]{1,0:T(8,128)S(1)} collective-permute-done((f32[128,256]{1,0:T(8,128)S(1)}, f32[128,256]{1,0:T(8,128)S(1)}, u32[]{:S(2)}, u32[]{:S(2)}) %collective-permute-start.16) | collective-permute-done | bytes 131104 | tf_op jit(solution)/shard_map/ppermute | solution.py:405
  103.3 1.5 %collective-permute-done.17.refs_6_ = f32[128,256]{1,0:T(8,128)S(1)} collective-permute-done((f32[128,256]{1,0:T(8,128)S(1)}, f32[128,256]{1,0:T(8,128)S(1)}, u32[]{:S(2)}, u32[]{:S(2)}) %collective-permute-start.17) | collective-permute-done | bytes 131104 | tf_op jit(solution)/shard_map/ppermute | solution.py:405
  104.8 4.4 %collective-permute-done.18.refs_7_ = f32[128,256]{1,0:T(8,128)S(1)} collective-permute-done((f32[128,256]{1,0:T(8,128)S(1)}, f32[128,256]{1,0:T(8,128)S(1)}, u32[]{:S(2)}, u32[]{:S(2)}) %collective-permute-start.18) | collective-permute-done | bytes 131104 | tf_op jit(solution)/shard_map/ppermute | solution.py:405
  109.2 1.2 %shard_map.117 = (bf16[128,4096]{1,0:T(8,128)(2,1)}, bf16[128,256]{1,0:T(8,128)(2,1)}, bf16[64,128]{1,0:T(8,128)(2,1)}) custom-call(bf16[128,1152]{1,0:T(8,128)(2,1)S(1)} %get-tuple-element.64.refs_0_, bf16[128,1152]{1,0:T(8,128)(2,1)S(1)} %collective-permute-done.13.refs_1_, bf16[128,1152]{1,0:T(8,128)(2,1)S(1)} %collective-permute-done.14.refs_2_, ...), custom_call_target="tpu_custom_call" | custom-call | bytes 4194304 | tf_op jit(solution)/shard_map/pallas_call | solution.py:464
  (42 shorter events, 5.6 us)
Async XLA Ops:
  0.6 1.2 %copy-start = (bf16[1,128,4096]{2,1,0:T(8,128)(2,1)S(1)}, bf16[1,128,4096]{2,1,0:T(8,128)(2,1)}, u32[]{:S(2)}) copy-start(bf16[1,128,4096]{2,1,0:T(8,128)(2,1)} %param.9) | copy-start | bytes 3145732
  1.9 1.2 %copy-start.1 = (bf16[1,128,4096]{2,1,0:T(8,128)(2,1)S(1)}, bf16[1,128,4096]{2,1,0:T(8,128)(2,1)}, u32[]{:S(2)}) copy-start(bf16[1,128,4096]{2,1,0:T(8,128)(2,1)} %param.17) | copy-start | bytes 3145732
  4.8 12.4 %collective-permute-start.4 = (bf16[128,1408]{1,0:T(8,128)(2,1)S(1)}, bf16[128,1408]{1,0:T(8,128)(2,1)S(1)}, u32[]{:S(2)}, u32[]{:S(2)}) collective-permute-start(bf16[128,1408]{1,0:T(8,128)(2,1)S(1)} %get-tuple-element.44), channel_id=1, source_target_pairs={{0,1},{1,0},{2,3},{3,2},{4,5},{5,4},{6,7},{7,6},{8,9},{9,8},{10,11... | collective-permute-start | bytes 1081352 | tf_op jit(solution)/shard_map/ppermute | solution.py:405
  7.9 15.1 %collective-permute-start.5 = (bf16[128,1408]{1,0:T(8,128)(2,1)S(1)}, bf16[128,1408]{1,0:T(8,128)(2,1)S(1)}, u32[]{:S(2)}, u32[]{:S(2)}) collective-permute-start(bf16[128,1408]{1,0:T(8,128)(2,1)S(1)} %get-tuple-element.45), channel_id=1, source_target_pairs={{0,2},{1,3},{2,0},{3,1},{4,6},{5,7},{6,4},{7,5},{8,10},{9,11},{10,... | collective-permute-start | bytes 1081352 | tf_op jit(solution)/shard_map/ppermute | solution.py:405
  9.5 20.9 %collective-permute-start.6 = (bf16[128,1408]{1,0:T(8,128)(2,1)S(1)}, bf16[128,1408]{1,0:T(8,128)(2,1)S(1)}, u32[]{:S(2)}, u32[]{:S(2)}) collective-permute-start(bf16[128,1408]{1,0:T(8,128)(2,1)S(1)} %get-tuple-element.46), channel_id=1, source_target_pairs={{0,3},{1,2},{2,1},{3,0},{4,7},{5,6},{6,5},{7,4},{8,11},{9,10},{10,... | collective-permute-start | bytes 1081352 | tf_op jit(solution)/shard_map/ppermute | solution.py:405
  9.5 1.3 %collective-permute-start.7 = (bf16[16,1280]{1,0:T(8,128)(2,1)S(1)}, bf16[16,1280]{1,0:T(8,128)(2,1)S(1)}, u32[]{:S(2)}, u32[]{:S(2)}) collective-permute-start(bf16[16,1280]{1,0:T(8,128)(2,1)S(1)} %get-tuple-element.47), channel_id=1, source_target_pairs={{3,4},{11,12},{19,20},{27,28}} | collective-permute-start | bytes 122888 | tf_op jit(solution)/shard_map/ppermute | solution.py:415
  10.1 1.4 %collective-permute-start.8 = (bf16[16,1280]{1,0:T(8,128)(2,1)S(1)}, bf16[16,1280]{1,0:T(8,128)(2,1)S(1)}, u32[]{:S(2)}, u32[]{:S(2)}) collective-permute-start(bf16[16,1280]{1,0:T(8,128)(2,1)S(1)} %get-tuple-element.48), channel_id=1, source_target_pairs={{3,5},{11,13},{19,21},{27,29}} | collective-permute-start | bytes 122888 | tf_op jit(solution)/shard_map/ppermute | solution.py:415
  10.8 1.4 %collective-permute-start.9 = (bf16[16,1280]{1,0:T(8,128)(2,1)S(1)}, bf16[16,1280]{1,0:T(8,128)(2,1)S(1)}, u32[]{:S(2)}, u32[]{:S(2)}) collective-permute-start(bf16[16,1280]{1,0:T(8,128)(2,1)S(1)} %get-tuple-element.49), channel_id=1, source_target_pairs={{3,6},{11,14},{19,22},{27,30}} | collective-permute-start | bytes 122888 | tf_op jit(solution)/shard_map/ppermute | solution.py:415
  11.5 1.2 %collective-permute-start.10 = (bf16[16,1280]{1,0:T(8,128)(2,1)S(1)}, bf16[16,1280]{1,0:T(8,128)(2,1)S(1)}, u32[]{:S(2)}, u32[]{:S(2)}) collective-permute-start(bf16[16,1280]{1,0:T(8,128)(2,1)S(1)} %get-tuple-element.50), channel_id=1, source_target_pairs={{3,7},{11,15},{19,23},{27,31}} | collective-permute-start | bytes 122888 | tf_op jit(solution)/shard_map/ppermute | solution.py:415
  12.2 26.1 %collective-permute-start = (bf16[128,1024]{1,0:T(8,128)(2,1)S(1)}, bf16[128,1024]{1,0:T(8,128)(2,1)S(1)}, u32[]{:S(2)}, u32[]{:S(2)}) collective-permute-start(bf16[128,1024]{1,0:T(8,128)(2,1)S(1)} %get-tuple-element.39), channel_id=1, source_target_pairs={{8,0},{9,1},{10,2},{11,3},{12,4},{13,5},{14,6},{15,7},{16,8},{17,9... | collective-permute-start | bytes 786440 | tf_op jit(solution)/shard_map/ppermute | solution.py:424
  12.7 25.6 %collective-permute-start.1 = (bf16[128,1024]{1,0:T(8,128)(2,1)S(1)}, bf16[128,1024]{1,0:T(8,128)(2,1)S(1)}, u32[]{:S(2)}, u32[]{:S(2)}) collective-permute-start(bf16[128,1024]{1,0:T(8,128)(2,1)S(1)} %get-tuple-element.40), channel_id=1, source_target_pairs={{8,1},{9,0},{10,3},{11,2},{12,5},{13,4},{14,7},{15,6},{16,9},{17,8... | collective-permute-start | bytes 786440 | tf_op jit(solution)/shard_map/ppermute | solution.py:424
  17.2 21.1 %collective-permute-start.2 = (bf16[128,1024]{1,0:T(8,128)(2,1)S(1)}, bf16[128,1024]{1,0:T(8,128)(2,1)S(1)}, u32[]{:S(2)}, u32[]{:S(2)}) collective-permute-start(bf16[128,1024]{1,0:T(8,128)(2,1)S(1)} %get-tuple-element.41), channel_id=1, source_target_pairs={{8,2},{9,3},{10,0},{11,1},{12,6},{13,7},{14,4},{15,5},{16,10},{17,... | collective-permute-start | bytes 786440 | tf_op jit(solution)/shard_map/ppermute | solution.py:424
  22.9 15.4 %collective-permute-start.3 = (bf16[128,1024]{1,0:T(8,128)(2,1)S(1)}, bf16[128,1024]{1,0:T(8,128)(2,1)S(1)}, u32[]{:S(2)}, u32[]{:S(2)}) collective-permute-start(bf16[128,1024]{1,0:T(8,128)(2,1)S(1)} %get-tuple-element.42), channel_id=1, source_target_pairs={{8,3},{9,2},{10,1},{11,0},{12,7},{13,6},{14,5},{15,4},{16,11},{17,... | collective-permute-start | bytes 786440 | tf_op jit(solution)/shard_map/ppermute | solution.py:424
  38.3 2.9 %copy-start.8 = (f32[1,64]{1,0:T(1,128)S(1)}, f32[1,64]{1,0:T(1,128)}, u32[]{:S(2)}) copy-start(f32[1,64]{1,0:T(1,128)} %refs_15_.1) | copy-start | bytes 772
  41.2 30.6 %collective-permute-start.11 = (f32[128,1024]{1,0:T(8,128)S(1)}, f32[128,1024]{1,0:T(8,128)S(1)}, u32[]{:S(2)}, u32[]{:S(2)}) collective-permute-start(f32[128,1024]{1,0:T(8,128)S(1)} %get-tuple-element.54), channel_id=1, source_target_pairs={{0,4},{1,5},{2,6},{3,7},{4,0},{5,1},{6,2},{7,3},{8,12},{9,13},{10,... | collective-permute-start | bytes 1572872 | tf_op jit(solution)/shard_map/ppermute | solution.py:405
  41.3 30.5 %copy-start.3 = (f32[1,4,4352]{2,1,0:T(4,128)S(1)}, f32[1,4,4352]{2,1,0:T(4,128)}, u32[]{:S(2)}) copy-start(f32[1,4,4352]{2,1,0:T(4,128)} %param.12) | copy-start | bytes 208900
  41.3 30.5 %copy-start.7 = (f32[1,64]{1,0:T(1,128)S(1)}, f32[1,64]{1,0:T(1,128)}, u32[]{:S(2)}) copy-start(f32[1,64]{1,0:T(1,128)} %refs_14_.1) | copy-start | bytes 772
  49.1 22.7 %collective-permute-start.12 = (f32[32,1024]{1,0:T(8,128)S(1)}, f32[32,1024]{1,0:T(8,128)S(1)}, u32[]{:S(2)}, u32[]{:S(2)}) collective-permute-start(f32[32,1024]{1,0:T(8,128)S(1)} %get-tuple-element.59), channel_id=1, source_target_pairs={{0,4},{1,5},{2,6},{3,7},{4,0},{5,1},{6,2},{7,3},{8,12},{9,13},{10,... | collective-permute-start | bytes 393224 | tf_op jit(solution)/shard_map/ppermute | solution.py:405
  84.3 24.8 %collective-permute-start.13 = (bf16[128,1152]{1,0:T(8,128)(2,1)S(1)}, bf16[128,1152]{1,0:T(8,128)(2,1)S(1)}, u32[]{:S(2)}, u32[]{:S(2)}) collective-permute-start(bf16[128,1152]{1,0:T(8,128)(2,1)S(1)} %get-tuple-element.65), channel_id=1, source_target_pairs={{0,1},{1,0},{2,3},{3,2},{4,5},{5,4},{6,7},{7,6},{8,9},{9,8},{10,11... | collective-permute-start | bytes 884744 | tf_op jit(solution)/shard_map/ppermute | solution.py:405
  86.8 22.3 %collective-permute-start.14 = (bf16[128,1152]{1,0:T(8,128)(2,1)S(1)}, bf16[128,1152]{1,0:T(8,128)(2,1)S(1)}, u32[]{:S(2)}, u32[]{:S(2)}) collective-permute-start(bf16[128,1152]{1,0:T(8,128)(2,1)S(1)} %get-tuple-element.66), channel_id=1, source_target_pairs={{0,2},{1,3},{2,0},{3,1},{4,6},{5,7},{6,4},{7,5},{8,10},{9,11},{10,... | collective-permute-start | bytes 884744 | tf_op jit(solution)/shard_map/ppermute | solution.py:405
  86.8 22.3 %collective-permute-start.15 = (bf16[128,1152]{1,0:T(8,128)(2,1)S(1)}, bf16[128,1152]{1,0:T(8,128)(2,1)S(1)}, u32[]{:S(2)}, u32[]{:S(2)}) collective-permute-start(bf16[128,1152]{1,0:T(8,128)(2,1)S(1)} %get-tuple-element.67), channel_id=1, source_target_pairs={{0,3},{1,2},{2,1},{3,0},{4,7},{5,6},{6,5},{7,4},{8,11},{9,10},{10,... | collective-permute-start | bytes 884744 | tf_op jit(solution)/shard_map/ppermute | solution.py:405
  88.4 14.9 %collective-permute-start.16 = (f32[128,256]{1,0:T(8,128)S(1)}, f32[128,256]{1,0:T(8,128)S(1)}, u32[]{:S(2)}, u32[]{:S(2)}) collective-permute-start(f32[128,256]{1,0:T(8,128)S(1)} %get-tuple-element.69), channel_id=1, source_target_pairs={{0,1},{1,0},{2,3},{3,2},{4,5},{5,4},{6,7},{7,6},{8,9},{9,8},{10,11... | collective-permute-start | bytes 393224 | tf_op jit(solution)/shard_map/ppermute | solution.py:405
  90.3 14.4 %collective-permute-start.17 = (f32[128,256]{1,0:T(8,128)S(1)}, f32[128,256]{1,0:T(8,128)S(1)}, u32[]{:S(2)}, u32[]{:S(2)}) collective-permute-start(f32[128,256]{1,0:T(8,128)S(1)} %get-tuple-element.70), channel_id=1, source_target_pairs={{0,2},{1,3},{2,0},{3,1},{4,6},{5,7},{6,4},{7,5},{8,10},{9,11},{10,... | collective-permute-start | bytes 393224 | tf_op jit(solution)/shard_map/ppermute | solution.py:405
  103.3 5.9 %collective-permute-start.18 = (f32[128,256]{1,0:T(8,128)S(1)}, f32[128,256]{1,0:T(8,128)S(1)}, u32[]{:S(2)}, u32[]{:S(2)}) collective-permute-start(f32[128,256]{1,0:T(8,128)S(1)} %get-tuple-element.71), channel_id=1, source_target_pairs={{0,3},{1,2},{2,1},{3,0},{4,7},{5,6},{6,5},{7,4},{8,11},{9,10},{10,... | collective-permute-start | bytes 393224 | tf_op jit(solution)/shard_map/ppermute | solution.py:405
  (6 other events, 4.5 us)

commit v3 on v2

v3 whole, which is shorter than its diff:
```python
import functools

import jax
import jax.numpy as jnp
from jax import lax
from jax.experimental import pallas as pl
from jax.experimental.pallas import tpu as pltpu
from jax.sharding import PartitionSpec as P

BLOCK = 128
LANES = 128
HEAD = 64
PAD = 8
PARTS = 2
F32 = jnp.float32
BF16 = jnp.bfloat16
NEG = -1e30
NN = (((1,), (0,)), ((), ()))
NT = (((1,), (1,)), ((), ()))
TN = (((0,), (0,)), ((), ()))


def mm(a, b, dims=NN):
    return lax.dot_general(a, b, dims, preferred_element_type=F32)


def split(a):
    high = a.astype(BF16)
    return high, (a - high.astype(F32)).astype(BF16)


def mm3(a, b, dims=NN):
    (ah, al), (bh, bl) = a, b
    return mm(ah, bh, dims) + (mm(ah, bl, dims) + mm(al, bh, dims))


def iota(shape, axis):
    return lax.broadcasted_iota(jnp.int32, shape, axis)


def wide(a):
    high, low = a
    return jnp.concatenate([high, low], axis=1), high


def mm_wide(a, b):
    (both, high), (bh, bl) = a, b
    return mm(both, jnp.concatenate([bh, bh], axis=0)) + mm(high, bl)


def mm_over(a, b):
    (ah, al), (bh, bl) = a, b
    n = bh.shape[0]
    both = mm(ah, jnp.concatenate([bh, bl], axis=0), NT)
    return both[:, :n] + (both[:, n:] + mm(al, bh, NT))


def expand(values, head, count=LANES):
    rows = values.shape[0]
    left = iota((rows, LANES), 1) < HEAD
    tiles = []
    for h in range(head, head + count // HEAD, 2):
        first = jnp.broadcast_to(values[:, h : h + 1], (rows, LANES))
        second = jnp.broadcast_to(values[:, h + 1 : h + 2], (rows, LANES))
        tiles.append(jnp.where(left, first, second))
    return tiles[0] if len(tiles) == 1 else jnp.concatenate(tiles, axis=1)


def head_sum(tile, head):
    shape = (tile.shape[1], LANES)
    onto = (iota(shape, 1) == head + iota(shape, 0) // HEAD).astype(F32).astype(BF16)
    high, low = split(tile)
    return mm(high, onto) + mm(low, onto)


class Plan:
    def __init__(self, devices, inner, state, heads):
        self.half = devices // 2
        self.inner = inner
        self.state = state
        self.maps = 2 * state
        self.heads = heads // self.half
        self.all = inner // self.half
        self.parts = PARTS
        self.width = self.all // PARTS
        self.tile = 2 * LANES if self.width % (2 * LANES) == 0 else LANES
        self.tiles = self.width // self.tile
        self.blocks = self.half
        self.tokens = self.half * BLOCK


class Stage:
    def __init__(self, plan, part):
        self.plan = plan
        self.part = part
        self.first = part == 0
        self.last = part == plan.parts - 1
        self.head = part * plan.width // HEAD
        self.start = part * plan.width

    def steps(self):
        tile = self.plan.tile
        for i in range(self.plan.tiles):
            lane = self.start + i * tile
            yield slice(i * tile, (i + 1) * tile), slice(lane, lane + tile), lane // HEAD


def place(plan):
    rank = lax.axis_index("ctx")
    return lax.rem(rank, plan.half), lax.div(rank, plan.half)


def call(kernel, stage, out_shape, scratch=(), flops=0):
    return pl.pallas_call(
        functools.partial(kernel, stage),
        out_shape=out_shape,
        scratch_shapes=list(scratch),
        compiler_params=pltpu.CompilerParams(vmem_limit_bytes=32 * 1024 * 1024),
        cost_estimate=pl.CostEstimate(flops=flops, transcendentals=0, bytes_accessed=4 << 20),
    )


def struct(*shape, dtype=F32):
    return jax.ShapeDtypeStruct(shape, dtype)


def near(*shape, dtype=F32):
    return pltpu.VMEM(shape, dtype)


def head_rows(plan, prm, refs, own):
    prm[...] = jnp.zeros_like(prm)
    for row, values in enumerate(refs):
        prm[row : row + 1, 0 : values.shape[1]] = values
    local = pltpu.roll(prm[...], lax.rem(LANES - own * plan.heads, LANES), 1)
    return [local[row : row + 1, :] for row in range(len(refs))]


def run_copies(pairs, sems):
    copies = [pltpu.make_async_copy(source, target, sems.at[n]) for n, (source, target) in enumerate(pairs)]
    for copy in copies:
        copy.start()
    for copy in copies:
        copy.wait()


def pack_kernel(plan, f_ref, m_ref, s_ref, *refs):
    pays, edges, sems = refs[: plan.half], refs[plan.half : -1], refs[-1]
    own, _ = place(plan)
    whole, heads = plan.all, s_ref.shape[0]
    pairs = []
    for k in range(plan.half):
        start = pl.multiple_of(jnp.bitwise_xor(own, k) * whole, LANES)
        pairs.append((f_ref.at[:, pl.ds(start, whole)], pays[k].at[:, pl.ds(0, whole)]))
        pairs.append((m_ref, pays[k].at[:, pl.ds(whole, plan.maps)]))
        for row in range(0, BLOCK, heads):
            pairs.append((s_ref, pays[k].at[pl.ds(row, heads), pl.ds(whole + plan.maps, LANES)]))
        tail = pl.ds(BLOCK - 16, 16)
        pairs.append((f_ref.at[tail, pl.ds(k * whole, whole)], edges[k].at[:, pl.ds(0, whole)]))
        pairs.append((m_ref.at[tail, :], edges[k].at[:, pl.ds(whole, plan.maps)]))
    run_copies(pairs, sems)


def cut_kernel(plan, o_ref, *refs):
    own, _ = place(plan)
    pairs = []
    for k in range(plan.half):
        start = pl.multiple_of(jnp.bitwise_xor(own, k) * plan.all, LANES)
        pairs.append((o_ref.at[:, pl.ds(start, plan.all)], refs[k]))
    run_copies(pairs, refs[-1])


def forward_kernel(plan, *refs):
    half, width, maps, tile = plan.half, plan.all, plan.maps, plan.tile
    conv = width + maps
    pays, edges = refs[:half], refs[half : 2 * half]
    (cw_ref, cb_ref, dl_ref, sb_ref, x_ref, ds_ref, el_ref, xm_ref, dm_ref, st_ref, sg_ref, cum_ref,
     raw, sraw, prm) = refs[2 * half :]
    own, _ = place(plan)
    heads = dl_ref.shape[1]
    halo = edges[0][...].astype(F32)
    for k in range(1, half):
        halo = halo + edges[k][...].astype(F32)
    raw[0:PAD, :] = halo[16 - PAD :, :]
    sraw[...] = jnp.zeros_like(sraw)
    for k in range(half):
        block = jnp.bitwise_xor(own, k) * BLOCK
        raw[pl.ds(pl.multiple_of(block + PAD, 8), BLOCK), :] = pays[k][:, :conv].astype(F32)
        sraw[pl.ds(pl.multiple_of(block, 8), BLOCK), 0:heads] = pays[k][0:heads, conv:].astype(F32).T
    rates, offsets = head_rows(plan, prm, [-jnp.exp(dl_ref[...]), sb_ref[...]], own)
    shift = lax.rem(LANES - own * plan.heads, LANES)
    lower = (iota((BLOCK, BLOCK), 0) >= iota((BLOCK, BLOCK), 1)).astype(F32)
    el_ref[0:BLOCK, :] = jnp.zeros((BLOCK, width), F32)

    def body(b, carry):
        row = pl.multiple_of(b * BLOCK, BLOCK)
        rows = pl.ds(row, BLOCK)
        for c in range(0, conv, tile):
            window = raw[pl.ds(row, BLOCK + PAD), c : c + tile]
            if c < width:
                cols = pl.ds(pl.multiple_of(own * width + c, LANES), tile)
                to_x, to_d, at = x_ref, ds_ref, c
            else:
                cols = slice(plan.inner + c - width, plan.inner + c - width + tile)
                to_x, to_d, at = xm_ref, dm_ref, c - width
            weight = cw_ref[:, cols]
            v = jnp.broadcast_to(cb_ref[:, cols], (BLOCK, tile))
            for k in range(weight.shape[0]):
                v = v + weight[k : k + 1, :] * window[PAD - k : PAD - k + BLOCK, :]
            s = 1.0 / (1.0 + jnp.exp(-v))
            to_x[rows, at : at + tile] = v * s
            to_d[rows, at : at + tile] = s * (1.0 + v * (1.0 - s))
        a = pltpu.roll(sraw[rows, :], shift, 1) + offsets
        e = jnp.exp(-jnp.abs(a))
        u = 1.0 + e
        d = u - 1.0
        step = jnp.maximum(a, 0.0) + jnp.where(d == 0.0, e, jnp.log(u) * (e / jnp.where(d == 0.0, 1.0, d)))
        st_ref[rows, :] = step
        sg_ref[rows, :] = jnp.where(a >= 0.0, 1.0, e) / u
        cum = lax.dot_general(lower, step * rates, NN, precision=lax.Precision.HIGHEST, preferred_element_type=F32)
        cum_ref[rows, :] = cum
        total = cum[BLOCK - 1 :, :]
        weighted = jnp.exp(total - cum) * step
        decay = jnp.exp(total)
        bt = wide(split(xm_ref[rows, : plan.state].T))
        nxt = pl.ds(pl.multiple_of(row + BLOCK, BLOCK), BLOCK)
        for c in range(0, width, tile):
            at, head = slice(c, c + tile), c // HEAD
            wx = split(x_ref[rows, at] * expand(weighted, head, tile))
            el_ref[nxt, at] = el_ref[rows, at] * expand(decay, head, tile) + mm_wide(bt, wx)
        return carry

    lax.fori_loop(0, plan.blocks, body, 0)


def gradient_kernel(stage, *refs):
    plan, first, last = stage.plan, stage.first, stage.last
    half, width, blocks, tile, state = plan.half, plan.width, plan.blocks, plan.tile, plan.state
    grads = refs[:half]
    xm_ref, cum_ref, el_ref, x_ref, ds_ref, dm_ref, st_ref, sk_ref = refs[half : half + 8]
    refs = refs[half + 8 :]
    if not first:
        top_old, refs = refs[0], refs[1:]
    gy_ref, gl_ref, send_ref = refs[:3]
    if not last:
        top_ref = refs[3]
    prm = refs[-1]
    own, late = place(plan)
    for k in range(half):
        block = pl.multiple_of(jnp.bitwise_xor(own, k) * BLOCK, BLOCK)
        gy_ref[pl.ds(block, BLOCK), :] = grads[k][:, stage.start : stage.start + width]
    gl_ref[blocks * BLOCK :, :] = jnp.zeros((BLOCK, width), F32)

    def body(t, carry):
        row = pl.multiple_of((blocks - 1 - t) * BLOCK, BLOCK)
        rows = pl.ds(row, BLOCK)
        nxt = pl.ds(pl.multiple_of(row + BLOCK, BLOCK), BLOCK)
        cum = cum_ref[rows, :]
        grown, decay = jnp.exp(cum), jnp.exp(cum[BLOCK - 1 :, :])
        ct = wide(split(xm_ref[rows, plan.state :].T))
        for at, _, head in stage.steps():
            ge = split(gy_ref[rows, at].astype(F32) * expand(grown, head, tile))
            gl_ref[rows, at] = gl_ref[nxt, at] * expand(decay, head, tile) + mm_wide(ct, ge)
        return carry

    lax.fori_loop(0, blocks, body, 0)

    @pl.when(late == 0)
    def _():
        send_ref[0:BLOCK, :] = el_ref[blocks * BLOCK :, stage.start : stage.start + width]
        send_ref[BLOCK:, :] = jnp.zeros((16, width), F32)
        if not last:
            top_ref[...] = jnp.zeros_like(top_ref)

    @pl.when(late != 0)
    def _():
        send_ref[0:BLOCK, :] = gl_ref[0:BLOCK, :]
        (skips,) = head_rows(plan, prm, [sk_ref[...]], own)
        top = slice(0, 16)
        edge = send_ref.at[BLOCK : BLOCK + 16, :]
        cum, step, cum_t = cum_ref[top, :], st_ref[top, :], cum_ref[0:BLOCK, :].T
        shrunk, grown = jnp.exp(cum_ref[BLOCK - 1 : BLOCK, :] - cum), jnp.exp(cum)
        top_b, first_c = split(xm_ref[top, :state]), split(xm_ref[0:BLOCK, state:])
        wide_b = wide(top_b)
        scores = mm3(top_b, first_c, NT)
        causal = iota((16, BLOCK), 0) <= iota((16, BLOCK), 1)
        if first:
            d_b, dsc = jnp.zeros((16, state), F32), jnp.zeros((16, BLOCK), F32)
        else:
            d_b, dsc = top_old[:, :state], top_old[:, state:]
        zero, blank = jnp.zeros((BLOCK, LANES), BF16), jnp.zeros((16, LANES), BF16)
        left, left_top = iota((BLOCK, LANES), 1) < HEAD, iota((16, LANES), 1) < HEAD
        for i in range(width // LANES):
            at, head = slice(i * LANES, (i + 1) * LANES), stage.head + 2 * i
            among = slice(head * HEAD, head * HEAD + LANES)
            step_x, shrunk_x = expand(step, head), expand(shrunk, head)
            xs = x_ref[top, among] * step_x
            gy = gy_ref[0:BLOCK, at]
            decays, mh, ml = [], [], []
            for h in (head, head + 1):
                spread = cum_t[h : h + 1, :] - jnp.broadcast_to(cum[:, h : h + 1], (16, BLOCK))
                decay = jnp.exp(jnp.where(causal, spread, NEG))
                high, low = split(scores * decay)
                decays.append(decay)
                mh.append(high)
                ml.append(low)
            gs = jnp.concatenate([jnp.where(left, gy, zero), jnp.where(left, zero, gy)], axis=0)
            dxs = mm(jnp.concatenate(mh, axis=1), gs) + mm(jnp.concatenate(ml, axis=1), gs)
            xh, xl = split(xs)
            rows = [jnp.where(left_top, xh, blank), jnp.where(left_top, blank, xh)]
            rows += [jnp.where(left_top, xl, blank), jnp.where(left_top, blank, xl)]
            dm = mm(jnp.concatenate(rows, axis=0), gy, NT)
            dsc = dsc + (dm[0:16] + dm[32:48]) * decays[0] + (dm[16:32] + dm[48:64]) * decays[1]
            leaving = split(gl_ref[BLOCK : 2 * BLOCK, at])
            dxs = dxs + shrunk_x * mm_wide(wide_b, leaving)
            d_b = d_b + mm_over(split(xs * shrunk_x), leaving)
            top_gy = gy[0:16].astype(F32)
            edge[0:PAD, at] = ((dxs * step_x + expand(skips, head) * top_gy) * ds_ref[top, among])[0:PAD]
            edge[PAD:, at] = (top_gy * expand(grown, head))[0:PAD]
        if last:
            parts = split(dsc)
            d_b = (d_b + mm3(parts, first_c)) * dm_ref[top, :state]
            d_c = mm3(parts, top_b, TN)
            silu_c = dm_ref[top, state:]
            edge[3:6, 0:state] = d_b[0:3]
            edge[6:8, 0:state] = silu_c[0:2]
            edge[11:14, 0:state] = d_c[0:3]
            edge[14:15, 0:state] = silu_c[2:3]
        else:
            top_ref[:, :state] = d_b
            top_ref[:, state:] = dsc


def within_kernel(stage, *refs):
    plan, first = stage.plan, stage.first
    x_ref, xm_ref, st_ref, cum_ref, gy_ref = refs[:5]
    refs = refs[5:]
    if not first:
        dsc_old, refs = refs[0], refs[1:]
    yw_ref, dw_ref, dsc_ref = refs
    width, state = plan.width, plan.state
    causal = iota((BLOCK, BLOCK), 0) >= iota((BLOCK, BLOCK), 1)
    left = iota((BLOCK, LANES), 1) < HEAD

    def body(b, carry):
        rows = pl.ds(pl.multiple_of(b * BLOCK, BLOCK), BLOCK)
        cum = cum_ref[rows, :]
        cum_t = cum.T
        step = st_ref[rows, :]
        b_maps = split(xm_ref[rows, :state])
        c_maps = split(xm_ref[rows, state:])
        scores = mm3(c_maps, b_maps, NT)
        total = jnp.zeros((BLOCK, BLOCK), F32) if first else dsc_old[rows, :]
        zero = jnp.zeros((BLOCK, LANES), BF16)
        for i in range(width // LANES):
            at, head = slice(i * LANES, (i + 1) * LANES), stage.head + 2 * i
            xs = x_ref[rows, head * HEAD : head * HEAD + LANES] * expand(step, head)
            xh, xl = split(xs)
            gy = gy_ref[rows, at]
            g0, g1 = jnp.where(left, gy, zero), jnp.where(left, zero, gy)
            decays, mh, ml = [], [], []
            for h in (head, head + 1):
                spread = jnp.broadcast_to(cum[:, h : h + 1], (BLOCK, BLOCK)) - cum_t[h : h + 1, :]
                decay = jnp.exp(jnp.where(causal, spread, NEG))
                high, low = split(scores * decay)
                decays.append(decay)
                mh.append(high)
                ml.append(low)
            both = jnp.concatenate(
                [
                    jnp.concatenate([jnp.where(left, xh, zero), jnp.where(left, xl, zero)], axis=1),
                    jnp.concatenate([jnp.where(left, zero, xh), jnp.where(left, zero, xl)], axis=1),
                ],
                axis=0,
            )
            high = mm(jnp.concatenate(mh, axis=1), both)
            low = mm(jnp.concatenate(ml, axis=1), both[:, :LANES])
            yw_ref[rows, at] = high[:, :LANES] + (high[:, LANES:] + low)
            gs = jnp.concatenate([g0, g1], axis=0)
            dw_ref[rows, at] = mm(jnp.concatenate(mh, axis=0), gs, TN) + mm(jnp.concatenate(ml, axis=0), gs, TN)
            dm = mm(jnp.concatenate([gs, gs], axis=1), jnp.concatenate([xh, xl], axis=1), NT)
            total = total + dm[:BLOCK] * decays[0] + dm[BLOCK:] * decays[1]
        dsc_ref[rows, :] = total
        return carry

    lax.fori_loop(0, plan.blocks, body, 0)


def final_kernel(stage, *refs):
    plan, first, last = stage.plan, stage.first, stage.last
    half, width, blocks, state, tile, maps = plan.half, plan.width, plan.blocks, plan.state, plan.tile, plan.maps
    (both_ref, x_ref, xm_ref, ds_ref, st_ref, sg_ref, cum_ref, el_ref, gl_ref, gy_ref, yw_ref, dw_ref,
     cw_ref, dl_ref, sk_ref) = refs[:15]
    refs = refs[15:]
    got_ref, edge_ref = both_ref.at[0:BLOCK, :], both_ref.at[BLOCK : BLOCK + 16, :]
    if last:
        dsc_ref, dm_ref, refs = refs[0], refs[1], refs[2:]
    if not first:
        bc_old, ac_old, dst_old, refs = refs[0], refs[1], refs[2], refs[3:]
    outs, refs = refs[:half], refs[half:]
    if last:
        map_outs, refs = refs[:half], refs[half:]
        m_sc = refs[-1]
    else:
        bc_ref, ac_ref, dst_ref, refs = refs[0], refs[1], refs[2], refs[3:]
    prm, dz, nxt_dz, carry_ref, o_sc, lc_sc = refs[:6]
    conv = width + maps if last else width
    own, late = place(plan)
    is_late = late.astype(F32)
    rates, skips = head_rows(plan, prm, [-jnp.exp(dl_ref[...]), sk_ref[...]], own)
    upper = (iota((BLOCK, BLOCK), 0) <= iota((BLOCK, BLOCK), 1)).astype(F32)
    after_c = jnp.zeros((16, state), F32) if first else ac_old[...]
    for at, among, _ in stage.steps():
        after_c = after_c + mm_over(split(edge_ref[:, at]), split(el_ref[blocks * BLOCK :, among]))
    early = iota((PAD, LANES), 0) * 0 + late == 0
    for c in range(0, width, LANES):
        nxt_dz[:, c : c + LANES] = jnp.where(early, edge_ref[0:PAD, c : c + LANES], 0.0)
    if last:
        rest = jnp.zeros((PAD - 3, state), F32)
        nxt_dz[:, width : width + state] = jnp.where(early, jnp.concatenate([edge_ref[3:6, 0:state], rest], axis=0), 0.0)
        silu_c = jnp.concatenate([edge_ref[6:8, 0:state], edge_ref[14:15, 0:state]], axis=0)
        after_c = (after_c[PAD : PAD + 3] + edge_ref[11:14, 0:state]) * silu_c
        nxt_dz[:, width + state :] = jnp.where(early, jnp.concatenate([after_c, rest], axis=0), 0.0)
    else:
        ac_ref[...] = after_c
    lc_sc[...] = jnp.zeros_like(lc_sc)
    for b in range(1, blocks):
        lc_sc[b : b + 1, :] = lc_sc[b - 1 : b, :] + cum_ref[b * BLOCK - 1 : b * BLOCK, :]
    whole = lc_sc[blocks - 1 : blocks, :] + cum_ref[blocks * BLOCK - 1 :, :]
    ends = jnp.zeros((8, LANES), F32)
    for at, among, head in stage.steps():
        product = jnp.sum(got_ref[:, at] * el_ref[blocks * BLOCK :, among], axis=0, keepdims=True)
        ends = ends + head_sum(jnp.broadcast_to(product, (8, tile)), head)
    carry_ref[...] = ends * (1.0 - is_late)

    def body(t, carry):
        b = blocks - 1 - t
        row = pl.multiple_of(b * BLOCK, BLOCK)
        rows = pl.ds(row, BLOCK)
        nxt = pl.ds(pl.multiple_of(row + BLOCK, BLOCK), BLOCK)
        cum, step = cum_ref[rows, :], st_ref[rows, :]
        total = cum[BLOCK - 1 :, :]
        grown, shrunk = jnp.exp(cum), jnp.exp(total - cum)
        before = lc_sc[pl.ds(b, 1), :]
        from_first = jnp.exp(before) * is_late
        to_last = jnp.exp(whole - before - total) * (1.0 - is_late)
        b_maps, c_maps = split(xm_ref[rows, :state]), split(xm_ref[rows, state:])
        b_wide, c_wide = wide(b_maps), wide(c_maps)
        if first:
            d_b = d_c = jnp.zeros((BLOCK, state), F32)
        else:
            d_b, d_c = bc_old[rows, :state], bc_old[rows, state:]
        if last:
            dsc = dsc_ref[rows, :]
            d_c = d_c + mm3(split(dsc), b_maps)
            d_b = d_b + mm3(split(dsc.T), c_maps)
        sums = jnp.zeros((BLOCK, LANES), F32)
        direct = jnp.zeros((BLOCK, LANES), F32)
        for at, among, head in stage.steps():
            got = got_ref[:, at]
            entering = split(el_ref[rows, among] + got * expand(from_first, head, tile))
            leaving = split(gl_ref[nxt, at] + got * expand(to_last, head, tile))
            x = x_ref[rows, among]
            step_x, shrunk_x, grown_x = expand(step, head, tile), expand(shrunk, head, tile), expand(grown, head, tile)
            xs = x * step_x
            gy = gy_ref[rows, at].astype(F32)
            y = yw_ref[rows, at] + grown_x * mm_wide(c_wide, entering)
            dxs = dw_ref[rows, at] + shrunk_x * mm_wide(b_wide, leaving)
            d_c = d_c + mm_over(split(gy * grown_x), entering)
            d_b = d_b + mm_over(split(xs * shrunk_x), leaving)
            sums = sums + head_sum(gy * y - xs * dxs, head)
            direct = direct + head_sum(dxs * x, head)
            dz[0:BLOCK, at] = (dxs * step_x + expand(skips, head, tile) * gy) * ds_ref[rows, among]
        d_log = lax.dot_general(upper, sums, NN, precision=lax.Precision.HIGHEST, preferred_element_type=F32)
        d_log = d_log + carry_ref[0:1, :]
        carry_ref[...] = jnp.broadcast_to(d_log[0:1, :], (8, LANES))
        d_step = (d_log * rates + direct) * sg_ref[rows, :]
        lane = iota((BLOCK, LANES), 1)
        d_step = jnp.where((lane >= stage.head) & (lane < stage.head + width // HEAD), d_step, 0.0)
        if not first:
            d_step = d_step + dst_old[rows, :]
        if last:
            o_sc[rows, width:] = d_step.astype(BF16)
            dz[0:BLOCK, width : width + state] = d_b * dm_ref[rows, :state]
            dz[0:BLOCK, width + state :] = d_c * dm_ref[rows, state:]
        else:
            dst_ref[rows, :] = d_step
            bc_ref[rows, :state] = d_b
            bc_ref[rows, state:] = d_c
        dz[BLOCK:, :] = nxt_dz[...]
        for c in range(0, conv, LANES):
            window = dz[:, c : c + LANES]
            if c < width:
                cols = pl.ds(pl.multiple_of(own * plan.all + stage.start + c, LANES), LANES)
            else:
                cols = slice(plan.inner + c - width, plan.inner + c - width + LANES)
            weight = cw_ref[:, cols]
            grad = weight[0:1, :] * window[0:BLOCK, :]
            for k in range(1, weight.shape[0]):
                grad = grad + weight[k : k + 1, :] * window[k : k + BLOCK, :]
            if c < width:
                o_sc[rows, c : c + LANES] = grad.astype(BF16)
            else:
                m_sc[rows, c - width : c - width + LANES] = grad
        nxt_dz[...] = dz[0:PAD, :]
        return carry

    lax.fori_loop(0, blocks, body, 0)
    for k in range(half):
        rows = pl.ds(pl.multiple_of(jnp.bitwise_xor(own, k) * BLOCK, BLOCK), BLOCK)
        outs[k][...] = o_sc[rows, :]
        if last:
            map_outs[k][...] = m_sc[rows, :]


def owner_kernel(plan, *refs):
    half, width, parts = plan.half, plan.width, plan.parts
    outs, maps = refs[: half * parts], refs[half * parts : half * (parts + 1)]
    f_ref, m_ref, s_ref = refs[half * (parts + 1) :]
    own, _ = place(plan)
    total = maps[0][...]
    steps = jnp.zeros((BLOCK, LANES), F32)
    for k in range(half):
        part = jnp.bitwise_xor(own, k)
        for p in range(parts):
            start = pl.multiple_of(part * plan.all + p * width, LANES)
            f_ref[:, pl.ds(start, width)] = outs[p * half + k][:, :width]
        steps = steps + pltpu.roll(outs[(parts - 1) * half + k][:, width:].astype(F32), part * plan.heads, 1)
        if k:
            total = total + maps[k][...]
    m_ref[...] = total.astype(BF16)
    s_ref[...] = steps.T[: s_ref.shape[0]].astype(BF16)


def per_device(sections, devices, features, state_maps, step_raw, conv_weight, conv_bias, decay_log, step_bias, skip_gain, output_grads):
    state = state_maps.shape[2] // 2
    heads = decay_log.shape[1]
    plan = Plan(devices, features.shape[2], state, heads)
    half, width, tokens, parts, maps = plan.half, plan.width, plan.tokens, plan.parts, plan.maps
    weight = conv_weight[0]
    stages = [Stage(plan, p) for p in range(parts)]

    def partner(array, k):
        return lax.ppermute(array, "ctx", [(i, i ^ k) for i in range(devices)])

    def shifted(array, k):
        route = [
            (((p + 1) % sections) * devices + i, p * devices + (i ^ k))
            for p in range(sections)
            for i in range(devices)
        ]
        return lax.ppermute(array, ("pipe", "ctx"), route)

    conv = plan.all + maps
    away = pl.BlockSpec(memory_space=pl.ANY)
    packed = pl.pallas_call(
        functools.partial(pack_kernel, plan),
        out_shape=[struct(BLOCK, conv + LANES, dtype=BF16)] * half + [struct(16, conv, dtype=BF16)] * half,
        in_specs=[away] * 3,
        scratch_shapes=[pltpu.SemaphoreType.DMA((half * (4 + BLOCK // heads),))],
    )(features[0], state_maps[0], step_raw[0].T)
    cuts = pl.pallas_call(
        functools.partial(cut_kernel, plan),
        out_shape=[struct(BLOCK, plan.all, dtype=BF16)] * half,
        in_specs=[away],
        scratch_shapes=[pltpu.SemaphoreType.DMA((half,))],
    )(output_grads[0])
    pays = [packed[0]] + [partner(packed[k], k) for k in range(1, half)]
    edges = [lax.ppermute(e, "ctx", [(half - 1, half + k)]) for k, e in enumerate(packed[half:])]
    grads = [shifted(cuts[k], k) for k in range(half)]
    big = 2 * tokens * state * width
    done = []
    small = pltpu.VMEM((8, LANES), F32)
    x_conv, dsilu, states, x_maps, d_maps, steps, sigmoids, cums = call(
        forward_kernel,
        plan,
        [near(tokens, plan.all), near(tokens, plan.all), near(tokens + BLOCK, plan.all), near(tokens, maps),
         near(tokens, maps)] + [near(tokens, LANES)] * 3,
        [pltpu.VMEM((tokens + PAD, conv), F32), pltpu.VMEM((tokens, LANES), F32), small],
        flops=6 * big * parts,
    )(*pays, *edges, weight, conv_bias, decay_log, step_bias)
    for stage in stages:
        first = stage.first
        args = [*grads, x_maps, cums, states, x_conv, dsilu, d_maps, steps, skip_gain]
        outs = [near(tokens, width, dtype=BF16), near(tokens + BLOCK, width), struct(BLOCK + 16, width)]
        if not first:
            args += [top]
        if not stage.last:
            outs += [near(16, state + BLOCK)]
        gy, back, send, *rest = call(gradient_kernel, stage, outs, [small], flops=3 * big)(*args)
        if rest:
            top = rest[0]
        got = partner(send, half)
        outs = [near(tokens, width), near(tokens, width), near(tokens, BLOCK)]
        args = [x_conv, x_maps, steps, cums, gy] + ([] if first else [scores])
        y_within, d_within, scores = call(within_kernel, stage, outs, flops=30 * big)(*args)
        done.append((got, x_conv, x_maps, dsilu, steps, sigmoids, cums, states, back, gy, y_within, d_within))
    feature_parts = []
    for stage, arrays in zip(stages, done):
        first, last = stage.first, stage.last
        conv = width + maps if last else width
        out = width + LANES if last else width
        args = [*arrays, weight, decay_log, skip_gain]
        outs = [struct(BLOCK, out, dtype=BF16)] * half
        scratch = [small, pltpu.VMEM((BLOCK + PAD, conv), F32), pltpu.VMEM((PAD, conv), F32), small,
                   pltpu.VMEM((tokens, out), BF16), pltpu.VMEM((max(8, plan.blocks), LANES), F32)]
        if last:
            args += [scores, d_maps]
            outs += [struct(BLOCK, maps)] * half
            scratch += [pltpu.VMEM((tokens, maps), F32)]
        else:
            outs += [near(tokens, maps), near(16, state), near(tokens, LANES)]
        if not first:
            args += carried
        result = call(final_kernel, stage, outs, scratch, flops=12 * big)(*args)
        feature_parts += [result[0]] + [partner(result[k], k) for k in range(1, half)]
        carried = result[half:]
    map_parts = [carried[0]] + [partner(carried[k], k) for k in range(1, half)]
    feature_grads, map_grads, step_grads = call(
        owner_kernel,
        plan,
        [struct(BLOCK, plan.inner, dtype=BF16), struct(BLOCK, maps, dtype=BF16), struct(heads, BLOCK, dtype=BF16)],
    )(*feature_parts, *map_parts)
    return (feature_grads[None], map_grads[None], step_grads.T[None])


def solution(mesh):
    return jax.shard_map(
        functools.partial(per_device, mesh.shape["pipe"], mesh.shape["ctx"]),
        mesh=mesh,
        in_specs=(
            P("pipe", "ctx", None),
            P("pipe", "ctx", None),
            P("pipe", "ctx", None),
            P("pipe", None, None),
            P("pipe", None),
            P("pipe", None),
            P("pipe", None),
            P("pipe", None),
            P("pipe", "ctx", None),
        ),
        out_specs=(P("pipe", "ctx", None), P("pipe", "ctx", None), P("pipe", "ctx", None)),
        check_vma=False,
    )
```

time: 111 us -> 96.1 us (0.87)
  waiting for transfers between devices: 40.7 us -> 26.6 us
  Pallas kernels: 29.5 us -> 35.9 us
  local copies, waits for them, and re-layouts: 6.92 us -> 1 us
    ppermute x11 -> x14, waiting for transfers between devices: 40.7 us -> 23.8 us  [partner(): return lax.ppermute(array, 'ctx', [(i, i ^ k) for i in range(devices)])]
    ppermute x4, starting transfers between devices: 16.1 us -> 9.55 us  [shifted(): return lax.ppermute(array, ('pipe', 'ctx'), route)]
    pallas_call x5 -> x9, Pallas kernels: 28.4 us -> 34.8 us  [the longest x2 11.8 us: per_device(): result = call(final_kernel, stage, outs, scratch, flops=12 * big)(*args)]
    unnamed x22 -> x12, local copies, waits for them, and re-layouts: 6.92 us -> 1 us
    ppermute x11 -> x14, starting transfers between devices: 13.6 us -> 19.3 us  [partner(): return lax.ppermute(array, 'ctx', [(i, i ^ k) for i in range(devices)])]
    ppermute x4, waiting for transfers between devices: 0.01 us -> 2.74 us  [shifted(): return lax.ppermute(array, ('pipe', 'ctx'), route)]
  transfers between devices with their start and end apart: 19 -> 22, of which waited for: 5 -> 6; matrix products, arithmetic and copies ran while one was open for 0% -> 0% of each run, Pallas kernels for 12% -> 31%
where the time goes in v3:
time: 96.1 us; the launch traced here: 95.9 us
  Pallas kernels  35.9 us (37%)
  starting transfers between devices  31.5 us (33%)
  waiting for transfers between devices  26.6 us (28%)
  local copies, waits for them, and re-layouts  1 us (1%)
    ppermute x14, waiting for transfers between devices, partner(): return lax.ppermute(array, 'ctx', [(i, i ^ k) for i in range(devices)])  23.8 us
    ppermute x14, starting transfers between devices, partner(): return lax.ppermute(array, 'ctx', [(i, i ^ k) for i in range(devices)])  19.3 us
    pallas_call x2, Pallas kernels, per_device(): result = call(final_kernel, stage, outs, scratch, flops=12 * big)(*args)  11.8 us
    ppermute x4, starting transfers between devices, shifted(): return lax.ppermute(array, ('pipe', 'ctx'), route)  9.55 us
    pallas_call x2, Pallas kernels, per_device(): call(within_kernel, stage, outs, flops=30 * big)(*args)  8.65 us
    pallas_call x1, Pallas kernels, per_device(): call(forward_kernel, plan, [near(tokens, plan.all), near(tokens, plan.all...  5.02 us
    pallas_call x2, Pallas kernels, per_device(): call(gradient_kernel, stage, outs, [small], flops=3 * big)(*args)  4.1 us
    pallas_call x1, Pallas kernels, per_device(): pl.pallas_call(functools.partial(pack_kernel, plan), out_shape=[struct(BL...  2.98 us
  transfers between devices with their start and end apart: 22, of which 6 were waited for; matrix products, arithmetic and copies ran while one was open for 0% of the time, Pallas kernels for 31%

profile of v3, /device:TPU:0, one launch (start us, length us, event | category | flops | bytes accessed | tf_op | source)
XLA Modules:
  0.0 95.9 jit_solution(13943693557916640715)
XLA Ops:
  0.7 3.0 %shard_map.113 = (bf16[128,1408]{1,0:T(8,128)(2,1)}, bf16[128,1408]{1,0:T(8,128)(2,1)}, bf16[128,1408]{1,0:T(8,128)(2,1)}, bf16[128,1408]{1,0:T(8,128)(2,1)}, bf...) custom-call(bf16[128,4096]{1,0:T(8,128)(2,1)} %bitcast.15, ...), custom_call_target="tpu_custom_call" | custom-call | tf_op jit(solution)/shard_map/pallas_call | solution.py:556
  3.7 3.0 %collective-permute-start.4 = (bf16[128,1408]{1,0:T(8,128)(2,1)}, bf16[128,1408]{1,0:T(8,128)(2,1)S(1)}, u32[]{:S(2)}, u32[]{:S(2)}) collective-permute-start(bf16[128,1408]{1,0:T(8,128)(2,1)} %get-tuple-element.59), channel_id=1, source_target_pairs={{0,1},{1,0},{2,3},{3,2},{4,5},{5,4},{6,7},{7,6},{8,9},{9,8},{10,11... | collective-permute-start | bytes 1081352 | tf_op jit(solution)/shard_map/ppermute | solution.py:544
  6.7 1.6 %collective-permute-start.5 = (bf16[128,1408]{1,0:T(8,128)(2,1)}, bf16[128,1408]{1,0:T(8,128)(2,1)S(1)}, u32[]{:S(2)}, u32[]{:S(2)}) collective-permute-start(bf16[128,1408]{1,0:T(8,128)(2,1)} %get-tuple-element.60), channel_id=1, source_target_pairs={{0,2},{1,3},{2,0},{3,1},{4,6},{5,7},{6,4},{7,5},{8,10},{9,11},{10,... | collective-permute-start | bytes 1081352 | tf_op jit(solution)/shard_map/ppermute | solution.py:544
  11.0 2.2 %shard_map.112 = (bf16[128,1024]{1,0:T(8,128)(2,1)}, bf16[128,1024]{1,0:T(8,128)(2,1)}, bf16[128,1024]{1,0:T(8,128)(2,1)}, bf16[128,1024]{1,0:T(8,128)(2,1)}) custom-call(bf16[128,4096]{1,0:T(8,128)(2,1)} %bitcast.16), custom_call_target="tpu_custom_call" | custom-call | tf_op jit(solution)/shard_map/pallas_call | solution.py:562
  13.7 2.5 %collective-permute-start.1 = (bf16[128,1024]{1,0:T(8,128)(2,1)}, bf16[128,1024]{1,0:T(8,128)(2,1)S(1)}, u32[]{:S(2)}, u32[]{:S(2)}) collective-permute-start(bf16[128,1024]{1,0:T(8,128)(2,1)} %get-tuple-element.55), channel_id=1, source_target_pairs={{8,1},{9,0},{10,3},{11,2},{12,5},{13,4},{14,7},{15,6},{16,9},{17,8... | collective-permute-start | bytes 786440 | tf_op jit(solution)/shard_map/ppermute | solution.py:552
  16.2 6.5 %collective-permute-start.2 = (bf16[128,1024]{1,0:T(8,128)(2,1)}, bf16[128,1024]{1,0:T(8,128)(2,1)S(1)}, u32[]{:S(2)}, u32[]{:S(2)}) collective-permute-start(bf16[128,1024]{1,0:T(8,128)(2,1)} %get-tuple-element.56), channel_id=1, source_target_pairs={{8,2},{9,3},{10,0},{11,1},{12,6},{13,7},{14,4},{15,5},{16,10},{17,... | collective-permute-start | bytes 786440 | tf_op jit(solution)/shard_map/ppermute | solution.py:552
  22.8 4.5 %collective-permute-done.6.refs_3_ = bf16[128,1408]{1,0:T(8,128)(2,1)S(1)} collective-permute-done((bf16[128,1408]{1,0:T(8,128)(2,1)}, bf16[128,1408]{1,0:T(8,128)(2,1)S(1)}, u32[]{:S(2)}, u32[]{:S(2)}) %collective-permute-start.6) | collective-permute-done | bytes 360480 | tf_op jit(solution)/shard_map/ppermute | solution.py:544
  28.2 5.0 %shard_map.114 = (f32[512,1024]{1,0:T(8,128)S(1)}, f32[512,1024]{1,0:T(8,128)S(1)}, f32[640,1024]{1,0:T(8,128)S(1)}, f32[512,256]{1,0:T(8,128)S(1)}, f32[512,256...) custom-call(bf16[128,1408]{1,0:T(8,128)(2,1)S(1)} %copy-done.3, ...), custom_call_target="tpu_custom_call" | custom-call | flops 805306368 | bytes 4194304 | tf_op jit(solution)/shard_map/pallas_call | solution.py:574
  33.3 2.7 %collective-permute-done.3.refs_3_ = bf16[128,1024]{1,0:T(8,128)(2,1)S(1)} collective-permute-done((bf16[128,1024]{1,0:T(8,128)(2,1)}, bf16[128,1024]{1,0:T(8,128)(2,1)S(1)}, u32[]{:S(2)}, u32[]{:S(2)}) %collective-permute-start.3) | collective-permute-done | bytes 262176 | tf_op jit(solution)/shard_map/ppermute | solution.py:552
  36.0 2.1 %shard_map.115 = (bf16[512,512]{1,0:T(8,128)(2,1)S(1)}, f32[640,512]{1,0:T(8,128)S(1)}, f32[144,512]{1,0:T(8,128)S(1)}, f32[16,256]{1,0:T(8,128)S(1)}) custom-call(bf16[128,1024]{1,0:T(8,128)(2,1)S(1)} %collective-permute-done.refs_0_, bf16[128,1024]{1,0:T(8,128)(2,1)S(1)} %collective-permute-done.1.refs_1_, ...), custom_call_target="tpu_custom_call" | custom-call | flops 201326592 | bytes 4194304 | tf_op jit(solution)/shard_map/pallas_call | solution.py:590
  38.1 4.0 %collective-permute-start.11 = (f32[144,512]{1,0:T(8,128)S(1)}, f32[144,512]{1,0:T(8,128)S(1)}, u32[]{:S(2)}, u32[]{:S(2)}) collective-permute-start(f32[144,512]{1,0:T(8,128)S(1)} %get-tuple-element.73), channel_id=1, source_target_pairs={{0,4},{1,5},{2,6},{3,7},{4,0},{5,1},{6,2},{7,3},{8,12},{9,13},{10,... | collective-permute-start | bytes 884744 | tf_op jit(solution)/shard_map/ppermute | solution.py:544
  42.1 2.1 %shard_map.118 = (bf16[512,512]{1,0:T(8,128)(2,1)S(1)}, f32[640,512]{1,0:T(8,128)S(1)}, f32[144,512]{1,0:T(8,128)S(1)}) custom-call(bf16[128,1024]{1,0:T(8,128)(2,1)S(1)} %collective-permute-done.refs_0_, bf16[128,1024]{1,0:T(8,128)(2,1)S(1)} %collective-permute-done.1.refs_1_, bf16[128,1024]{1,0:T(8,128)(2,1)S(1)} %collective-permute-done.2.refs_2_, ...), custom_call_target="tpu_custom_call" | custom-call | flops 201326592 | bytes 4194304 | tf_op jit(solution)/shard_map/pallas_call | solution.py:590
  45.1 4.3 %shard_map.116 = (f32[512,512]{1,0:T(8,128)S(1)}, f32[512,512]{1,0:T(8,128)S(1)}, f32[512,128]{1,0:T(8,128)S(1)}) custom-call(f32[512,1024]{1,0:T(8,128)S(1)} %get-tuple-element.69.refs_7_.refs_0_.refs_1_, f32[512,256]{1,0:T(8,128)S(1)} %get-tuple-element.66.refs_4_.refs_1_.refs_2_, f32[512,128]{1,0:T(8,128)S(1)} %get-tuple-element.72.refs_10_.refs_2_.refs_4_, ...), custom_call_target="tpu_custom_call" | custom-call | flops 2013265920 | bytes 4194304 | tf_op jit(solution)/shard_map/pallas_call | solution.py:596
  49.4 4.3 %shard_map.119 = (f32[512,512]{1,0:T(8,128)S(1)}, f32[512,512]{1,0:T(8,128)S(1)}, f32[512,128]{1,0:T(8,128)S(1)}) custom-call(f32[512,1024]{1,0:T(8,128)S(1)} %get-tuple-element.69.refs_7_.refs_0_.refs_1_, f32[512,256]{1,0:T(8,128)S(1)} %get-tuple-element.66.refs_4_.refs_1_.refs_2_, f32[512,128]{1,0:T(8,128)S(1)} %get-tuple-element.72.refs_10_.refs_2_.refs_4_, ...), custom_call_target="tpu_custom_call" | custom-call | flops 2013265920 | bytes 4194304 | tf_op jit(solution)/shard_map/pallas_call | solution.py:596
  53.8 8.3 %collective-permute-done.11.refs_0_ = f32[144,512]{1,0:T(8,128)S(1)} collective-permute-done((f32[144,512]{1,0:T(8,128)S(1)}, f32[144,512]{1,0:T(8,128)S(1)}, u32[]{:S(2)}, u32[]{:S(2)}) %collective-permute-start.11) | collective-permute-done | bytes 294944 | tf_op jit(solution)/shard_map/ppermute | solution.py:544
  62.1 5.7 %shard_map.117 = (bf16[128,512]{1,0:T(8,128)(2,1)S(1)}, bf16[128,512]{1,0:T(8,128)(2,1)S(1)}, bf16[128,512]{1,0:T(8,128)(2,1)S(1)}, bf16[128,512]{1,0:T(8,128)(2...) custom-call(f32[144,512]{1,0:T(8,128)S(1)} %collective-permute-done.11.refs_0_, ...), custom_call_target="tpu_custom_call" | custom-call | flops 805306368 | bytes 4194304 | tf_op jit(solution)/shard_map/pallas_call | solution.py:615
  67.8 1.6 %collective-permute-start.12 = (bf16[128,512]{1,0:T(8,128)(2,1)S(1)}, bf16[128,512]{1,0:T(8,128)(2,1)S(1)}, u32[]{:S(2)}, u32[]{:S(2)}) collective-permute-start(bf16[128,512]{1,0:T(8,128)(2,1)S(1)} %get-tuple-element.80), channel_id=1, source_target_pairs={{0,1},{1,0},{2,3},{3,2},{4,5},{5,4},{6,7},{7,6},{8,9},{9,8},{10,11... | collective-permute-start | bytes 393224 | tf_op jit(solution)/shard_map/ppermute | solution.py:544
  69.4 2.0 %collective-permute-start.14 = (bf16[128,512]{1,0:T(8,128)(2,1)S(1)}, bf16[128,512]{1,0:T(8,128)(2,1)S(1)}, u32[]{:S(2)}, u32[]{:S(2)}) collective-permute-start(bf16[128,512]{1,0:T(8,128)(2,1)S(1)} %get-tuple-element.82), channel_id=1, source_target_pairs={{0,3},{1,2},{2,1},{3,0},{4,7},{5,6},{6,5},{7,4},{8,11},{9,10},{10,... | collective-permute-start | bytes 393224 | tf_op jit(solution)/shard_map/ppermute | solution.py:544
  71.4 6.1 %shard_map.120 = (bf16[128,640]{1,0:T(8,128)(2,1)S(1)}, bf16[128,640]{1,0:T(8,128)(2,1)S(1)}, bf16[128,640]{1,0:T(8,128)(2,1)S(1)}, bf16[128,640]{1,0:T(8,128)(2...) custom-call(f32[144,512]{1,0:T(8,128)S(1)} %collective-permute-done., ...), custom_call_target="tpu_custom_call" | custom-call | flops 805306368 | bytes 4194304 | tf_op jit(solution)/shard_map/pallas_call | solution.py:615
  77.5 1.6 %collective-permute-start.19 = (f32[128,256]{1,0:T(8,128)S(1)}, f32[128,256]{1,0:T(8,128)S(1)}, u32[]{:S(2)}, u32[]{:S(2)}) collective-permute-start(f32[128,256]{1,0:T(8,128)S(1)} %get-tuple-element.99), channel_id=1, source_target_pairs={{0,1},{1,0},{2,3},{3,2},{4,5},{5,4},{6,7},{7,6},{8,9},{9,8},{10,11... | collective-permute-start | bytes 393224 | tf_op jit(solution)/shard_map/ppermute | solution.py:544
  80.1 2.5 %collective-permute-start.18 = (bf16[128,640]{1,0:T(8,128)(2,1)S(1)}, bf16[128,640]{1,0:T(8,128)(2,1)S(1)}, u32[]{:S(2)}, u32[]{:S(2)}) collective-permute-start(bf16[128,640]{1,0:T(8,128)(2,1)S(1)} %get-tuple-element.97), channel_id=1, source_target_pairs={{0,3},{1,2},{2,1},{3,0},{4,7},{5,6},{6,5},{7,4},{8,11},{9,10},{10,... | collective-permute-start | bytes 491528 | tf_op jit(solution)/shard_map/ppermute | solution.py:544
  82.6 1.3 %collective-permute-done.19.refs_9_ = f32[128,256]{1,0:T(8,128)S(1)} collective-permute-done((f32[128,256]{1,0:T(8,128)S(1)}, f32[128,256]{1,0:T(8,128)S(1)}, u32[]{:S(2)}, u32[]{:S(2)}) %collective-permute-start.19) | collective-permute-done | bytes 131104 | tf_op jit(solution)/shard_map/ppermute | solution.py:544
  84.9 8.1 %collective-permute-done.20.refs_10_ = f32[128,256]{1,0:T(8,128)S(1)} collective-permute-done((f32[128,256]{1,0:T(8,128)S(1)}, f32[128,256]{1,0:T(8,128)S(1)}, u32[]{:S(2)}, u32[]{:S(2)}) %collective-permute-start.20) | collective-permute-done | bytes 131104 | tf_op jit(solution)/shard_map/ppermute | solution.py:544
  93.0 1.6 %collective-permute-done.21.refs_11_ = f32[128,256]{1,0:T(8,128)S(1)} collective-permute-done((f32[128,256]{1,0:T(8,128)S(1)}, f32[128,256]{1,0:T(8,128)S(1)}, u32[]{:S(2)}, u32[]{:S(2)}) %collective-permute-start.21) | collective-permute-done | bytes 131104 | tf_op jit(solution)/shard_map/ppermute | solution.py:544
  (42 shorter events, 8.4 us)
Async XLA Ops:
  0.6 26.6 %copy-start = (f32[1,4,4352]{2,1,0:T(4,128)S(1)}, f32[1,4,4352]{2,1,0:T(4,128)}, u32[]{:S(2)}) copy-start(f32[1,4,4352]{2,1,0:T(4,128)} %param.12) | copy-start | bytes 208900
  3.7 32.4 %copy-start.1 = (f32[1,64]{1,0:T(1,128)S(1)}, f32[1,64]{1,0:T(1,128)}, u32[]{:S(2)}) copy-start(f32[1,64]{1,0:T(1,128)} %refs_14_.3) | copy-start | bytes 772
  3.7 12.5 %collective-permute-start.4 = (bf16[128,1408]{1,0:T(8,128)(2,1)}, bf16[128,1408]{1,0:T(8,128)(2,1)S(1)}, u32[]{:S(2)}, u32[]{:S(2)}) collective-permute-start(bf16[128,1408]{1,0:T(8,128)(2,1)} %get-tuple-element.59), channel_id=1, source_target_pairs={{0,1},{1,0},{2,3},{3,2},{4,5},{5,4},{6,7},{7,6},{8,9},{9,8},{10,11... | collective-permute-start | bytes 1081352 | tf_op jit(solution)/shard_map/ppermute | solution.py:544
  6.7 16.1 %collective-permute-start.5 = (bf16[128,1408]{1,0:T(8,128)(2,1)}, bf16[128,1408]{1,0:T(8,128)(2,1)S(1)}, u32[]{:S(2)}, u32[]{:S(2)}) collective-permute-start(bf16[128,1408]{1,0:T(8,128)(2,1)} %get-tuple-element.60), channel_id=1, source_target_pairs={{0,2},{1,3},{2,0},{3,1},{4,6},{5,7},{6,4},{7,5},{8,10},{9,11},{10,... | collective-permute-start | bytes 1081352 | tf_op jit(solution)/shard_map/ppermute | solution.py:544
  8.3 18.9 %collective-permute-start.6 = (bf16[128,1408]{1,0:T(8,128)(2,1)}, bf16[128,1408]{1,0:T(8,128)(2,1)S(1)}, u32[]{:S(2)}, u32[]{:S(2)}) collective-permute-start(bf16[128,1408]{1,0:T(8,128)(2,1)} %get-tuple-element.61), channel_id=1, source_target_pairs={{0,3},{1,2},{2,1},{3,0},{4,7},{5,6},{6,5},{7,4},{8,11},{9,10},{10,... | collective-permute-start | bytes 1081352 | tf_op jit(solution)/shard_map/ppermute | solution.py:544
  8.3 1.3 %collective-permute-start.7 = (bf16[16,1280]{1,0:T(8,128)(2,1)}, bf16[16,1280]{1,0:T(8,128)(2,1)S(1)}, u32[]{:S(2)}, u32[]{:S(2)}) collective-permute-start(bf16[16,1280]{1,0:T(8,128)(2,1)} %get-tuple-element.62), channel_id=1, source_target_pairs={{3,4},{11,12},{19,20},{27,28}} | collective-permute-start | bytes 122888 | tf_op jit(solution)/shard_map/ppermute | solution.py:569
  9.0 1.4 %collective-permute-start.8 = (bf16[16,1280]{1,0:T(8,128)(2,1)}, bf16[16,1280]{1,0:T(8,128)(2,1)S(1)}, u32[]{:S(2)}, u32[]{:S(2)}) collective-permute-start(bf16[16,1280]{1,0:T(8,128)(2,1)} %get-tuple-element.63), channel_id=1, source_target_pairs={{3,5},{11,13},{19,21},{27,29}} | collective-permute-start | bytes 122888 | tf_op jit(solution)/shard_map/ppermute | solution.py:569
  9.6 3.6 %collective-permute-start.9 = (bf16[16,1280]{1,0:T(8,128)(2,1)}, bf16[16,1280]{1,0:T(8,128)(2,1)S(1)}, u32[]{:S(2)}, u32[]{:S(2)}) collective-permute-start(bf16[16,1280]{1,0:T(8,128)(2,1)} %get-tuple-element.64), channel_id=1, source_target_pairs={{3,6},{11,14},{19,22},{27,30}} | collective-permute-start | bytes 122888 | tf_op jit(solution)/shard_map/ppermute | solution.py:569
  10.3 3.4 %collective-permute-start.10 = (bf16[16,1280]{1,0:T(8,128)(2,1)}, bf16[16,1280]{1,0:T(8,128)(2,1)S(1)}, u32[]{:S(2)}, u32[]{:S(2)}) collective-permute-start(bf16[16,1280]{1,0:T(8,128)(2,1)} %get-tuple-element.65), channel_id=1, source_target_pairs={{3,7},{11,15},{19,23},{27,31}} | collective-permute-start | bytes 122888 | tf_op jit(solution)/shard_map/ppermute | solution.py:569
  13.2 20.1 %collective-permute-start = (bf16[128,1024]{1,0:T(8,128)(2,1)}, bf16[128,1024]{1,0:T(8,128)(2,1)S(1)}, u32[]{:S(2)}, u32[]{:S(2)}) collective-permute-start(bf16[128,1024]{1,0:T(8,128)(2,1)} %get-tuple-element.54), channel_id=1, source_target_pairs={{8,0},{9,1},{10,2},{11,3},{12,4},{13,5},{14,6},{15,7},{16,8},{17,9... | collective-permute-start | bytes 786440 | tf_op jit(solution)/shard_map/ppermute | solution.py:552
  13.7 19.5 %collective-permute-start.1 = (bf16[128,1024]{1,0:T(8,128)(2,1)}, bf16[128,1024]{1,0:T(8,128)(2,1)S(1)}, u32[]{:S(2)}, u32[]{:S(2)}) collective-permute-start(bf16[128,1024]{1,0:T(8,128)(2,1)} %get-tuple-element.55), channel_id=1, source_target_pairs={{8,1},{9,0},{10,3},{11,2},{12,5},{13,4},{14,7},{15,6},{16,9},{17,8... | collective-permute-start | bytes 786440 | tf_op jit(solution)/shard_map/ppermute | solution.py:552
  16.2 17.1 %collective-permute-start.2 = (bf16[128,1024]{1,0:T(8,128)(2,1)}, bf16[128,1024]{1,0:T(8,128)(2,1)S(1)}, u32[]{:S(2)}, u32[]{:S(2)}) collective-permute-start(bf16[128,1024]{1,0:T(8,128)(2,1)} %get-tuple-element.56), channel_id=1, source_target_pairs={{8,2},{9,3},{10,0},{11,1},{12,6},{13,7},{14,4},{15,5},{16,10},{17,... | collective-permute-start | bytes 786440 | tf_op jit(solution)/shard_map/ppermute | solution.py:552
  22.8 13.3 %collective-permute-start.3 = (bf16[128,1024]{1,0:T(8,128)(2,1)}, bf16[128,1024]{1,0:T(8,128)(2,1)S(1)}, u32[]{:S(2)}, u32[]{:S(2)}) collective-permute-start(bf16[128,1024]{1,0:T(8,128)(2,1)} %get-tuple-element.57), channel_id=1, source_target_pairs={{8,3},{9,2},{10,1},{11,0},{12,7},{13,6},{14,5},{15,4},{16,11},{17,... | collective-permute-start | bytes 786440 | tf_op jit(solution)/shard_map/ppermute | solution.py:552
  38.1 24.0 %collective-permute-start.11 = (f32[144,512]{1,0:T(8,128)S(1)}, f32[144,512]{1,0:T(8,128)S(1)}, u32[]{:S(2)}, u32[]{:S(2)}) collective-permute-start(f32[144,512]{1,0:T(8,128)S(1)} %get-tuple-element.73), channel_id=1, source_target_pairs={{0,4},{1,5},{2,6},{3,7},{4,0},{5,1},{6,2},{7,3},{8,12},{9,13},{10,... | collective-permute-start | bytes 884744 | tf_op jit(solution)/shard_map/ppermute | solution.py:544
  44.2 27.2 %collective-permute-start.15 = (f32[144,512]{1,0:T(8,128)S(1)}, f32[144,512]{1,0:T(8,128)S(1)}, u32[]{:S(2)}, u32[]{:S(2)}) collective-permute-start(f32[144,512]{1,0:T(8,128)S(1)} %get-tuple-element.84), channel_id=1, source_target_pairs={{0,4},{1,5},{2,6},{3,7},{4,0},{5,1},{6,2},{7,3},{8,12},{9,13},{10,... | collective-permute-start | bytes 884744 | tf_op jit(solution)/shard_map/ppermute | solution.py:544
  67.8 11.7 %collective-permute-start.12 = (bf16[128,512]{1,0:T(8,128)(2,1)S(1)}, bf16[128,512]{1,0:T(8,128)(2,1)S(1)}, u32[]{:S(2)}, u32[]{:S(2)}) collective-permute-start(bf16[128,512]{1,0:T(8,128)(2,1)S(1)} %get-tuple-element.80), channel_id=1, source_target_pairs={{0,1},{1,0},{2,3},{3,2},{4,5},{5,4},{6,7},{7,6},{8,9},{9,8},{10,11... | collective-permute-start | bytes 393224 | tf_op jit(solution)/shard_map/ppermute | solution.py:544
  69.4 10.7 %collective-permute-start.13 = (bf16[128,512]{1,0:T(8,128)(2,1)S(1)}, bf16[128,512]{1,0:T(8,128)(2,1)S(1)}, u32[]{:S(2)}, u32[]{:S(2)}) collective-permute-start(bf16[128,512]{1,0:T(8,128)(2,1)S(1)} %get-tuple-element.81), channel_id=1, source_target_pairs={{0,2},{1,3},{2,0},{3,1},{4,6},{5,7},{6,4},{7,5},{8,10},{9,11},{10,... | collective-permute-start | bytes 393224 | tf_op jit(solution)/shard_map/ppermute | solution.py:544
  69.4 13.1 %collective-permute-start.14 = (bf16[128,512]{1,0:T(8,128)(2,1)S(1)}, bf16[128,512]{1,0:T(8,128)(2,1)S(1)}, u32[]{:S(2)}, u32[]{:S(2)}) collective-permute-start(bf16[128,512]{1,0:T(8,128)(2,1)S(1)} %get-tuple-element.82), channel_id=1, source_target_pairs={{0,3},{1,2},{2,1},{3,0},{4,7},{5,6},{6,5},{7,4},{8,11},{9,10},{10,... | collective-permute-start | bytes 393224 | tf_op jit(solution)/shard_map/ppermute | solution.py:544
  77.5 6.4 %collective-permute-start.19 = (f32[128,256]{1,0:T(8,128)S(1)}, f32[128,256]{1,0:T(8,128)S(1)}, u32[]{:S(2)}, u32[]{:S(2)}) collective-permute-start(f32[128,256]{1,0:T(8,128)S(1)} %get-tuple-element.99), channel_id=1, source_target_pairs={{0,1},{1,0},{2,3},{3,2},{4,5},{5,4},{6,7},{7,6},{8,9},{9,8},{10,11... | collective-permute-start | bytes 393224 | tf_op jit(solution)/shard_map/ppermute | solution.py:544
  79.1 15.6 %collective-permute-start.16 = (bf16[128,640]{1,0:T(8,128)(2,1)S(1)}, bf16[128,640]{1,0:T(8,128)(2,1)S(1)}, u32[]{:S(2)}, u32[]{:S(2)}) collective-permute-start(bf16[128,640]{1,0:T(8,128)(2,1)S(1)} %get-tuple-element.95), channel_id=1, source_target_pairs={{0,1},{1,0},{2,3},{3,2},{4,5},{5,4},{6,7},{7,6},{8,9},{9,8},{10,11... | collective-permute-start | bytes 491528 | tf_op jit(solution)/shard_map/ppermute | solution.py:544
  79.6 15.1 %collective-permute-start.17 = (bf16[128,640]{1,0:T(8,128)(2,1)S(1)}, bf16[128,640]{1,0:T(8,128)(2,1)S(1)}, u32[]{:S(2)}, u32[]{:S(2)}) collective-permute-start(bf16[128,640]{1,0:T(8,128)(2,1)S(1)} %get-tuple-element.96), channel_id=1, source_target_pairs={{0,2},{1,3},{2,0},{3,1},{4,6},{5,7},{6,4},{7,5},{8,10},{9,11},{10,... | collective-permute-start | bytes 491528 | tf_op jit(solution)/shard_map/ppermute | solution.py:544
  80.1 14.6 %collective-permute-start.18 = (bf16[128,640]{1,0:T(8,128)(2,1)S(1)}, bf16[128,640]{1,0:T(8,128)(2,1)S(1)}, u32[]{:S(2)}, u32[]{:S(2)}) collective-permute-start(bf16[128,640]{1,0:T(8,128)(2,1)S(1)} %get-tuple-element.97), channel_id=1, source_target_pairs={{0,3},{1,2},{2,1},{3,0},{4,7},{5,6},{6,5},{7,4},{8,11},{9,10},{10,... | collective-permute-start | bytes 491528 | tf_op jit(solution)/shard_map/ppermute | solution.py:544
  82.6 10.5 %collective-permute-start.20 = (f32[128,256]{1,0:T(8,128)S(1)}, f32[128,256]{1,0:T(8,128)S(1)}, u32[]{:S(2)}, u32[]{:S(2)}) collective-permute-start(f32[128,256]{1,0:T(8,128)S(1)} %get-tuple-element.100), channel_id=1, source_target_pairs={{0,2},{1,3},{2,0},{3,1},{4,6},{5,7},{6,4},{7,5},{8,10},{9,11},{10,... | collective-permute-start | bytes 393224 | tf_op jit(solution)/shard_map/ppermute | solution.py:544
  83.9 10.8 %collective-permute-start.21 = (f32[128,256]{1,0:T(8,128)S(1)}, f32[128,256]{1,0:T(8,128)S(1)}, u32[]{:S(2)}, u32[]{:S(2)}) collective-permute-start(f32[128,256]{1,0:T(8,128)S(1)} %get-tuple-element.101), channel_id=1, source_target_pairs={{0,3},{1,2},{2,1},{3,0},{4,7},{5,6},{6,5},{7,4},{8,11},{9,10},{10,... | collective-permute-start | bytes 393224 | tf_op jit(solution)/shard_map/ppermute | solution.py:544
  (4 other events, 80.7 us)

commit v4 on v3

--- a/solution.py
+++ b/solution.py
@@ -66,11 +66,15 @@
     return tiles[0] if len(tiles) == 1 else jnp.concatenate(tiles, axis=1)
 
 
-def head_sum(tile, head):
-    shape = (tile.shape[1], LANES)
-    onto = (iota(shape, 1) == head + iota(shape, 0) // HEAD).astype(F32).astype(BF16)
-    high, low = split(tile)
-    return mm(high, onto) + mm(low, onto)
+def onto_heads(head, count):
+    shape = (count, LANES)
+    return (iota(shape, 1) == head + iota(shape, 0) // HEAD).astype(F32).astype(BF16)
+
+
+def head_sums(values, onto):
+    rows = values[0].shape[0]
+    sums = mm(jnp.concatenate([part for value in values for part in split(value)], axis=0), onto)
+    return [sums[2 * n * rows : (2 * n + 1) * rows] + sums[(2 * n + 1) * rows : (2 * n + 2) * rows] for n in range(len(values))]
 
 
 class Plan:
@@ -110,13 +114,14 @@
     return lax.rem(rank, plan.half), lax.div(rank, plan.half)
 
 
-def call(kernel, stage, out_shape, scratch=(), flops=0):
+def call(kernel, stage, out_shape, scratch=(), work=1.0, **more):
     return pl.pallas_call(
         functools.partial(kernel, stage),
         out_shape=out_shape,
         scratch_shapes=list(scratch),
         compiler_params=pltpu.CompilerParams(vmem_limit_bytes=32 * 1024 * 1024),
-        cost_estimate=pl.CostEstimate(flops=flops, transcendentals=0, bytes_accessed=4 << 20),
+        cost_estimate=pl.CostEstimate(flops=int(work * 1.15e9), transcendentals=0, bytes_accessed=1 << 20),
+        **more,
     )
 
 
@@ -236,19 +241,21 @@
 def gradient_kernel(stage, *refs):
     plan, first, last = stage.plan, stage.first, stage.last
     half, width, blocks, tile, state = plan.half, plan.width, plan.blocks, plan.tile, plan.state
-    grads = refs[:half]
-    xm_ref, cum_ref, el_ref, x_ref, ds_ref, dm_ref, st_ref, sk_ref = refs[half : half + 8]
-    refs = refs[half + 8 :]
-    if not first:
-        top_old, refs = refs[0], refs[1:]
-    gy_ref, gl_ref, send_ref = refs[:3]
+    if first:
+        grads, refs = refs[:half], refs[half:]
+    else:
+        gy_ref, top_old, after, refs = refs[0], refs[1], refs[2], refs[3:]
+    xm_ref, cum_ref, el_ref, x_ref, ds_ref, dm_ref, st_ref, sk_ref, gl_ref, send_ref = refs[:10]
     if not last:
-        top_ref = refs[3]
+        top_ref = refs[10]
+    if first:
+        gy_ref = refs[11]
     prm = refs[-1]
     own, late = place(plan)
-    for k in range(half):
-        block = pl.multiple_of(jnp.bitwise_xor(own, k) * BLOCK, BLOCK)
-        gy_ref[pl.ds(block, BLOCK), :] = grads[k][:, stage.start : stage.start + width]
+    if first:
+        for k in range(half):
+            block = pl.multiple_of(jnp.bitwise_xor(own, k) * BLOCK, BLOCK)
+            gy_ref[pl.ds(block, BLOCK), :] = grads[k][...]
     gl_ref[blocks * BLOCK :, :] = jnp.zeros((BLOCK, width), F32)
 
     def body(t, carry):
@@ -258,8 +265,8 @@
         cum = cum_ref[rows, :]
         grown, decay = jnp.exp(cum), jnp.exp(cum[BLOCK - 1 :, :])
         ct = wide(split(xm_ref[rows, plan.state :].T))
-        for at, _, head in stage.steps():
-            ge = split(gy_ref[rows, at].astype(F32) * expand(grown, head, tile))
+        for at, among, head in stage.steps():
+            ge = split(gy_ref[rows, among].astype(F32) * expand(grown, head, tile))
             gl_ref[rows, at] = gl_ref[nxt, at] * expand(decay, head, tile) + mm_wide(ct, ge)
         return carry
 
@@ -295,7 +302,7 @@
             among = slice(head * HEAD, head * HEAD + LANES)
             step_x, shrunk_x = expand(step, head), expand(shrunk, head)
             xs = x_ref[top, among] * step_x
-            gy = gy_ref[0:BLOCK, at]
+            gy = gy_ref[0:BLOCK, among]
             decays, mh, ml = [], [], []
             for h in (head, head + 1):
                 spread = cum_t[h : h + 1, :] - jnp.broadcast_to(cum[:, h : h + 1], (16, BLOCK))
@@ -356,7 +363,7 @@
             at, head = slice(i * LANES, (i + 1) * LANES), stage.head + 2 * i
             xs = x_ref[rows, head * HEAD : head * HEAD + LANES] * expand(step, head)
             xh, xl = split(xs)
-            gy = gy_ref[rows, at]
+            gy = gy_ref[rows, head * HEAD : head * HEAD + LANES]
             g0, g1 = jnp.where(left, gy, zero), jnp.where(left, zero, gy)
             decays, mh, ml = [], [], []
             for h in (head, head + 1):
@@ -398,17 +405,14 @@
     if not first:
         bc_old, ac_old, dst_old, refs = refs[0], refs[1], refs[2], refs[3:]
     outs, refs = refs[:half], refs[half:]
-    if last:
-        map_outs, refs = refs[:half], refs[half:]
-        m_sc = refs[-1]
-    else:
+    if not last:
         bc_ref, ac_ref, dst_ref, refs = refs[0], refs[1], refs[2], refs[3:]
     prm, dz, nxt_dz, carry_ref, o_sc, lc_sc = refs[:6]
     conv = width + maps if last else width
     own, late = place(plan)
     is_late = late.astype(F32)
     rates, skips = head_rows(plan, prm, [-jnp.exp(dl_ref[...]), sk_ref[...]], own)
-    upper = (iota((BLOCK, BLOCK), 0) <= iota((BLOCK, BLOCK), 1)).astype(F32)
+    upper = (iota((BLOCK, BLOCK), 0) <= iota((BLOCK, BLOCK), 1)).astype(F32).astype(BF16)
     after_c = jnp.zeros((16, state), F32) if first else ac_old[...]
     for at, among, _ in stage.steps():
         after_c = after_c + mm_over(split(edge_ref[:, at]), split(el_ref[blocks * BLOCK :, among]))
@@ -428,9 +432,10 @@
         lc_sc[b : b + 1, :] = lc_sc[b - 1 : b, :] + cum_ref[b * BLOCK - 1 : b * BLOCK, :]
     whole = lc_sc[blocks - 1 : blocks, :] + cum_ref[blocks * BLOCK - 1 :, :]
     ends = jnp.zeros((8, LANES), F32)
+    ontos = {head: onto_heads(head, tile) for _, _, head in stage.steps()}
     for at, among, head in stage.steps():
         product = jnp.sum(got_ref[:, at] * el_ref[blocks * BLOCK :, among], axis=0, keepdims=True)
-        ends = ends + head_sum(jnp.broadcast_to(product, (8, tile)), head)
+        ends = ends + head_sums([jnp.broadcast_to(product, (16, tile))], ontos[head])[0][0:8]
     carry_ref[...] = ends * (1.0 - is_late)
 
     def body(t, carry):
@@ -463,16 +468,16 @@
             x = x_ref[rows, among]
             step_x, shrunk_x, grown_x = expand(step, head, tile), expand(shrunk, head, tile), expand(grown, head, tile)
             xs = x * step_x
-            gy = gy_ref[rows, at].astype(F32)
+            gy = gy_ref[rows, among].astype(F32)
             y = yw_ref[rows, at] + grown_x * mm_wide(c_wide, entering)
             dxs = dw_ref[rows, at] + shrunk_x * mm_wide(b_wide, leaving)
             d_c = d_c + mm_over(split(gy * grown_x), entering)
             d_b = d_b + mm_over(split(xs * shrunk_x), leaving)
-            sums = sums + head_sum(gy * y - xs * dxs, head)
-            direct = direct + head_sum(dxs * x, head)
+            both = head_sums([gy * y - xs * dxs, dxs * x], ontos[head])
+            sums, direct = sums + both[0], direct + both[1]
             dz[0:BLOCK, at] = (dxs * step_x + expand(skips, head, tile) * gy) * ds_ref[rows, among]
-        d_log = lax.dot_general(upper, sums, NN, precision=lax.Precision.HIGHEST, preferred_element_type=F32)
-        d_log = d_log + carry_ref[0:1, :]
+        sums_high, sums_low = split(sums)
+        d_log = mm(upper, sums_high) + mm(upper, sums_low) + carry_ref[0:1, :]
         carry_ref[...] = jnp.broadcast_to(d_log[0:1, :], (8, LANES))
         d_step = (d_log * rates + direct) * sg_ref[rows, :]
         lane = iota((BLOCK, LANES), 1)
@@ -480,7 +485,7 @@
         if not first:
             d_step = d_step + dst_old[rows, :]
         if last:
-            o_sc[rows, width:] = d_step.astype(BF16)
+            o_sc[rows, width : width + LANES] = d_step.astype(BF16)
             dz[0:BLOCK, width : width + state] = d_b * dm_ref[rows, :state]
             dz[0:BLOCK, width + state :] = d_c * dm_ref[rows, state:]
         else:
@@ -501,7 +506,9 @@
             if c < width:
                 o_sc[rows, c : c + LANES] = grad.astype(BF16)
             else:
-                m_sc[rows, c - width : c - width + LANES] = grad
+                high, low = split(grad)
+                o_sc[rows, LANES + c : 2 * LANES + c] = high
+                o_sc[rows, LANES + maps + c : 2 * LANES + maps + c] = low
         nxt_dz[...] = dz[0:PAD, :]
         return carry
 
@@ -509,27 +516,36 @@
     for k in range(half):
         rows = pl.ds(pl.multiple_of(jnp.bitwise_xor(own, k) * BLOCK, BLOCK), BLOCK)
         outs[k][...] = o_sc[rows, :]
-        if last:
-            map_outs[k][...] = m_sc[rows, :]
-
-
-def owner_kernel(plan, *refs):
-    half, width, parts = plan.half, plan.width, plan.parts
-    outs, maps = refs[: half * parts], refs[half * parts : half * (parts + 1)]
-    f_ref, m_ref, s_ref = refs[half * (parts + 1) :]
+
+
+def owner_kernel(stage, *refs):
+    plan, last, maps = stage.plan, stage.last, stage.plan.maps
+    half, width = plan.half, plan.width
+    outs, refs = refs[:half], refs[half:]
+    if stage.part:
+        refs = refs[1:]
+    f_ref = refs[0]
     own, _ = place(plan)
-    total = maps[0][...]
-    steps = jnp.zeros((BLOCK, LANES), F32)
+    pairs = []
     for k in range(half):
-        part = jnp.bitwise_xor(own, k)
-        for p in range(parts):
-            start = pl.multiple_of(part * plan.all + p * width, LANES)
-            f_ref[:, pl.ds(start, width)] = outs[p * half + k][:, :width]
-        steps = steps + pltpu.roll(outs[(parts - 1) * half + k][:, width:].astype(F32), part * plan.heads, 1)
-        if k:
-            total = total + maps[k][...]
-    m_ref[...] = total.astype(BF16)
-    s_ref[...] = steps.T[: s_ref.shape[0]].astype(BF16)
+        start = pl.multiple_of(jnp.bitwise_xor(own, k) * plan.all + stage.start, LANES)
+        pairs.append((outs[k].at[:, pl.ds(0, width)], f_ref.at[:, pl.ds(start, width)]))
+    copies = [pltpu.make_async_copy(source, target, refs[-1].at[n]) for n, (source, target) in enumerate(pairs)]
+    for copy in copies:
+        copy.start()
+    if last:
+        m_ref, s_ref = refs[1:3]
+        total = jnp.zeros((BLOCK, maps), F32)
+        steps = jnp.zeros((BLOCK, LANES), F32)
+        for k in range(half):
+            part, end = jnp.bitwise_xor(own, k), outs[k]
+            steps = steps + pltpu.roll(end[:, width : width + LANES].astype(F32), part * plan.heads, 1)
+            high, low = end[:, width + LANES : width + LANES + maps], end[:, width + LANES + maps :]
+            total = total + (high.astype(F32) + low.astype(F32))
+        m_ref[...] = total.astype(BF16)
+        s_ref[...] = steps.T[: s_ref.shape[0]].astype(BF16)
+    for copy in copies:
+        copy.wait()
 
 
 def per_device(sections, devices, features, state_maps, step_raw, conv_weight, conv_bias, decay_log, step_bias, skip_gain, output_grads):
@@ -553,22 +569,30 @@
 
     conv = plan.all + maps
     away = pl.BlockSpec(memory_space=pl.ANY)
-    packed = pl.pallas_call(
-        functools.partial(pack_kernel, plan),
-        out_shape=[struct(BLOCK, conv + LANES, dtype=BF16)] * half + [struct(16, conv, dtype=BF16)] * half,
-        in_specs=[away] * 3,
-        scratch_shapes=[pltpu.SemaphoreType.DMA((half * (4 + BLOCK // heads),))],
-    )(features[0], state_maps[0], step_raw[0].T)
-    cuts = pl.pallas_call(
-        functools.partial(cut_kernel, plan),
-        out_shape=[struct(BLOCK, plan.all, dtype=BF16)] * half,
-        in_specs=[away],
-        scratch_shapes=[pltpu.SemaphoreType.DMA((half,))],
-    )(output_grads[0])
+    far = pl.BlockSpec(memory_space=pltpu.HBM)
+
+    def hold(array):
+        return pltpu.with_memory_space_constraint(array, pltpu.HBM)
+
+    packed = call(
+        pack_kernel,
+        plan,
+        [struct(BLOCK, conv + LANES, dtype=BF16)] * half + [struct(16, conv, dtype=BF16)] * half,
+        [pltpu.SemaphoreType.DMA((half * (4 + BLOCK // heads),))],
+        work=3.0,
+        in_specs=[far] * 3,
+    )(hold(features[0]), hold(state_maps[0]), hold(step_raw[0].T))
+    cuts = call(
+        cut_kernel,
+        plan,
+        [struct(BLOCK, plan.all, dtype=BF16)] * half,
+        [pltpu.SemaphoreType.DMA((half,))],
+        work=2.2,
+        in_specs=[far],
+    )(hold(output_grads[0]))
     pays = [packed[0]] + [partner(packed[k], k) for k in range(1, half)]
     edges = [lax.ppermute(e, "ctx", [(half - 1, half + k)]) for k, e in enumerate(packed[half:])]
     grads = [shifted(cuts[k], k) for k in range(half)]
-    big = 2 * tokens * state * width
     done = []
     small = pltpu.VMEM((8, LANES), F32)
     x_conv, dsilu, states, x_maps, d_maps, steps, sigmoids, cums = call(
@@ -577,50 +601,63 @@
         [near(tokens, plan.all), near(tokens, plan.all), near(tokens + BLOCK, plan.all), near(tokens, maps),
          near(tokens, maps)] + [near(tokens, LANES)] * 3,
         [pltpu.VMEM((tokens + PAD, conv), F32), pltpu.VMEM((tokens, LANES), F32), small],
-        flops=6 * big * parts,
+        work=5.0,
     )(*pays, *edges, weight, conv_bias, decay_log, step_bias)
     for stage in stages:
         first = stage.first
-        args = [*grads, x_maps, cums, states, x_conv, dsilu, d_maps, steps, skip_gain]
-        outs = [near(tokens, width, dtype=BF16), near(tokens + BLOCK, width), struct(BLOCK + 16, width)]
-        if not first:
-            args += [top]
+        args = [] if first else [gy, top, scores]
+        args += [*(grads if first else ()), x_maps, cums, states, x_conv, dsilu, d_maps, steps, skip_gain]
+        outs = [near(tokens + BLOCK, width), struct(BLOCK + 16, width)]
         if not stage.last:
             outs += [near(16, state + BLOCK)]
-        gy, back, send, *rest = call(gradient_kernel, stage, outs, [small], flops=3 * big)(*args)
-        if rest:
-            top = rest[0]
+        if first:
+            outs += [near(tokens, plan.all, dtype=BF16)]
+        back, send, *rest = call(gradient_kernel, stage, outs, [small], work=2.1)(*args)
+        if first:
+            top, gy = rest
+            within = []
+            for other in stages:
+                outs = [near(tokens, width), near(tokens, width), near(tokens, BLOCK)]
+                args = [x_conv, x_maps, steps, cums, gy] + ([] if other.first else [scores])
+                y_within, d_within, scores = call(within_kernel, other, outs, work=2.0)(*args)
+                within.append((y_within, d_within))
         got = partner(send, half)
-        outs = [near(tokens, width), near(tokens, width), near(tokens, BLOCK)]
-        args = [x_conv, x_maps, steps, cums, gy] + ([] if first else [scores])
-        y_within, d_within, scores = call(within_kernel, stage, outs, flops=30 * big)(*args)
-        done.append((got, x_conv, x_maps, dsilu, steps, sigmoids, cums, states, back, gy, y_within, d_within))
+        done.append((got, x_conv, x_maps, dsilu, steps, sigmoids, cums, states, back, gy, *within[stage.part]))
     feature_parts = []
     for stage, arrays in zip(stages, done):
         first, last = stage.first, stage.last
         conv = width + maps if last else width
-        out = width + LANES if last else width
+        out = width + LANES + 2 * maps if last else width
         args = [*arrays, weight, decay_log, skip_gain]
         outs = [struct(BLOCK, out, dtype=BF16)] * half
         scratch = [small, pltpu.VMEM((BLOCK + PAD, conv), F32), pltpu.VMEM((PAD, conv), F32), small,
                    pltpu.VMEM((tokens, out), BF16), pltpu.VMEM((max(8, plan.blocks), LANES), F32)]
         if last:
             args += [scores, d_maps]
-            outs += [struct(BLOCK, maps)] * half
-            scratch += [pltpu.VMEM((tokens, maps), F32)]
         else:
             outs += [near(tokens, maps), near(16, state), near(tokens, LANES)]
         if not first:
             args += carried
-        result = call(final_kernel, stage, outs, scratch, flops=12 * big)(*args)
+        result = call(final_kernel, stage, outs, scratch, work=5.8)(*args)
         feature_parts += [result[0]] + [partner(result[k], k) for k in range(1, half)]
         carried = result[half:]
-    map_parts = [carried[0]] + [partner(carried[k], k) for k in range(1, half)]
-    feature_grads, map_grads, step_grads = call(
-        owner_kernel,
-        plan,
-        [struct(BLOCK, plan.inner, dtype=BF16), struct(BLOCK, maps, dtype=BF16), struct(heads, BLOCK, dtype=BF16)],
-    )(*feature_parts, *map_parts)
+    inside = pl.BlockSpec(memory_space=pltpu.VMEM)
+    for stage in stages:
+        more = [feature_grads] if stage.part else []
+        outs = [struct(BLOCK, plan.inner, dtype=BF16)]
+        if stage.last:
+            outs += [struct(BLOCK, maps, dtype=BF16), struct(heads, BLOCK, dtype=BF16)]
+        feature_grads, *others = call(
+            owner_kernel,
+            stage,
+            outs,
+            [pltpu.SemaphoreType.DMA((half,))],
+            work=2.0,
+            in_specs=[inside] * half + [away] * len(more),
+            out_specs=[away] + [inside] * (len(outs) - 1),
+            input_output_aliases={half: 0} if more else {},
+        )(*feature_parts[stage.part * half : (stage.part + 1) * half], *more)
+    map_grads, step_grads = others
     return (feature_grads[None], map_grads[None], step_grads.T[None])
 
 

time: 96.1 us -> 91.4 us (0.951)
  starting transfers between devices: 31.5 us -> 27.7 us
  waiting for transfers between devices: 26.6 us -> 27.9 us
  Pallas kernels: 35.9 us -> 34.7 us
  local copies, waits for them, and re-layouts: 1 us -> 0.03 us
    ppermute x14 -> x11, starting transfers between devices: 19.3 us -> 15.6 us  [partner(): return lax.ppermute(array, 'ctx', [(i, i ^ k) for i in range(devices)])]
    pallas_call x9 -> x10, Pallas kernels: 30.9 us -> 29.7 us  [the longest x2 11.6 us: per_device(): result = call(final_kernel, stage, outs, scratch, work=5.8)(*args)]
    ppermute x4, waiting for transfers between devices: 2.74 us -> 3.85 us  [shifted(): return lax.ppermute(array, ('pipe', 'ctx'), route)]
    unnamed x12 -> x10, local copies, waits for them, and re-layouts: 1 us -> 0.03 us
    ppermute x14 -> x11, waiting for transfers between devices: 23.8 us -> 24 us  [partner(): return lax.ppermute(array, 'ctx', [(i, i ^ k) for i in range(devices)])]
  transfers between devices with their start and end apart: 22 -> 19, of which waited for: 6 -> 7; matrix products, arithmetic and copies ran while one was open for 0% -> 0% of each run, Pallas kernels for 31% -> 32%
where the time goes in v4:
time: 91.4 us; the launch traced here: 91.1 us
  Pallas kernels  34.7 us (38%)
  waiting for transfers between devices  27.9 us (31%)
  starting transfers between devices  27.7 us (30%)
    ppermute x11, waiting for transfers between devices, partner(): return lax.ppermute(array, 'ctx', [(i, i ^ k) for i in range(devices)])  24 us
    ppermute x11, starting transfers between devices, partner(): return lax.ppermute(array, 'ctx', [(i, i ^ k) for i in range(devices)])  15.6 us
    pallas_call x2, Pallas kernels, per_device(): result = call(final_kernel, stage, outs, scratch, work=5.8)(*args)  11.6 us
    ppermute x4, starting transfers between devices, shifted(): return lax.ppermute(array, ('pipe', 'ctx'), route)  9.43 us
    pallas_call x2, Pallas kernels, per_device(): call(within_kernel, other, outs, work=2.0)(*args)  8.69 us
    pallas_call x1, Pallas kernels, per_device(): call(forward_kernel, plan, [near(tokens, plan.all), near(tokens, plan.all...  5.02 us
    pallas_call x2, Pallas kernels, per_device(): call(gradient_kernel, stage, outs, [small], work=2.1)(*args)  4.12 us
    ppermute x4, waiting for transfers between devices, shifted(): return lax.ppermute(array, ('pipe', 'ctx'), route)  3.85 us
  transfers between devices with their start and end apart: 19, of which 7 were waited for; matrix products, arithmetic and copies ran while one was open for 0% of the time, Pallas kernels for 32%

profile of v4, /device:TPU:0, one launch (start us, length us, event | category | flops | bytes accessed | tf_op | source)
XLA Modules:
  0.0 91.1 jit_solution(11924389614361834987)
XLA Ops:
  0.6 1.7 %shard_map.113 = (bf16[128,1408]{1,0:T(8,128)(2,1)S(1)}, bf16[128,1408]{1,0:T(8,128)(2,1)S(1)}, bf16[128,1408]{1,0:T(8,128)(2,1)S(1)}, bf16[128,1408]{1,0:T(8,12...) custom-call(bf16[128,4096]{1,0:T(8,128)(2,1)} %bitcast.15, ...), custom_call_target="tpu_custom_call" | custom-call | flops 3449999872 | bytes 1048576 | tf_op jit(solution)/shard_map/pallas_call | solution.py:577
  2.3 3.0 %collective-permute-start.4 = (bf16[128,1408]{1,0:T(8,128)(2,1)S(1)}, bf16[128,1408]{1,0:T(8,128)(2,1)S(1)}, u32[]{:S(2)}, u32[]{:S(2)}) collective-permute-start(bf16[128,1408]{1,0:T(8,128)(2,1)S(1)} %get-tuple-element.54), channel_id=1, source_target_pairs={{0,1},{1,0},{2,3},{3,2},{4,5},{5,4},{6,7},{7,6},{8,9},{9,8},{10,11... | collective-permute-start | bytes 1081352 | tf_op jit(solution)/shard_map/ppermute | solution.py:560
  5.4 1.6 %collective-permute-start.5 = (bf16[128,1408]{1,0:T(8,128)(2,1)S(1)}, bf16[128,1408]{1,0:T(8,128)(2,1)S(1)}, u32[]{:S(2)}, u32[]{:S(2)}) collective-permute-start(bf16[128,1408]{1,0:T(8,128)(2,1)S(1)} %get-tuple-element.55), channel_id=1, source_target_pairs={{0,2},{1,3},{2,0},{3,1},{4,6},{5,7},{6,4},{7,5},{8,10},{9,11},{10,... | collective-permute-start | bytes 1081352 | tf_op jit(solution)/shard_map/ppermute | solution.py:560
  11.5 2.5 %collective-permute-start.1 = (bf16[128,1024]{1,0:T(8,128)(2,1)S(1)}, bf16[128,1024]{1,0:T(8,128)(2,1)S(1)}, u32[]{:S(2)}, u32[]{:S(2)}) collective-permute-start(bf16[128,1024]{1,0:T(8,128)(2,1)S(1)} %get-tuple-element.50), channel_id=1, source_target_pairs={{8,1},{9,0},{10,3},{11,2},{12,5},{13,4},{14,7},{15,6},{16,9},{17,8... | collective-permute-start | bytes 786440 | tf_op jit(solution)/shard_map/ppermute | solution.py:568
  14.0 6.4 %collective-permute-start.2 = (bf16[128,1024]{1,0:T(8,128)(2,1)S(1)}, bf16[128,1024]{1,0:T(8,128)(2,1)S(1)}, u32[]{:S(2)}, u32[]{:S(2)}) collective-permute-start(bf16[128,1024]{1,0:T(8,128)(2,1)S(1)} %get-tuple-element.51), channel_id=1, source_target_pairs={{8,2},{9,3},{10,0},{11,1},{12,6},{13,7},{14,4},{15,5},{16,10},{17,... | collective-permute-start | bytes 786440 | tf_op jit(solution)/shard_map/ppermute | solution.py:568
  20.4 6.0 %collective-permute-done.6.refs_3_ = bf16[128,1408]{1,0:T(8,128)(2,1)S(1)} collective-permute-done((bf16[128,1408]{1,0:T(8,128)(2,1)S(1)}, bf16[128,1408]{1,0:T(8,128)(2,1)S(1)}, u32[]{:S(2)}, u32[]{:S(2)}) %collective-permute-start.6) | collective-permute-done | bytes 360480 | tf_op jit(solution)/shard_map/ppermute | solution.py:560
  26.5 5.0 %shard_map.114 = (f32[512,1024]{1,0:T(8,128)S(1)}, f32[512,1024]{1,0:T(8,128)S(1)}, f32[640,1024]{1,0:T(8,128)S(1)}, f32[512,256]{1,0:T(8,128)S(1)}, f32[512,256...) custom-call(bf16[128,1408]{1,0:T(8,128)(2,1)S(1)} %get-tuple-element.53.refs_0_, ...), custom_call_target="tpu_custom_call" | custom-call | flops 5750000128 | bytes 1048576 | tf_op jit(solution)/shard_map/pallas_call | solution.py:598
  31.5 3.8 %collective-permute-done.3.refs_3_ = bf16[128,1024]{1,0:T(8,128)(2,1)S(1)} collective-permute-done((bf16[128,1024]{1,0:T(8,128)(2,1)S(1)}, bf16[128,1024]{1,0:T(8,128)(2,1)S(1)}, u32[]{:S(2)}, u32[]{:S(2)}) %collective-permute-start.3) | collective-permute-done | bytes 262176 | tf_op jit(solution)/shard_map/ppermute | solution.py:568
  35.4 2.1 %shard_map.115 = (f32[640,512]{1,0:T(8,128)S(1)}, f32[144,512]{1,0:T(8,128)S(1)}, f32[16,256]{1,0:T(8,128)S(1)}, bf16[512,1024]{1,0:T(8,128)(2,1)S(1)}) custom-call(bf16[128,1024]{1,0:T(8,128)(2,1)S(1)} %collective-permute-done.refs_0_, bf16[128,1024]{1,0:T(8,128)(2,1)S(1)} %collective-permute-done.1.refs_1_, ...), custom_call_target="tpu_custom_call" | custom-call | flops 2415000064 | bytes 1048576 | tf_op jit(solution)/shard_map/pallas_call | solution.py:615
  37.5 1.9 %collective-permute-start.12 = (f32[144,512]{1,0:T(8,128)S(1)}, f32[144,512]{1,0:T(8,128)S(1)}, u32[]{:S(2)}, u32[]{:S(2)}) collective-permute-start(f32[144,512]{1,0:T(8,128)S(1)} %get-tuple-element.77), channel_id=1, source_target_pairs={{0,4},{1,5},{2,6},{3,7},{4,0},{5,1},{6,2},{7,3},{8,12},{9,13},{10,... | collective-permute-start | bytes 884744 | tf_op jit(solution)/shard_map/ppermute | solution.py:560
  39.4 4.3 %shard_map.116 = (f32[512,512]{1,0:T(8,128)S(1)}, f32[512,512]{1,0:T(8,128)S(1)}, f32[512,128]{1,0:T(8,128)S(1)}) custom-call(f32[512,1024]{1,0:T(8,128)S(1)} %get-tuple-element.64.refs_7_.refs_0_.refs_6_.refs_1_, f32[512,256]{1,0:T(8,128)S(1)} %get-tuple-element.61.refs_4_.refs_1_.refs_3_.refs_2_, ...), custom_call_target="tpu_custom_call" | custom-call | flops 2300000000 | bytes 1048576 | tf_op jit(solution)/shard_map/pallas_call | solution.py:622
  43.7 4.3 %shard_map.117 = (f32[512,512]{1,0:T(8,128)S(1)}, f32[512,512]{1,0:T(8,128)S(1)}, f32[512,128]{1,0:T(8,128)S(1)}) custom-call(f32[512,1024]{1,0:T(8,128)S(1)} %get-tuple-element.64.refs_7_.refs_0_.refs_6_.refs_1_, f32[512,256]{1,0:T(8,128)S(1)} %get-tuple-element.61.refs_4_.refs_1_.refs_3_.refs_2_, ...), custom_call_target="tpu_custom_call" | custom-call | flops 2300000000 | bytes 1048576 | tf_op jit(solution)/shard_map/pallas_call | solution.py:622
  48.1 2.0 %shard_map.118 = (f32[640,512]{1,0:T(8,128)S(1)}, f32[144,512]{1,0:T(8,128)S(1)}) custom-call(bf16[512,1024]{1,0:T(8,128)(2,1)S(1)} %get-tuple-element.68.refs_4_.refs_0_.refs_9_, f32[16,256]{1,0:T(8,128)S(1)} %get-tuple-element.69.refs_1_, f32[512,128]{1,0:T(8,128)S(1)} %get-tuple-element.71.refs_2_.refs_15_, ...), custom_call_target="tpu_custom_call" | custom-call | flops 2415000064 | bytes 1048576 | tf_op jit(solution)/shard_map/pallas_call | solution.py:615
  50.1 2.0 %collective-permute-start.11 = (f32[144,512]{1,0:T(8,128)S(1)}, f32[144,512]{1,0:T(8,128)S(1)}, u32[]{:S(2)}, u32[]{:S(2)}) collective-permute-start(f32[144,512]{1,0:T(8,128)S(1)} %get-tuple-element.72), channel_id=1, source_target_pairs={{0,4},{1,5},{2,6},{3,7},{4,0},{5,1},{6,2},{7,3},{8,12},{9,13},{10,... | collective-permute-start | bytes 884744 | tf_op jit(solution)/shard_map/ppermute | solution.py:560
  53.5 5.7 %shard_map.119 = (bf16[128,512]{1,0:T(8,128)(2,1)S(1)}, bf16[128,512]{1,0:T(8,128)(2,1)S(1)}, bf16[128,512]{1,0:T(8,128)(2,1)S(1)}, bf16[128,512]{1,0:T(8,128)(2...) custom-call(f32[144,512]{1,0:T(8,128)S(1)} %collective-permute-done.12.refs_0_, ...), custom_call_target="tpu_custom_call" | custom-call | flops 6670000128 | bytes 1048576 | tf_op jit(solution)/shard_map/pallas_call | solution.py:641
  59.1 1.9 %collective-permute-start.16 = (bf16[128,512]{1,0:T(8,128)(2,1)S(1)}, bf16[128,512]{1,0:T(8,128)(2,1)S(1)}, u32[]{:S(2)}, u32[]{:S(2)}) collective-permute-start(bf16[128,512]{1,0:T(8,128)(2,1)S(1)} %get-tuple-element.89), channel_id=1, source_target_pairs={{0,1},{1,0},{2,3},{3,2},{4,5},{5,4},{6,7},{7,6},{8,9},{9,8},{10,11... | collective-permute-start | bytes 393224 | tf_op jit(solution)/shard_map/ppermute | solution.py:560
  61.0 1.7 %collective-permute-start.18 = (bf16[128,512]{1,0:T(8,128)(2,1)S(1)}, bf16[128,512]{1,0:T(8,128)(2,1)S(1)}, u32[]{:S(2)}, u32[]{:S(2)}) collective-permute-start(bf16[128,512]{1,0:T(8,128)(2,1)S(1)} %get-tuple-element.91), channel_id=1, source_target_pairs={{0,3},{1,2},{2,1},{3,0},{4,7},{5,6},{6,5},{7,4},{8,11},{9,10},{10,... | collective-permute-start | bytes 393224 | tf_op jit(solution)/shard_map/ppermute | solution.py:560
  62.7 4.4 %collective-permute-done.11.refs_0_ = f32[144,512]{1,0:T(8,128)S(1)} collective-permute-done((f32[144,512]{1,0:T(8,128)S(1)}, f32[144,512]{1,0:T(8,128)S(1)}, u32[]{:S(2)}, u32[]{:S(2)}) %collective-permute-start.11) | collective-permute-done | bytes 294944 | tf_op jit(solution)/shard_map/ppermute | solution.py:560
  67.1 5.9 %shard_map.120 = (bf16[128,1152]{1,0:T(8,128)(2,1)S(1)}, bf16[128,1152]{1,0:T(8,128)(2,1)S(1)}, bf16[128,1152]{1,0:T(8,128)(2,1)S(1)}, bf16[128,1152]{1,0:T(8,128)(2,1)S(1)}) custom-call(f32[144,512]{1,0:T(8,128)S(1)} %collective-permute-done.11.refs_0_, f32[512,1024]{1,0:T(8,128)S(1)} %get-tuple-element.64.refs_7_.refs_0_.refs_6_.refs_1_, ...), custom_call_target="tpu_custom_call" | custom-call | flops 6670000128 | bytes 1048576 | tf_op jit(solution)/shard_map/pallas_call | solution.py:641
  73.0 1.7 %collective-permute-start.13 = (bf16[128,1152]{1,0:T(8,128)(2,1)S(1)}, bf16[128,1152]{1,0:T(8,128)(2,1)S(1)}, u32[]{:S(2)}, u32[]{:S(2)}) collective-permute-start(bf16[128,1152]{1,0:T(8,128)(2,1)S(1)} %get-tuple-element.85), channel_id=1, source_target_pairs={{0,1},{1,0},{2,3},{3,2},{4,5},{5,4},{6,7},{7,6},{8,9},{9,8},{10,11... | collective-permute-start | bytes 884744 | tf_op jit(solution)/shard_map/ppermute | solution.py:560
  74.7 1.9 %collective-permute-start.15 = (bf16[128,1152]{1,0:T(8,128)(2,1)S(1)}, bf16[128,1152]{1,0:T(8,128)(2,1)S(1)}, u32[]{:S(2)}, u32[]{:S(2)}) collective-permute-start(bf16[128,1152]{1,0:T(8,128)(2,1)S(1)} %get-tuple-element.87), channel_id=1, source_target_pairs={{0,3},{1,2},{2,1},{3,0},{4,7},{5,6},{6,5},{7,4},{8,11},{9,10},{10,... | collective-permute-start | bytes 884744 | tf_op jit(solution)/shard_map/ppermute | solution.py:560
  77.4 4.7 %collective-permute-done.13.refs_1_ = bf16[128,1152]{1,0:T(8,128)(2,1)S(1)} collective-permute-done((bf16[128,1152]{1,0:T(8,128)(2,1)S(1)}, bf16[128,1152]{1,0:T(8,128)(2,1)S(1)}, u32[]{:S(2)}, u32[]{:S(2)}) %collective-permute-start.13) | collective-permute-done | bytes 294944 | tf_op jit(solution)/shard_map/ppermute | solution.py:560
  82.1 2.4 %collective-permute-done.14.refs_2_ = bf16[128,1152]{1,0:T(8,128)(2,1)S(1)} collective-permute-done((bf16[128,1152]{1,0:T(8,128)(2,1)S(1)}, bf16[128,1152]{1,0:T(8,128)(2,1)S(1)}, u32[]{:S(2)}, u32[]{:S(2)}) %collective-permute-start.14) | collective-permute-done | bytes 294944 | tf_op jit(solution)/shard_map/ppermute | solution.py:560
  84.6 5.1 %collective-permute-done.15.refs_3_ = bf16[128,1152]{1,0:T(8,128)(2,1)S(1)} collective-permute-done((bf16[128,1152]{1,0:T(8,128)(2,1)S(1)}, bf16[128,1152]{1,0:T(8,128)(2,1)S(1)}, u32[]{:S(2)}, u32[]{:S(2)}) %collective-permute-start.15) | collective-permute-done | bytes 294944 | tf_op jit(solution)/shard_map/ppermute | solution.py:560
  (35 shorter events, 8.2 us)
Async XLA Ops:
  2.3 11.6 %collective-permute-start.4 = (bf16[128,1408]{1,0:T(8,128)(2,1)S(1)}, bf16[128,1408]{1,0:T(8,128)(2,1)S(1)}, u32[]{:S(2)}, u32[]{:S(2)}) collective-permute-start(bf16[128,1408]{1,0:T(8,128)(2,1)S(1)} %get-tuple-element.54), channel_id=1, source_target_pairs={{0,1},{1,0},{2,3},{3,2},{4,5},{5,4},{6,7},{7,6},{8,9},{9,8},{10,11... | collective-permute-start | bytes 1081352 | tf_op jit(solution)/shard_map/ppermute | solution.py:560
  5.4 15.0 %collective-permute-start.5 = (bf16[128,1408]{1,0:T(8,128)(2,1)S(1)}, bf16[128,1408]{1,0:T(8,128)(2,1)S(1)}, u32[]{:S(2)}, u32[]{:S(2)}) collective-permute-start(bf16[128,1408]{1,0:T(8,128)(2,1)S(1)} %get-tuple-element.55), channel_id=1, source_target_pairs={{0,2},{1,3},{2,0},{3,1},{4,6},{5,7},{6,4},{7,5},{8,10},{9,11},{10,... | collective-permute-start | bytes 1081352 | tf_op jit(solution)/shard_map/ppermute | solution.py:560
  6.9 19.5 %collective-permute-start.6 = (bf16[128,1408]{1,0:T(8,128)(2,1)S(1)}, bf16[128,1408]{1,0:T(8,128)(2,1)S(1)}, u32[]{:S(2)}, u32[]{:S(2)}) collective-permute-start(bf16[128,1408]{1,0:T(8,128)(2,1)S(1)} %get-tuple-element.56), channel_id=1, source_target_pairs={{0,3},{1,2},{2,1},{3,0},{4,7},{5,6},{6,5},{7,4},{8,11},{9,10},{10,... | collective-permute-start | bytes 1081352 | tf_op jit(solution)/shard_map/ppermute | solution.py:560
  6.9 1.3 %collective-permute-start.7 = (bf16[16,1280]{1,0:T(8,128)(2,1)S(1)}, bf16[16,1280]{1,0:T(8,128)(2,1)S(1)}, u32[]{:S(2)}, u32[]{:S(2)}) collective-permute-start(bf16[16,1280]{1,0:T(8,128)(2,1)S(1)} %get-tuple-element.57), channel_id=1, source_target_pairs={{3,4},{11,12},{19,20},{27,28}} | collective-permute-start | bytes 122888 | tf_op jit(solution)/shard_map/ppermute | solution.py:594
  7.6 1.4 %collective-permute-start.8 = (bf16[16,1280]{1,0:T(8,128)(2,1)S(1)}, bf16[16,1280]{1,0:T(8,128)(2,1)S(1)}, u32[]{:S(2)}, u32[]{:S(2)}) collective-permute-start(bf16[16,1280]{1,0:T(8,128)(2,1)S(1)} %get-tuple-element.58), channel_id=1, source_target_pairs={{3,5},{11,13},{19,21},{27,29}} | collective-permute-start | bytes 122888 | tf_op jit(solution)/shard_map/ppermute | solution.py:594
  8.3 2.7 %collective-permute-start.9 = (bf16[16,1280]{1,0:T(8,128)(2,1)S(1)}, bf16[16,1280]{1,0:T(8,128)(2,1)S(1)}, u32[]{:S(2)}, u32[]{:S(2)}) collective-permute-start(bf16[16,1280]{1,0:T(8,128)(2,1)S(1)} %get-tuple-element.59), channel_id=1, source_target_pairs={{3,6},{11,14},{19,22},{27,30}} | collective-permute-start | bytes 122888 | tf_op jit(solution)/shard_map/ppermute | solution.py:594
  9.0 2.5 %collective-permute-start.10 = (bf16[16,1280]{1,0:T(8,128)(2,1)S(1)}, bf16[16,1280]{1,0:T(8,128)(2,1)S(1)}, u32[]{:S(2)}, u32[]{:S(2)}) collective-permute-start(bf16[16,1280]{1,0:T(8,128)(2,1)S(1)} %get-tuple-element.60), channel_id=1, source_target_pairs={{3,7},{11,15},{19,23},{27,31}} | collective-permute-start | bytes 122888 | tf_op jit(solution)/shard_map/ppermute | solution.py:594
  9.6 16.8 %copy-start.1 = (f32[1,4,4352]{2,1,0:T(4,128)S(1)}, f32[1,4,4352]{2,1,0:T(4,128)}, u32[]{:S(2)}) copy-start(f32[1,4,4352]{2,1,0:T(4,128)} %param.12) | copy-start | bytes 208900
  9.7 16.8 %copy-start.2 = (f32[1,4352]{1,0:T(1,128)S(1)}, f32[1,4352]{1,0:T(1,128)}, u32[]{:S(2)}) copy-start(f32[1,4352]{1,0:T(1,128)} %refs_9_.1) | copy-start | bytes 52228
  9.7 16.8 %copy-start.3 = (f32[1,64]{1,0:T(1,128)S(1)}, f32[1,64]{1,0:T(1,128)}, u32[]{:S(2)}) copy-start(f32[1,64]{1,0:T(1,128)} %refs_11_.2) | copy-start | bytes 772
  9.7 16.8 %copy-start.4 = (f32[1,64]{1,0:T(1,128)S(1)}, f32[1,64]{1,0:T(1,128)}, u32[]{:S(2)}) copy-start(f32[1,64]{1,0:T(1,128)} %refs_13_.3) | copy-start | bytes 772
  11.0 20.5 %collective-permute-start = (bf16[128,1024]{1,0:T(8,128)(2,1)S(1)}, bf16[128,1024]{1,0:T(8,128)(2,1)S(1)}, u32[]{:S(2)}, u32[]{:S(2)}) collective-permute-start(bf16[128,1024]{1,0:T(8,128)(2,1)S(1)} %get-tuple-element.49), channel_id=1, source_target_pairs={{8,0},{9,1},{10,2},{11,3},{12,4},{13,5},{14,6},{15,7},{16,8},{17,9... | collective-permute-start | bytes 786440 | tf_op jit(solution)/shard_map/ppermute | solution.py:568
  11.5 20.0 %collective-permute-start.1 = (bf16[128,1024]{1,0:T(8,128)(2,1)S(1)}, bf16[128,1024]{1,0:T(8,128)(2,1)S(1)}, u32[]{:S(2)}, u32[]{:S(2)}) collective-permute-start(bf16[128,1024]{1,0:T(8,128)(2,1)S(1)} %get-tuple-element.50), channel_id=1, source_target_pairs={{8,1},{9,0},{10,3},{11,2},{12,5},{13,4},{14,7},{15,6},{16,9},{17,8... | collective-permute-start | bytes 786440 | tf_op jit(solution)/shard_map/ppermute | solution.py:568
  14.0 17.5 %collective-permute-start.2 = (bf16[128,1024]{1,0:T(8,128)(2,1)S(1)}, bf16[128,1024]{1,0:T(8,128)(2,1)S(1)}, u32[]{:S(2)}, u32[]{:S(2)}) collective-permute-start(bf16[128,1024]{1,0:T(8,128)(2,1)S(1)} %get-tuple-element.51), channel_id=1, source_target_pairs={{8,2},{9,3},{10,0},{11,1},{12,6},{13,7},{14,4},{15,5},{16,10},{17,... | collective-permute-start | bytes 786440 | tf_op jit(solution)/shard_map/ppermute | solution.py:568
  20.4 15.0 %collective-permute-start.3 = (bf16[128,1024]{1,0:T(8,128)(2,1)S(1)}, bf16[128,1024]{1,0:T(8,128)(2,1)S(1)}, u32[]{:S(2)}, u32[]{:S(2)}) collective-permute-start(bf16[128,1024]{1,0:T(8,128)(2,1)S(1)} %get-tuple-element.52), channel_id=1, source_target_pairs={{8,3},{9,2},{10,1},{11,0},{12,7},{13,6},{14,5},{15,4},{16,11},{17,... | collective-permute-start | bytes 786440 | tf_op jit(solution)/shard_map/ppermute | solution.py:568
  26.5 8.9 %copy-start = (f32[1,64]{1,0:T(1,128)S(1)}, f32[1,64]{1,0:T(1,128)}, u32[]{:S(2)}) copy-start(f32[1,64]{1,0:T(1,128)} %refs_14_.3) | copy-start | bytes 772
  37.5 16.0 %collective-permute-start.12 = (f32[144,512]{1,0:T(8,128)S(1)}, f32[144,512]{1,0:T(8,128)S(1)}, u32[]{:S(2)}, u32[]{:S(2)}) collective-permute-start(f32[144,512]{1,0:T(8,128)S(1)} %get-tuple-element.77), channel_id=1, source_target_pairs={{0,4},{1,5},{2,6},{3,7},{4,0},{5,1},{6,2},{7,3},{8,12},{9,13},{10,... | collective-permute-start | bytes 884744 | tf_op jit(solution)/shard_map/ppermute | solution.py:560
  50.1 17.0 %collective-permute-start.11 = (f32[144,512]{1,0:T(8,128)S(1)}, f32[144,512]{1,0:T(8,128)S(1)}, u32[]{:S(2)}, u32[]{:S(2)}) collective-permute-start(f32[144,512]{1,0:T(8,128)S(1)} %get-tuple-element.72), channel_id=1, source_target_pairs={{0,4},{1,5},{2,6},{3,7},{4,0},{5,1},{6,2},{7,3},{8,12},{9,13},{10,... | collective-permute-start | bytes 884744 | tf_op jit(solution)/shard_map/ppermute | solution.py:560
  59.1 15.5 %collective-permute-start.16 = (bf16[128,512]{1,0:T(8,128)(2,1)S(1)}, bf16[128,512]{1,0:T(8,128)(2,1)S(1)}, u32[]{:S(2)}, u32[]{:S(2)}) collective-permute-start(bf16[128,512]{1,0:T(8,128)(2,1)S(1)} %get-tuple-element.89), channel_id=1, source_target_pairs={{0,1},{1,0},{2,3},{3,2},{4,5},{5,4},{6,7},{7,6},{8,9},{9,8},{10,11... | collective-permute-start | bytes 393224 | tf_op jit(solution)/shard_map/ppermute | solution.py:560
  61.0 15.6 %collective-permute-start.17 = (bf16[128,512]{1,0:T(8,128)(2,1)S(1)}, bf16[128,512]{1,0:T(8,128)(2,1)S(1)}, u32[]{:S(2)}, u32[]{:S(2)}) collective-permute-start(bf16[128,512]{1,0:T(8,128)(2,1)S(1)} %get-tuple-element.90), channel_id=1, source_target_pairs={{0,2},{1,3},{2,0},{3,1},{4,6},{5,7},{6,4},{7,5},{8,10},{9,11},{10,... | collective-permute-start | bytes 393224 | tf_op jit(solution)/shard_map/ppermute | solution.py:560
  61.0 15.6 %collective-permute-start.18 = (bf16[128,512]{1,0:T(8,128)(2,1)S(1)}, bf16[128,512]{1,0:T(8,128)(2,1)S(1)}, u32[]{:S(2)}, u32[]{:S(2)}) collective-permute-start(bf16[128,512]{1,0:T(8,128)(2,1)S(1)} %get-tuple-element.91), channel_id=1, source_target_pairs={{0,3},{1,2},{2,1},{3,0},{4,7},{5,6},{6,5},{7,4},{8,11},{9,10},{10,... | collective-permute-start | bytes 393224 | tf_op jit(solution)/shard_map/ppermute | solution.py:560
  73.0 9.1 %collective-permute-start.13 = (bf16[128,1152]{1,0:T(8,128)(2,1)S(1)}, bf16[128,1152]{1,0:T(8,128)(2,1)S(1)}, u32[]{:S(2)}, u32[]{:S(2)}) collective-permute-start(bf16[128,1152]{1,0:T(8,128)(2,1)S(1)} %get-tuple-element.85), channel_id=1, source_target_pairs={{0,1},{1,0},{2,3},{3,2},{4,5},{5,4},{6,7},{7,6},{8,9},{9,8},{10,11... | collective-permute-start | bytes 884744 | tf_op jit(solution)/shard_map/ppermute | solution.py:560
  74.7 9.9 %collective-permute-start.14 = (bf16[128,1152]{1,0:T(8,128)(2,1)S(1)}, bf16[128,1152]{1,0:T(8,128)(2,1)S(1)}, u32[]{:S(2)}, u32[]{:S(2)}) collective-permute-start(bf16[128,1152]{1,0:T(8,128)(2,1)S(1)} %get-tuple-element.86), channel_id=1, source_target_pairs={{0,2},{1,3},{2,0},{3,1},{4,6},{5,7},{6,4},{7,5},{8,10},{9,11},{10,... | collective-permute-start | bytes 884744 | tf_op jit(solution)/shard_map/ppermute | solution.py:560
  74.7 15.0 %collective-permute-start.15 = (bf16[128,1152]{1,0:T(8,128)(2,1)S(1)}, bf16[128,1152]{1,0:T(8,128)(2,1)S(1)}, u32[]{:S(2)}, u32[]{:S(2)}) collective-permute-start(bf16[128,1152]{1,0:T(8,128)(2,1)S(1)} %get-tuple-element.87), channel_id=1, source_target_pairs={{0,3},{1,2},{2,1},{3,0},{4,7},{5,6},{6,5},{7,4},{8,11},{9,10},{10,... | collective-permute-start | bytes 884744 | tf_op jit(solution)/shard_map/ppermute | solution.py:560

commit v5 on v4

--- a/solution.py
+++ b/solution.py
@@ -12,6 +12,7 @@
 HEAD = 64
 PAD = 8
 PARTS = 2
+UNROLL = 4
 F32 = jnp.float32
 BF16 = jnp.bfloat16
 NEG = -1e30
@@ -107,6 +108,14 @@
         for i in range(self.plan.tiles):
             lane = self.start + i * tile
             yield slice(i * tile, (i + 1) * tile), slice(lane, lane + tile), lane // HEAD
+
+
+def each_block(blocks, body):
+    if blocks <= UNROLL:
+        for b in range(blocks):
+            body(b, 0)
+    else:
+        lax.fori_loop(0, blocks, body, 0)
 
 
 def place(plan):
@@ -270,7 +279,7 @@
             gl_ref[rows, at] = gl_ref[nxt, at] * expand(decay, head, tile) + mm_wide(ct, ge)
         return carry
 
-    lax.fori_loop(0, blocks, body, 0)
+    each_block(blocks, body)
 
     @pl.when(late == 0)
     def _():
@@ -512,7 +521,7 @@
         nxt_dz[...] = dz[0:PAD, :]
         return carry
 
-    lax.fori_loop(0, blocks, body, 0)
+    each_block(blocks, body)
     for k in range(half):
         rows = pl.ds(pl.multiple_of(jnp.bitwise_xor(own, k) * BLOCK, BLOCK), BLOCK)
         outs[k][...] = o_sc[rows, :]

time: 91.4 us -> 89.4 us (0.978)
  starting transfers between devices: 27.7 us -> 32.9 us
  Pallas kernels: 34.7 us -> 30.7 us
  waiting for transfers between devices: 27.9 us -> 24.5 us
    ppermute x11, starting transfers between devices: 15.6 us -> 20.8 us  [partner(): return lax.ppermute(array, 'ctx', [(i, i ^ k) for i in range(devices)])]
    ppermute x11, waiting for transfers between devices: 24 us -> 20.7 us  [partner(): return lax.ppermute(array, 'ctx', [(i, i ^ k) for i in range(devices)])]
    pallas_call x2, Pallas kernels: 11.6 us -> 9.36 us  [per_device(): result = call(final_kernel, stage, outs, scratch, work=5.8)(*args)]
    pallas_call x2, Pallas kernels: 4.12 us -> 2.39 us  [per_device(): call(gradient_kernel, stage, outs, [small], work=2.1)(*args)]
  transfers between devices with their start and end apart: 19 -> 19, of which waited for: 7 -> 6; matrix products, arithmetic and copies ran while one was open for 0% -> 0% of each run, Pallas kernels for 32% -> 30%
where the time goes in v5:
time: 89.4 us; the launch traced here: 89.2 us
  starting transfers between devices  32.9 us (37%)
  Pallas kernels  30.7 us (34%)
  waiting for transfers between devices  24.5 us (27%)
  between operations  1.01 us (1%)
    ppermute x11, starting transfers between devices, partner(): return lax.ppermute(array, 'ctx', [(i, i ^ k) for i in range(devices)])  20.8 us
    ppermute x11, waiting for transfers between devices, partner(): return lax.ppermute(array, 'ctx', [(i, i ^ k) for i in range(devices)])  20.7 us
    ppermute x4, starting transfers between devices, shifted(): return lax.ppermute(array, ('pipe', 'ctx'), route)  9.43 us
    pallas_call x2, Pallas kernels, per_device(): result = call(final_kernel, stage, outs, scratch, work=5.8)(*args)  9.36 us
    pallas_call x2, Pallas kernels, per_device(): call(within_kernel, other, outs, work=2.0)(*args)  8.69 us
    pallas_call x1, Pallas kernels, per_device(): call(forward_kernel, plan, [near(tokens, plan.all), near(tokens, plan.all...  5.02 us
    ppermute x4, waiting for transfers between devices, shifted(): return lax.ppermute(array, ('pipe', 'ctx'), route)  3.85 us
    ppermute x4, starting transfers between devices, per_device(): lax.ppermute(e, 'ctx', [(half - 1, half + k)])  2.64 us
  transfers between devices with their start and end apart: 19, of which 6 were waited for; matrix products, arithmetic and copies ran while one was open for 0% of the time, Pallas kernels for 30%

profile of v5, /device:TPU:0, one launch (start us, length us, event | category | flops | bytes accessed | tf_op | source)
XLA Modules:
  0.0 89.2 jit_solution(14460901402664997115)
XLA Ops:
  0.6 1.7 %shard_map.113 = (bf16[128,1408]{1,0:T(8,128)(2,1)S(1)}, bf16[128,1408]{1,0:T(8,128)(2,1)S(1)}, bf16[128,1408]{1,0:T(8,128)(2,1)S(1)}, bf16[128,1408]{1,0:T(8,12...) custom-call(bf16[128,4096]{1,0:T(8,128)(2,1)} %bitcast.15, ...), custom_call_target="tpu_custom_call" | custom-call | flops 3449999872 | bytes 1048576 | tf_op jit(solution)/shard_map/pallas_call | solution.py:586
  2.3 3.0 %collective-permute-start.4 = (bf16[128,1408]{1,0:T(8,128)(2,1)S(1)}, bf16[128,1408]{1,0:T(8,128)(2,1)S(1)}, u32[]{:S(2)}, u32[]{:S(2)}) collective-permute-start(bf16[128,1408]{1,0:T(8,128)(2,1)S(1)} %get-tuple-element.54), channel_id=1, source_target_pairs={{0,1},{1,0},{2,3},{3,2},{4,5},{5,4},{6,7},{7,6},{8,9},{9,8},{10,11... | collective-permute-start | bytes 1081352 | tf_op jit(solution)/shard_map/ppermute | solution.py:569
  5.4 1.6 %collective-permute-start.5 = (bf16[128,1408]{1,0:T(8,128)(2,1)S(1)}, bf16[128,1408]{1,0:T(8,128)(2,1)S(1)}, u32[]{:S(2)}, u32[]{:S(2)}) collective-permute-start(bf16[128,1408]{1,0:T(8,128)(2,1)S(1)} %get-tuple-element.55), channel_id=1, source_target_pairs={{0,2},{1,3},{2,0},{3,1},{4,6},{5,7},{6,4},{7,5},{8,10},{9,11},{10,... | collective-permute-start | bytes 1081352 | tf_op jit(solution)/shard_map/ppermute | solution.py:569
  11.5 2.5 %collective-permute-start.1 = (bf16[128,1024]{1,0:T(8,128)(2,1)S(1)}, bf16[128,1024]{1,0:T(8,128)(2,1)S(1)}, u32[]{:S(2)}, u32[]{:S(2)}) collective-permute-start(bf16[128,1024]{1,0:T(8,128)(2,1)S(1)} %get-tuple-element.50), channel_id=1, source_target_pairs={{8,1},{9,0},{10,3},{11,2},{12,5},{13,4},{14,7},{15,6},{16,9},{17,8... | collective-permute-start | bytes 786440 | tf_op jit(solution)/shard_map/ppermute | solution.py:577
  14.0 6.4 %collective-permute-start.2 = (bf16[128,1024]{1,0:T(8,128)(2,1)S(1)}, bf16[128,1024]{1,0:T(8,128)(2,1)S(1)}, u32[]{:S(2)}, u32[]{:S(2)}) collective-permute-start(bf16[128,1024]{1,0:T(8,128)(2,1)S(1)} %get-tuple-element.51), channel_id=1, source_target_pairs={{8,2},{9,3},{10,0},{11,1},{12,6},{13,7},{14,4},{15,5},{16,10},{17,... | collective-permute-start | bytes 786440 | tf_op jit(solution)/shard_map/ppermute | solution.py:577
  20.4 6.0 %collective-permute-done.6.refs_3_ = bf16[128,1408]{1,0:T(8,128)(2,1)S(1)} collective-permute-done((bf16[128,1408]{1,0:T(8,128)(2,1)S(1)}, bf16[128,1408]{1,0:T(8,128)(2,1)S(1)}, u32[]{:S(2)}, u32[]{:S(2)}) %collective-permute-start.6) | collective-permute-done | bytes 360480 | tf_op jit(solution)/shard_map/ppermute | solution.py:569
  26.5 5.0 %shard_map.114 = (f32[512,1024]{1,0:T(8,128)S(1)}, f32[512,1024]{1,0:T(8,128)S(1)}, f32[640,1024]{1,0:T(8,128)S(1)}, f32[512,256]{1,0:T(8,128)S(1)}, f32[512,256...) custom-call(bf16[128,1408]{1,0:T(8,128)(2,1)S(1)} %get-tuple-element.53.refs_0_, ...), custom_call_target="tpu_custom_call" | custom-call | flops 5750000128 | bytes 1048576 | tf_op jit(solution)/shard_map/pallas_call | solution.py:607
  31.5 3.8 %collective-permute-done.3.refs_3_ = bf16[128,1024]{1,0:T(8,128)(2,1)S(1)} collective-permute-done((bf16[128,1024]{1,0:T(8,128)(2,1)S(1)}, bf16[128,1024]{1,0:T(8,128)(2,1)S(1)}, u32[]{:S(2)}, u32[]{:S(2)}) %collective-permute-start.3) | collective-permute-done | bytes 262176 | tf_op jit(solution)/shard_map/ppermute | solution.py:577
  36.5 1.9 %collective-permute-start.12 = (f32[144,512]{1,0:T(8,128)S(1)}, f32[144,512]{1,0:T(8,128)S(1)}, u32[]{:S(2)}, u32[]{:S(2)}) collective-permute-start(f32[144,512]{1,0:T(8,128)S(1)} %get-tuple-element.77), channel_id=1, source_target_pairs={{0,4},{1,5},{2,6},{3,7},{4,0},{5,1},{6,2},{7,3},{8,12},{9,13},{10,... | collective-permute-start | bytes 884744 | tf_op jit(solution)/shard_map/ppermute | solution.py:569
  38.4 4.3 %shard_map.116 = (f32[512,512]{1,0:T(8,128)S(1)}, f32[512,512]{1,0:T(8,128)S(1)}, f32[512,128]{1,0:T(8,128)S(1)}) custom-call(f32[512,1024]{1,0:T(8,128)S(1)} %get-tuple-element.64.refs_7_.refs_0_.refs_6_.refs_1_, f32[512,256]{1,0:T(8,128)S(1)} %get-tuple-element.61.refs_4_.refs_1_.refs_3_.refs_2_, ...), custom_call_target="tpu_custom_call" | custom-call | flops 2300000000 | bytes 1048576 | tf_op jit(solution)/shard_map/pallas_call | solution.py:631
  42.8 4.3 %shard_map.117 = (f32[512,512]{1,0:T(8,128)S(1)}, f32[512,512]{1,0:T(8,128)S(1)}, f32[512,128]{1,0:T(8,128)S(1)}) custom-call(f32[512,1024]{1,0:T(8,128)S(1)} %get-tuple-element.64.refs_7_.refs_0_.refs_6_.refs_1_, f32[512,256]{1,0:T(8,128)S(1)} %get-tuple-element.61.refs_4_.refs_1_.refs_3_.refs_2_, ...), custom_call_target="tpu_custom_call" | custom-call | flops 2300000000 | bytes 1048576 | tf_op jit(solution)/shard_map/pallas_call | solution.py:631
  48.4 2.0 %collective-permute-start.11 = (f32[144,512]{1,0:T(8,128)S(1)}, f32[144,512]{1,0:T(8,128)S(1)}, u32[]{:S(2)}, u32[]{:S(2)}) collective-permute-start(f32[144,512]{1,0:T(8,128)S(1)} %get-tuple-element.72), channel_id=1, source_target_pairs={{0,4},{1,5},{2,6},{3,7},{4,0},{5,1},{6,2},{7,3},{8,12},{9,13},{10,... | collective-permute-start | bytes 884744 | tf_op jit(solution)/shard_map/ppermute | solution.py:569
  50.4 2.1 %collective-permute-done.12.refs_0_ = f32[144,512]{1,0:T(8,128)S(1)} collective-permute-done((f32[144,512]{1,0:T(8,128)S(1)}, f32[144,512]{1,0:T(8,128)S(1)}, u32[]{:S(2)}, u32[]{:S(2)}) %collective-permute-start.12) | collective-permute-done | bytes 294944 | tf_op jit(solution)/shard_map/ppermute | solution.py:569
  52.5 4.5 %shard_map.119 = (bf16[128,512]{1,0:T(8,128)(2,1)S(1)}, bf16[128,512]{1,0:T(8,128)(2,1)S(1)}, bf16[128,512]{1,0:T(8,128)(2,1)S(1)}, bf16[128,512]{1,0:T(8,128)(2...) custom-call(f32[144,512]{1,0:T(8,128)S(1)} %collective-permute-done.12.refs_0_, ...), custom_call_target="tpu_custom_call" | custom-call | flops 6670000128 | bytes 1048576 | tf_op jit(solution)/shard_map/pallas_call | solution.py:650
  57.0 1.9 %collective-permute-start.16 = (bf16[128,512]{1,0:T(8,128)(2,1)S(1)}, bf16[128,512]{1,0:T(8,128)(2,1)S(1)}, u32[]{:S(2)}, u32[]{:S(2)}) collective-permute-start(bf16[128,512]{1,0:T(8,128)(2,1)S(1)} %get-tuple-element.89), channel_id=1, source_target_pairs={{0,1},{1,0},{2,3},{3,2},{4,5},{5,4},{6,7},{7,6},{8,9},{9,8},{10,11... | collective-permute-start | bytes 393224 | tf_op jit(solution)/shard_map/ppermute | solution.py:569
  58.8 5.5 %collective-permute-start.17 = (bf16[128,512]{1,0:T(8,128)(2,1)S(1)}, bf16[128,512]{1,0:T(8,128)(2,1)S(1)}, u32[]{:S(2)}, u32[]{:S(2)}) collective-permute-start(bf16[128,512]{1,0:T(8,128)(2,1)S(1)} %get-tuple-element.90), channel_id=1, source_target_pairs={{0,2},{1,3},{2,0},{3,1},{4,6},{5,7},{6,4},{7,5},{8,10},{9,11},{10,... | collective-permute-start | bytes 393224 | tf_op jit(solution)/shard_map/ppermute | solution.py:569
  64.3 1.4 %collective-permute-start.18 = (bf16[128,512]{1,0:T(8,128)(2,1)S(1)}, bf16[128,512]{1,0:T(8,128)(2,1)S(1)}, u32[]{:S(2)}, u32[]{:S(2)}) collective-permute-start(bf16[128,512]{1,0:T(8,128)(2,1)S(1)} %get-tuple-element.91), channel_id=1, source_target_pairs={{0,3},{1,2},{2,1},{3,0},{4,7},{5,6},{6,5},{7,4},{8,11},{9,10},{10,... | collective-permute-start | bytes 393224 | tf_op jit(solution)/shard_map/ppermute | solution.py:569
  65.7 4.9 %shard_map.120 = (bf16[128,1152]{1,0:T(8,128)(2,1)S(1)}, bf16[128,1152]{1,0:T(8,128)(2,1)S(1)}, bf16[128,1152]{1,0:T(8,128)(2,1)S(1)}, bf16[128,1152]{1,0:T(8,128)(2,1)S(1)}) custom-call(f32[144,512]{1,0:T(8,128)S(1)} %collective-permute-done.11.refs_0_, f32[512,1024]{1,0:T(8,128)S(1)} %get-tuple-element.64.refs_7_.refs_0_.refs_6_.refs_1_, ...), custom_call_target="tpu_custom_call" | custom-call | flops 6670000128 | bytes 1048576 | tf_op jit(solution)/shard_map/pallas_call | solution.py:650
  70.6 1.3 %collective-permute-start.13 = (bf16[128,1152]{1,0:T(8,128)(2,1)S(1)}, bf16[128,1152]{1,0:T(8,128)(2,1)S(1)}, u32[]{:S(2)}, u32[]{:S(2)}) collective-permute-start(bf16[128,1152]{1,0:T(8,128)(2,1)S(1)} %get-tuple-element.85), channel_id=1, source_target_pairs={{0,1},{1,0},{2,3},{3,2},{4,5},{5,4},{6,7},{7,6},{8,9},{9,8},{10,11... | collective-permute-start | bytes 884744 | tf_op jit(solution)/shard_map/ppermute | solution.py:569
  72.7 1.4 %collective-permute-start.15 = (bf16[128,1152]{1,0:T(8,128)(2,1)S(1)}, bf16[128,1152]{1,0:T(8,128)(2,1)S(1)}, u32[]{:S(2)}, u32[]{:S(2)}) collective-permute-start(bf16[128,1152]{1,0:T(8,128)(2,1)S(1)} %get-tuple-element.87), channel_id=1, source_target_pairs={{0,3},{1,2},{2,1},{3,0},{4,7},{5,6},{6,5},{7,4},{8,11},{9,10},{10,... | collective-permute-start | bytes 884744 | tf_op jit(solution)/shard_map/ppermute | solution.py:569
  75.0 5.1 %collective-permute-done.13.refs_1_ = bf16[128,1152]{1,0:T(8,128)(2,1)S(1)} collective-permute-done((bf16[128,1152]{1,0:T(8,128)(2,1)S(1)}, bf16[128,1152]{1,0:T(8,128)(2,1)S(1)}, u32[]{:S(2)}, u32[]{:S(2)}) %collective-permute-start.13) | collective-permute-done | bytes 294944 | tf_op jit(solution)/shard_map/ppermute | solution.py:569
  80.0 1.7 %collective-permute-done.14.refs_2_ = bf16[128,1152]{1,0:T(8,128)(2,1)S(1)} collective-permute-done((bf16[128,1152]{1,0:T(8,128)(2,1)S(1)}, bf16[128,1152]{1,0:T(8,128)(2,1)S(1)}, u32[]{:S(2)}, u32[]{:S(2)}) %collective-permute-start.14) | collective-permute-done | bytes 294944 | tf_op jit(solution)/shard_map/ppermute | solution.py:569
  81.7 5.8 %collective-permute-done.15.refs_3_ = bf16[128,1152]{1,0:T(8,128)(2,1)S(1)} collective-permute-done((bf16[128,1152]{1,0:T(8,128)(2,1)S(1)}, bf16[128,1152]{1,0:T(8,128)(2,1)S(1)}, u32[]{:S(2)}, u32[]{:S(2)}) %collective-permute-start.15) | collective-permute-done | bytes 294944 | tf_op jit(solution)/shard_map/ppermute | solution.py:569
  87.5 1.5 %shard_map.122 = (bf16[128,4096]{1,0:T(8,128)(2,1)}, bf16[128,256]{1,0:T(8,128)(2,1)}, bf16[64,128]{1,0:T(8,128)(2,1)}) custom-call(bf16[128,1152]{1,0:T(8,128)(2,1)S(1)} %get-tuple-element.84.refs_0_, bf16[128,1152]{1,0:T(8,128)(2,1)S(1)} %collective-permute-done.13.refs_1_, ...), custom_call_target="tpu_custom_call", output_to_operand_aliasing={{0}: (4, {})} | custom-call | flops 2300000000 | bytes 1048576 | tf_op jit(solution)/shard_map/pallas_call | solution.py:659
  (35 shorter events, 8.5 us)
Async XLA Ops:
  2.3 11.6 %collective-permute-start.4 = (bf16[128,1408]{1,0:T(8,128)(2,1)S(1)}, bf16[128,1408]{1,0:T(8,128)(2,1)S(1)}, u32[]{:S(2)}, u32[]{:S(2)}) collective-permute-start(bf16[128,1408]{1,0:T(8,128)(2,1)S(1)} %get-tuple-element.54), channel_id=1, source_target_pairs={{0,1},{1,0},{2,3},{3,2},{4,5},{5,4},{6,7},{7,6},{8,9},{9,8},{10,11... | collective-permute-start | bytes 1081352 | tf_op jit(solution)/shard_map/ppermute | solution.py:569
  5.4 15.0 %collective-permute-start.5 = (bf16[128,1408]{1,0:T(8,128)(2,1)S(1)}, bf16[128,1408]{1,0:T(8,128)(2,1)S(1)}, u32[]{:S(2)}, u32[]{:S(2)}) collective-permute-start(bf16[128,1408]{1,0:T(8,128)(2,1)S(1)} %get-tuple-element.55), channel_id=1, source_target_pairs={{0,2},{1,3},{2,0},{3,1},{4,6},{5,7},{6,4},{7,5},{8,10},{9,11},{10,... | collective-permute-start | bytes 1081352 | tf_op jit(solution)/shard_map/ppermute | solution.py:569
  6.9 19.5 %collective-permute-start.6 = (bf16[128,1408]{1,0:T(8,128)(2,1)S(1)}, bf16[128,1408]{1,0:T(8,128)(2,1)S(1)}, u32[]{:S(2)}, u32[]{:S(2)}) collective-permute-start(bf16[128,1408]{1,0:T(8,128)(2,1)S(1)} %get-tuple-element.56), channel_id=1, source_target_pairs={{0,3},{1,2},{2,1},{3,0},{4,7},{5,6},{6,5},{7,4},{8,11},{9,10},{10,... | collective-permute-start | bytes 1081352 | tf_op jit(solution)/shard_map/ppermute | solution.py:569
  6.9 1.3 %collective-permute-start.7 = (bf16[16,1280]{1,0:T(8,128)(2,1)S(1)}, bf16[16,1280]{1,0:T(8,128)(2,1)S(1)}, u32[]{:S(2)}, u32[]{:S(2)}) collective-permute-start(bf16[16,1280]{1,0:T(8,128)(2,1)S(1)} %get-tuple-element.57), channel_id=1, source_target_pairs={{3,4},{11,12},{19,20},{27,28}} | collective-permute-start | bytes 122888 | tf_op jit(solution)/shard_map/ppermute | solution.py:603
  7.6 1.4 %collective-permute-start.8 = (bf16[16,1280]{1,0:T(8,128)(2,1)S(1)}, bf16[16,1280]{1,0:T(8,128)(2,1)S(1)}, u32[]{:S(2)}, u32[]{:S(2)}) collective-permute-start(bf16[16,1280]{1,0:T(8,128)(2,1)S(1)} %get-tuple-element.58), channel_id=1, source_target_pairs={{3,5},{11,13},{19,21},{27,29}} | collective-permute-start | bytes 122888 | tf_op jit(solution)/shard_map/ppermute | solution.py:603
  8.3 2.7 %collective-permute-start.9 = (bf16[16,1280]{1,0:T(8,128)(2,1)S(1)}, bf16[16,1280]{1,0:T(8,128)(2,1)S(1)}, u32[]{:S(2)}, u32[]{:S(2)}) collective-permute-start(bf16[16,1280]{1,0:T(8,128)(2,1)S(1)} %get-tuple-element.59), channel_id=1, source_target_pairs={{3,6},{11,14},{19,22},{27,30}} | collective-permute-start | bytes 122888 | tf_op jit(solution)/shard_map/ppermute | solution.py:603
  9.0 2.5 %collective-permute-start.10 = (bf16[16,1280]{1,0:T(8,128)(2,1)S(1)}, bf16[16,1280]{1,0:T(8,128)(2,1)S(1)}, u32[]{:S(2)}, u32[]{:S(2)}) collective-permute-start(bf16[16,1280]{1,0:T(8,128)(2,1)S(1)} %get-tuple-element.60), channel_id=1, source_target_pairs={{3,7},{11,15},{19,23},{27,31}} | collective-permute-start | bytes 122888 | tf_op jit(solution)/shard_map/ppermute | solution.py:603
  9.6 16.8 %copy-start.1 = (f32[1,4,4352]{2,1,0:T(4,128)S(1)}, f32[1,4,4352]{2,1,0:T(4,128)}, u32[]{:S(2)}) copy-start(f32[1,4,4352]{2,1,0:T(4,128)} %param.12) | copy-start | bytes 208900
  9.7 16.8 %copy-start.2 = (f32[1,4352]{1,0:T(1,128)S(1)}, f32[1,4352]{1,0:T(1,128)}, u32[]{:S(2)}) copy-start(f32[1,4352]{1,0:T(1,128)} %refs_9_.1) | copy-start | bytes 52228
  9.7 16.8 %copy-start.3 = (f32[1,64]{1,0:T(1,128)S(1)}, f32[1,64]{1,0:T(1,128)}, u32[]{:S(2)}) copy-start(f32[1,64]{1,0:T(1,128)} %refs_11_.2) | copy-start | bytes 772
  9.7 16.8 %copy-start.4 = (f32[1,64]{1,0:T(1,128)S(1)}, f32[1,64]{1,0:T(1,128)}, u32[]{:S(2)}) copy-start(f32[1,64]{1,0:T(1,128)} %refs_13_.3) | copy-start | bytes 772
  11.0 20.5 %collective-permute-start = (bf16[128,1024]{1,0:T(8,128)(2,1)S(1)}, bf16[128,1024]{1,0:T(8,128)(2,1)S(1)}, u32[]{:S(2)}, u32[]{:S(2)}) collective-permute-start(bf16[128,1024]{1,0:T(8,128)(2,1)S(1)} %get-tuple-element.49), channel_id=1, source_target_pairs={{8,0},{9,1},{10,2},{11,3},{12,4},{13,5},{14,6},{15,7},{16,8},{17,9... | collective-permute-start | bytes 786440 | tf_op jit(solution)/shard_map/ppermute | solution.py:577
  11.5 20.0 %collective-permute-start.1 = (bf16[128,1024]{1,0:T(8,128)(2,1)S(1)}, bf16[128,1024]{1,0:T(8,128)(2,1)S(1)}, u32[]{:S(2)}, u32[]{:S(2)}) collective-permute-start(bf16[128,1024]{1,0:T(8,128)(2,1)S(1)} %get-tuple-element.50), channel_id=1, source_target_pairs={{8,1},{9,0},{10,3},{11,2},{12,5},{13,4},{14,7},{15,6},{16,9},{17,8... | collective-permute-start | bytes 786440 | tf_op jit(solution)/shard_map/ppermute | solution.py:577
  14.0 17.6 %collective-permute-start.2 = (bf16[128,1024]{1,0:T(8,128)(2,1)S(1)}, bf16[128,1024]{1,0:T(8,128)(2,1)S(1)}, u32[]{:S(2)}, u32[]{:S(2)}) collective-permute-start(bf16[128,1024]{1,0:T(8,128)(2,1)S(1)} %get-tuple-element.51), channel_id=1, source_target_pairs={{8,2},{9,3},{10,0},{11,1},{12,6},{13,7},{14,4},{15,5},{16,10},{17,... | collective-permute-start | bytes 786440 | tf_op jit(solution)/shard_map/ppermute | solution.py:577
  20.4 15.0 %collective-permute-start.3 = (bf16[128,1024]{1,0:T(8,128)(2,1)S(1)}, bf16[128,1024]{1,0:T(8,128)(2,1)S(1)}, u32[]{:S(2)}, u32[]{:S(2)}) collective-permute-start(bf16[128,1024]{1,0:T(8,128)(2,1)S(1)} %get-tuple-element.52), channel_id=1, source_target_pairs={{8,3},{9,2},{10,1},{11,0},{12,7},{13,6},{14,5},{15,4},{16,11},{17,... | collective-permute-start | bytes 786440 | tf_op jit(solution)/shard_map/ppermute | solution.py:577
  26.5 8.9 %copy-start = (f32[1,64]{1,0:T(1,128)S(1)}, f32[1,64]{1,0:T(1,128)}, u32[]{:S(2)}) copy-start(f32[1,64]{1,0:T(1,128)} %refs_14_.3) | copy-start | bytes 772
  36.5 16.0 %collective-permute-start.12 = (f32[144,512]{1,0:T(8,128)S(1)}, f32[144,512]{1,0:T(8,128)S(1)}, u32[]{:S(2)}, u32[]{:S(2)}) collective-permute-start(f32[144,512]{1,0:T(8,128)S(1)} %get-tuple-element.77), channel_id=1, source_target_pairs={{0,4},{1,5},{2,6},{3,7},{4,0},{5,1},{6,2},{7,3},{8,12},{9,13},{10,... | collective-permute-start | bytes 884744 | tf_op jit(solution)/shard_map/ppermute | solution.py:569
  48.4 17.3 %collective-permute-start.11 = (f32[144,512]{1,0:T(8,128)S(1)}, f32[144,512]{1,0:T(8,128)S(1)}, u32[]{:S(2)}, u32[]{:S(2)}) collective-permute-start(f32[144,512]{1,0:T(8,128)S(1)} %get-tuple-element.72), channel_id=1, source_target_pairs={{0,4},{1,5},{2,6},{3,7},{4,0},{5,1},{6,2},{7,3},{8,12},{9,13},{10,... | collective-permute-start | bytes 884744 | tf_op jit(solution)/shard_map/ppermute | solution.py:569
  57.0 15.8 %collective-permute-start.16 = (bf16[128,512]{1,0:T(8,128)(2,1)S(1)}, bf16[128,512]{1,0:T(8,128)(2,1)S(1)}, u32[]{:S(2)}, u32[]{:S(2)}) collective-permute-start(bf16[128,512]{1,0:T(8,128)(2,1)S(1)} %get-tuple-element.89), channel_id=1, source_target_pairs={{0,1},{1,0},{2,3},{3,2},{4,5},{5,4},{6,7},{7,6},{8,9},{9,8},{10,11... | collective-permute-start | bytes 393224 | tf_op jit(solution)/shard_map/ppermute | solution.py:569
  58.8 15.3 %collective-permute-start.17 = (bf16[128,512]{1,0:T(8,128)(2,1)S(1)}, bf16[128,512]{1,0:T(8,128)(2,1)S(1)}, u32[]{:S(2)}, u32[]{:S(2)}) collective-permute-start(bf16[128,512]{1,0:T(8,128)(2,1)S(1)} %get-tuple-element.90), channel_id=1, source_target_pairs={{0,2},{1,3},{2,0},{3,1},{4,6},{5,7},{6,4},{7,5},{8,10},{9,11},{10,... | collective-permute-start | bytes 393224 | tf_op jit(solution)/shard_map/ppermute | solution.py:569
  64.3 9.9 %collective-permute-start.18 = (bf16[128,512]{1,0:T(8,128)(2,1)S(1)}, bf16[128,512]{1,0:T(8,128)(2,1)S(1)}, u32[]{:S(2)}, u32[]{:S(2)}) collective-permute-start(bf16[128,512]{1,0:T(8,128)(2,1)S(1)} %get-tuple-element.91), channel_id=1, source_target_pairs={{0,3},{1,2},{2,1},{3,0},{4,7},{5,6},{6,5},{7,4},{8,11},{9,10},{10,... | collective-permute-start | bytes 393224 | tf_op jit(solution)/shard_map/ppermute | solution.py:569
  70.6 9.5 %collective-permute-start.13 = (bf16[128,1152]{1,0:T(8,128)(2,1)S(1)}, bf16[128,1152]{1,0:T(8,128)(2,1)S(1)}, u32[]{:S(2)}, u32[]{:S(2)}) collective-permute-start(bf16[128,1152]{1,0:T(8,128)(2,1)S(1)} %get-tuple-element.85), channel_id=1, source_target_pairs={{0,1},{1,0},{2,3},{3,2},{4,5},{5,4},{6,7},{7,6},{8,9},{9,8},{10,11... | collective-permute-start | bytes 884744 | tf_op jit(solution)/shard_map/ppermute | solution.py:569
  71.9 9.8 %collective-permute-start.14 = (bf16[128,1152]{1,0:T(8,128)(2,1)S(1)}, bf16[128,1152]{1,0:T(8,128)(2,1)S(1)}, u32[]{:S(2)}, u32[]{:S(2)}) collective-permute-start(bf16[128,1152]{1,0:T(8,128)(2,1)S(1)} %get-tuple-element.86), channel_id=1, source_target_pairs={{0,2},{1,3},{2,0},{3,1},{4,6},{5,7},{6,4},{7,5},{8,10},{9,11},{10,... | collective-permute-start | bytes 884744 | tf_op jit(solution)/shard_map/ppermute | solution.py:569
  72.7 14.8 %collective-permute-start.15 = (bf16[128,1152]{1,0:T(8,128)(2,1)S(1)}, bf16[128,1152]{1,0:T(8,128)(2,1)S(1)}, u32[]{:S(2)}, u32[]{:S(2)}) collective-permute-start(bf16[128,1152]{1,0:T(8,128)(2,1)S(1)} %get-tuple-element.87), channel_id=1, source_target_pairs={{0,3},{1,2},{2,1},{3,0},{4,7},{5,6},{6,5},{7,4},{8,11},{9,10},{10,... | collective-permute-start | bytes 884744 | tf_op jit(solution)/shard_map/ppermute | solution.py:569

commit v6 on v5

--- a/solution.py
+++ b/solution.py
@@ -91,6 +91,7 @@
         self.tile = 2 * LANES if self.width % (2 * LANES) == 0 else LANES
         self.tiles = self.width // self.tile
         self.blocks = self.half
+        self.spans = -(-self.heads // PAD)
         self.tokens = self.half * BLOCK
 
 
@@ -102,6 +103,9 @@
         self.last = part == plan.parts - 1
         self.head = part * plan.width // HEAD
         self.start = part * plan.width
+
+        self.edge = 2 * PAD if self.last else PAD
+        self.grown = PAD if self.last else 3
 
     def steps(self):
         tile = self.plan.tile
@@ -284,7 +288,7 @@
     @pl.when(late == 0)
     def _():
         send_ref[0:BLOCK, :] = el_ref[blocks * BLOCK :, stage.start : stage.start + width]
-        send_ref[BLOCK:, :] = jnp.zeros((16, width), F32)
+        send_ref[BLOCK:, :] = jnp.zeros((stage.edge, width), F32)
         if not last:
             top_ref[...] = jnp.zeros_like(top_ref)
 
@@ -293,7 +297,7 @@
         send_ref[0:BLOCK, :] = gl_ref[0:BLOCK, :]
         (skips,) = head_rows(plan, prm, [sk_ref[...]], own)
         top = slice(0, 16)
-        edge = send_ref.at[BLOCK : BLOCK + 16, :]
+        edge = send_ref.at[BLOCK : BLOCK + stage.edge, :]
         cum, step, cum_t = cum_ref[top, :], st_ref[top, :], cum_ref[0:BLOCK, :].T
         shrunk, grown = jnp.exp(cum_ref[BLOCK - 1 : BLOCK, :] - cum), jnp.exp(cum)
         top_b, first_c = split(xm_ref[top, :state]), split(xm_ref[0:BLOCK, state:])
@@ -332,7 +336,7 @@
             d_b = d_b + mm_over(split(xs * shrunk_x), leaving)
             top_gy = gy[0:16].astype(F32)
             edge[0:PAD, at] = ((dxs * step_x + expand(skips, head) * top_gy) * ds_ref[top, among])[0:PAD]
-            edge[PAD:, at] = (top_gy * expand(grown, head))[0:PAD]
+            edge[stage.grown : stage.edge, at] = (top_gy * expand(grown, head))[0 : stage.edge - stage.grown]
         if last:
             parts = split(dsc)
             d_b = (d_b + mm3(parts, first_c)) * dm_ref[top, :state]
@@ -408,7 +412,7 @@
     (both_ref, x_ref, xm_ref, ds_ref, st_ref, sg_ref, cum_ref, el_ref, gl_ref, gy_ref, yw_ref, dw_ref,
      cw_ref, dl_ref, sk_ref) = refs[:15]
     refs = refs[15:]
-    got_ref, edge_ref = both_ref.at[0:BLOCK, :], both_ref.at[BLOCK : BLOCK + 16, :]
+    got_ref, edge_ref = both_ref.at[0:BLOCK, :], both_ref.at[BLOCK : BLOCK + stage.edge, :]
     if last:
         dsc_ref, dm_ref, refs = refs[0], refs[1], refs[2:]
     if not first:
@@ -417,6 +421,9 @@
     if not last:
         bc_ref, ac_ref, dst_ref, refs = refs[0], refs[1], refs[2], refs[3:]
     prm, dz, nxt_dz, carry_ref, o_sc, lc_sc = refs[:6]
+    if last:
+        s_sc = refs[6]
+        s_sc[...] = jnp.zeros_like(s_sc)
     conv = width + maps if last else width
     own, late = place(plan)
     is_late = late.astype(F32)
@@ -424,7 +431,10 @@
     upper = (iota((BLOCK, BLOCK), 0) <= iota((BLOCK, BLOCK), 1)).astype(F32).astype(BF16)
     after_c = jnp.zeros((16, state), F32) if first else ac_old[...]
     for at, among, _ in stage.steps():
-        after_c = after_c + mm_over(split(edge_ref[:, at]), split(el_ref[blocks * BLOCK :, among]))
+        rows = edge_ref[:, at]
+        if not last:
+            rows = jnp.concatenate([jnp.zeros((PAD, tile), F32), rows[3:6], jnp.zeros((5, tile), F32)], axis=0)
+        after_c = after_c + mm_over(split(rows), split(el_ref[blocks * BLOCK :, among]))
     early = iota((PAD, LANES), 0) * 0 + late == 0
     for c in range(0, width, LANES):
         nxt_dz[:, c : c + LANES] = jnp.where(early, edge_ref[0:PAD, c : c + LANES], 0.0)
@@ -494,7 +504,9 @@
         if not first:
             d_step = d_step + dst_old[rows, :]
         if last:
-            o_sc[rows, width : width + LANES] = d_step.astype(BF16)
+            turned = d_step.T
+            for n in range(plan.spans):
+                s_sc[pl.ds(b * PAD, PAD), n * LANES : (n + 1) * LANES] = turned[n * PAD : (n + 1) * PAD]
             dz[0:BLOCK, width : width + state] = d_b * dm_ref[rows, :state]
             dz[0:BLOCK, width + state :] = d_c * dm_ref[rows, state:]
         else:
@@ -516,15 +528,17 @@
                 o_sc[rows, c : c + LANES] = grad.astype(BF16)
             else:
                 high, low = split(grad)
-                o_sc[rows, LANES + c : 2 * LANES + c] = high
-                o_sc[rows, LANES + maps + c : 2 * LANES + maps + c] = low
+                o_sc[rows, c : c + LANES] = high
+                o_sc[rows, maps + c : maps + c + LANES] = low
         nxt_dz[...] = dz[0:PAD, :]
         return carry
 
     each_block(blocks, body)
     for k in range(half):
-        rows = pl.ds(pl.multiple_of(jnp.bitwise_xor(own, k) * BLOCK, BLOCK), BLOCK)
-        outs[k][...] = o_sc[rows, :]
+        to = jnp.bitwise_xor(own, k)
+        outs[k][0:BLOCK, :] = o_sc[pl.ds(pl.multiple_of(to * BLOCK, BLOCK), BLOCK), :]
+        if last:
+            outs[k][BLOCK:, :] = s_sc[pl.ds(pl.multiple_of(to * PAD, PAD), PAD), :].astype(BF16)
 
 
 def owner_kernel(stage, *refs):
@@ -538,21 +552,24 @@
     pairs = []
     for k in range(half):
         start = pl.multiple_of(jnp.bitwise_xor(own, k) * plan.all + stage.start, LANES)
-        pairs.append((outs[k].at[:, pl.ds(0, width)], f_ref.at[:, pl.ds(start, width)]))
+        pairs.append((outs[k].at[pl.ds(0, BLOCK), pl.ds(0, width)], f_ref.at[:, pl.ds(start, width)]))
     copies = [pltpu.make_async_copy(source, target, refs[-1].at[n]) for n, (source, target) in enumerate(pairs)]
     for copy in copies:
         copy.start()
     if last:
         m_ref, s_ref = refs[1:3]
         total = jnp.zeros((BLOCK, maps), F32)
-        steps = jnp.zeros((BLOCK, LANES), F32)
+        steps = jnp.zeros((LANES, BLOCK), F32)
         for k in range(half):
             part, end = jnp.bitwise_xor(own, k), outs[k]
-            steps = steps + pltpu.roll(end[:, width : width + LANES].astype(F32), part * plan.heads, 1)
-            high, low = end[:, width + LANES : width + LANES + maps], end[:, width + LANES + maps :]
+            turned = end[BLOCK:, :].astype(F32)
+            mine = [turned[:, n * LANES : (n + 1) * LANES] for n in range(plan.spans)]
+            mine.append(jnp.zeros((LANES - plan.spans * PAD, LANES), F32))
+            steps = steps + pltpu.roll(jnp.concatenate(mine, axis=0), part * plan.heads, 0)
+            high, low = end[0:BLOCK, width : width + maps], end[0:BLOCK, width + maps :]
             total = total + (high.astype(F32) + low.astype(F32))
         m_ref[...] = total.astype(BF16)
-        s_ref[...] = steps.T[: s_ref.shape[0]].astype(BF16)
+        s_ref[...] = steps[: s_ref.shape[0]].astype(BF16)
     for copy in copies:
         copy.wait()
 
@@ -616,7 +633,7 @@
         first = stage.first
         args = [] if first else [gy, top, scores]
         args += [*(grads if first else ()), x_maps, cums, states, x_conv, dsilu, d_maps, steps, skip_gain]
-        outs = [near(tokens + BLOCK, width), struct(BLOCK + 16, width)]
+        outs = [near(tokens + BLOCK, width), struct(BLOCK + stage.edge, width)]
         if not stage.last:
             outs += [near(16, state + BLOCK)]
         if first:
@@ -636,13 +653,14 @@
     for stage, arrays in zip(stages, done):
         first, last = stage.first, stage.last
         conv = width + maps if last else width
-        out = width + LANES + 2 * maps if last else width
+        out = width + 2 * maps if last else width
         args = [*arrays, weight, decay_log, skip_gain]
-        outs = [struct(BLOCK, out, dtype=BF16)] * half
+        outs = [struct(BLOCK + (PAD if last else 0), out, dtype=BF16)] * half
         scratch = [small, pltpu.VMEM((BLOCK + PAD, conv), F32), pltpu.VMEM((PAD, conv), F32), small,
                    pltpu.VMEM((tokens, out), BF16), pltpu.VMEM((max(8, plan.blocks), LANES), F32)]
         if last:
             args += [scores, d_maps]
+            scratch += [pltpu.VMEM((PAD * plan.blocks, out), F32)]
         else:
             outs += [near(tokens, maps), near(16, state), near(tokens, LANES)]
         if not first:

time: 89.4 us -> 88 us (0.984)
  starting transfers between devices: 32.9 us -> 27.7 us
  waiting for transfers between devices: 24.5 us -> 28.3 us
    ppermute x11, starting transfers between devices: 20.8 us -> 15.6 us  [partner(): return lax.ppermute(array, 'ctx', [(i, i ^ k) for i in range(devices)])]
    ppermute x11, waiting for transfers between devices: 20.7 us -> 24.5 us  [partner(): return lax.ppermute(array, 'ctx', [(i, i ^ k) for i in range(devices)])]
  transfers between devices with their start and end apart: 19 -> 19, of which waited for: 6 -> 7; matrix products, arithmetic and copies ran while one was open for 0% -> 0% of each run, Pallas kernels for 30% -> 30%
where the time goes in v6:
time: 88 us; the launch traced here: 87.8 us
  Pallas kernels  30.7 us (35%)
  waiting for transfers between devices  28.3 us (32%)
  starting transfers between devices  27.7 us (31%)
  between operations  1.01 us (1%)
    ppermute x11, waiting for transfers between devices, partner(): return lax.ppermute(array, 'ctx', [(i, i ^ k) for i in range(devices)])  24.5 us
    ppermute x11, starting transfers between devices, partner(): return lax.ppermute(array, 'ctx', [(i, i ^ k) for i in range(devices)])  15.6 us
    ppermute x4, starting transfers between devices, shifted(): return lax.ppermute(array, ('pipe', 'ctx'), route)  9.43 us
    pallas_call x2, Pallas kernels, per_device(): result = call(final_kernel, stage, outs, scratch, work=5.8)(*args)  9.4 us
    pallas_call x2, Pallas kernels, per_device(): call(within_kernel, other, outs, work=2.0)(*args)  8.69 us
    pallas_call x1, Pallas kernels, per_device(): call(forward_kernel, plan, [near(tokens, plan.all), near(tokens, plan.all...  5.02 us
    ppermute x4, waiting for transfers between devices, shifted(): return lax.ppermute(array, ('pipe', 'ctx'), route)  3.85 us
    ppermute x4, starting transfers between devices, per_device(): lax.ppermute(e, 'ctx', [(half - 1, half + k)])  2.64 us
  transfers between devices with their start and end apart: 19, of which 7 were waited for; matrix products, arithmetic and copies ran while one was open for 0% of the time, Pallas kernels for 30%

profile of v6, /device:TPU:0, one launch (start us, length us, event | category | flops | bytes accessed | tf_op | source)
XLA Modules:
  0.0 87.8 jit_solution(16419517047917272373)
XLA Ops:
  0.6 1.7 %shard_map.113 = (bf16[128,1408]{1,0:T(8,128)(2,1)S(1)}, bf16[128,1408]{1,0:T(8,128)(2,1)S(1)}, bf16[128,1408]{1,0:T(8,128)(2,1)S(1)}, bf16[128,1408]{1,0:T(8,12...) custom-call(bf16[128,4096]{1,0:T(8,128)(2,1)} %bitcast.15, ...), custom_call_target="tpu_custom_call" | custom-call | flops 3449999872 | bytes 1048576 | tf_op jit(solution)/shard_map/pallas_call | solution.py:603
  2.3 3.0 %collective-permute-start.4 = (bf16[128,1408]{1,0:T(8,128)(2,1)S(1)}, bf16[128,1408]{1,0:T(8,128)(2,1)S(1)}, u32[]{:S(2)}, u32[]{:S(2)}) collective-permute-start(bf16[128,1408]{1,0:T(8,128)(2,1)S(1)} %get-tuple-element.54), channel_id=1, source_target_pairs={{0,1},{1,0},{2,3},{3,2},{4,5},{5,4},{6,7},{7,6},{8,9},{9,8},{10,11... | collective-permute-start | bytes 1081352 | tf_op jit(solution)/shard_map/ppermute | solution.py:586
  5.4 1.6 %collective-permute-start.5 = (bf16[128,1408]{1,0:T(8,128)(2,1)S(1)}, bf16[128,1408]{1,0:T(8,128)(2,1)S(1)}, u32[]{:S(2)}, u32[]{:S(2)}) collective-permute-start(bf16[128,1408]{1,0:T(8,128)(2,1)S(1)} %get-tuple-element.55), channel_id=1, source_target_pairs={{0,2},{1,3},{2,0},{3,1},{4,6},{5,7},{6,4},{7,5},{8,10},{9,11},{10,... | collective-permute-start | bytes 1081352 | tf_op jit(solution)/shard_map/ppermute | solution.py:586
  11.5 2.5 %collective-permute-start.1 = (bf16[128,1024]{1,0:T(8,128)(2,1)S(1)}, bf16[128,1024]{1,0:T(8,128)(2,1)S(1)}, u32[]{:S(2)}, u32[]{:S(2)}) collective-permute-start(bf16[128,1024]{1,0:T(8,128)(2,1)S(1)} %get-tuple-element.50), channel_id=1, source_target_pairs={{8,1},{9,0},{10,3},{11,2},{12,5},{13,4},{14,7},{15,6},{16,9},{17,8... | collective-permute-start | bytes 786440 | tf_op jit(solution)/shard_map/ppermute | solution.py:594
  14.0 6.4 %collective-permute-start.2 = (bf16[128,1024]{1,0:T(8,128)(2,1)S(1)}, bf16[128,1024]{1,0:T(8,128)(2,1)S(1)}, u32[]{:S(2)}, u32[]{:S(2)}) collective-permute-start(bf16[128,1024]{1,0:T(8,128)(2,1)S(1)} %get-tuple-element.51), channel_id=1, source_target_pairs={{8,2},{9,3},{10,0},{11,1},{12,6},{13,7},{14,4},{15,5},{16,10},{17,... | collective-permute-start | bytes 786440 | tf_op jit(solution)/shard_map/ppermute | solution.py:594
  20.4 6.0 %collective-permute-done.6.refs_3_ = bf16[128,1408]{1,0:T(8,128)(2,1)S(1)} collective-permute-done((bf16[128,1408]{1,0:T(8,128)(2,1)S(1)}, bf16[128,1408]{1,0:T(8,128)(2,1)S(1)}, u32[]{:S(2)}, u32[]{:S(2)}) %collective-permute-start.6) | collective-permute-done | bytes 360480 | tf_op jit(solution)/shard_map/ppermute | solution.py:586
  26.5 5.0 %shard_map.114 = (f32[512,1024]{1,0:T(8,128)S(1)}, f32[512,1024]{1,0:T(8,128)S(1)}, f32[640,1024]{1,0:T(8,128)S(1)}, f32[512,256]{1,0:T(8,128)S(1)}, f32[512,256...) custom-call(bf16[128,1408]{1,0:T(8,128)(2,1)S(1)} %get-tuple-element.53.refs_0_, ...), custom_call_target="tpu_custom_call" | custom-call | flops 5750000128 | bytes 1048576 | tf_op jit(solution)/shard_map/pallas_call | solution.py:624
  31.5 3.8 %collective-permute-done.3.refs_3_ = bf16[128,1024]{1,0:T(8,128)(2,1)S(1)} collective-permute-done((bf16[128,1024]{1,0:T(8,128)(2,1)S(1)}, bf16[128,1024]{1,0:T(8,128)(2,1)S(1)}, u32[]{:S(2)}, u32[]{:S(2)}) %collective-permute-start.3) | collective-permute-done | bytes 262176 | tf_op jit(solution)/shard_map/ppermute | solution.py:594
  36.5 1.9 %collective-permute-start.12 = (f32[136,512]{1,0:T(8,128)S(1)}, f32[136,512]{1,0:T(8,128)S(1)}, u32[]{:S(2)}, u32[]{:S(2)}) collective-permute-start(f32[136,512]{1,0:T(8,128)S(1)} %get-tuple-element.77), channel_id=1, source_target_pairs={{0,4},{1,5},{2,6},{3,7},{4,0},{5,1},{6,2},{7,3},{8,12},{9,13},{10,... | collective-permute-start | bytes 835592 | tf_op jit(solution)/shard_map/ppermute | solution.py:586
  38.4 4.3 %shard_map.116 = (f32[512,512]{1,0:T(8,128)S(1)}, f32[512,512]{1,0:T(8,128)S(1)}, f32[512,128]{1,0:T(8,128)S(1)}) custom-call(f32[512,1024]{1,0:T(8,128)S(1)} %get-tuple-element.64.refs_7_.refs_0_.refs_6_.refs_1_, f32[512,256]{1,0:T(8,128)S(1)} %get-tuple-element.61.refs_4_.refs_1_.refs_3_.refs_2_, ...), custom_call_target="tpu_custom_call" | custom-call | flops 2300000000 | bytes 1048576 | tf_op jit(solution)/shard_map/pallas_call | solution.py:648
  42.8 4.3 %shard_map.117 = (f32[512,512]{1,0:T(8,128)S(1)}, f32[512,512]{1,0:T(8,128)S(1)}, f32[512,128]{1,0:T(8,128)S(1)}) custom-call(f32[512,1024]{1,0:T(8,128)S(1)} %get-tuple-element.64.refs_7_.refs_0_.refs_6_.refs_1_, f32[512,256]{1,0:T(8,128)S(1)} %get-tuple-element.61.refs_4_.refs_1_.refs_3_.refs_2_, ...), custom_call_target="tpu_custom_call" | custom-call | flops 2300000000 | bytes 1048576 | tf_op jit(solution)/shard_map/pallas_call | solution.py:648
  48.4 2.0 %collective-permute-start.11 = (f32[144,512]{1,0:T(8,128)S(1)}, f32[144,512]{1,0:T(8,128)S(1)}, u32[]{:S(2)}, u32[]{:S(2)}) collective-permute-start(f32[144,512]{1,0:T(8,128)S(1)} %get-tuple-element.72), channel_id=1, source_target_pairs={{0,4},{1,5},{2,6},{3,7},{4,0},{5,1},{6,2},{7,3},{8,12},{9,13},{10,... | collective-permute-start | bytes 884744 | tf_op jit(solution)/shard_map/ppermute | solution.py:586
  50.4 1.4 %collective-permute-done.12.refs_0_ = f32[136,512]{1,0:T(8,128)S(1)} collective-permute-done((f32[136,512]{1,0:T(8,128)S(1)}, f32[136,512]{1,0:T(8,128)S(1)}, u32[]{:S(2)}, u32[]{:S(2)}) %collective-permute-start.12) | collective-permute-done | bytes 278560 | tf_op jit(solution)/shard_map/ppermute | solution.py:586
  51.8 4.5 %shard_map.119 = (bf16[128,512]{1,0:T(8,128)(2,1)S(1)}, bf16[128,512]{1,0:T(8,128)(2,1)S(1)}, bf16[128,512]{1,0:T(8,128)(2,1)S(1)}, bf16[128,512]{1,0:T(8,128)(2...) custom-call(f32[136,512]{1,0:T(8,128)S(1)} %collective-permute-done.12.refs_0_, ...), custom_call_target="tpu_custom_call" | custom-call | flops 6670000128 | bytes 1048576 | tf_op jit(solution)/shard_map/pallas_call | solution.py:668
  56.3 1.8 %collective-permute-start.16 = (bf16[128,512]{1,0:T(8,128)(2,1)S(1)}, bf16[128,512]{1,0:T(8,128)(2,1)S(1)}, u32[]{:S(2)}, u32[]{:S(2)}) collective-permute-start(bf16[128,512]{1,0:T(8,128)(2,1)S(1)} %get-tuple-element.89), channel_id=1, source_target_pairs={{0,1},{1,0},{2,3},{3,2},{4,5},{5,4},{6,7},{7,6},{8,9},{9,8},{10,11... | collective-permute-start | bytes 393224 | tf_op jit(solution)/shard_map/ppermute | solution.py:586
  58.1 1.7 %collective-permute-start.18 = (bf16[128,512]{1,0:T(8,128)(2,1)S(1)}, bf16[128,512]{1,0:T(8,128)(2,1)S(1)}, u32[]{:S(2)}, u32[]{:S(2)}) collective-permute-start(bf16[128,512]{1,0:T(8,128)(2,1)S(1)} %get-tuple-element.91), channel_id=1, source_target_pairs={{0,3},{1,2},{2,1},{3,0},{4,7},{5,6},{6,5},{7,4},{8,11},{9,10},{10,... | collective-permute-start | bytes 393224 | tf_op jit(solution)/shard_map/ppermute | solution.py:586
  59.8 5.6 %collective-permute-done.11.refs_0_ = f32[144,512]{1,0:T(8,128)S(1)} collective-permute-done((f32[144,512]{1,0:T(8,128)S(1)}, f32[144,512]{1,0:T(8,128)S(1)}, u32[]{:S(2)}, u32[]{:S(2)}) %collective-permute-start.11) | collective-permute-done | bytes 294944 | tf_op jit(solution)/shard_map/ppermute | solution.py:586
  65.4 4.9 %shard_map.120 = (bf16[136,1024]{1,0:T(8,128)(2,1)S(1)}, bf16[136,1024]{1,0:T(8,128)(2,1)S(1)}, bf16[136,1024]{1,0:T(8,128)(2,1)S(1)}, bf16[136,1024]{1,0:T(8,128)(2,1)S(1)}) custom-call(f32[144,512]{1,0:T(8,128)S(1)} %collective-permute-done.11.refs_0_, f32[512,1024]{1,0:T(8,128)S(1)} %get-tuple-element.64.refs_7_.refs_0_.refs_6_.refs_1_, ...), custom_call_target="tpu_custom_call" | custom-call | flops 6670000128 | bytes 1048576 | tf_op jit(solution)/shard_map/pallas_call | solution.py:668
  70.3 1.5 %collective-permute-start.13 = (bf16[136,1024]{1,0:T(8,128)(2,1)S(1)}, bf16[136,1024]{1,0:T(8,128)(2,1)S(1)}, u32[]{:S(2)}, u32[]{:S(2)}) collective-permute-start(bf16[136,1024]{1,0:T(8,128)(2,1)S(1)} %get-tuple-element.85), channel_id=1, source_target_pairs={{0,1},{1,0},{2,3},{3,2},{4,5},{5,4},{6,7},{7,6},{8,9},{9,8},{10,11... | collective-permute-start | bytes 835592 | tf_op jit(solution)/shard_map/ppermute | solution.py:586
  71.8 2.0 %collective-permute-start.15 = (bf16[136,1024]{1,0:T(8,128)(2,1)S(1)}, bf16[136,1024]{1,0:T(8,128)(2,1)S(1)}, u32[]{:S(2)}, u32[]{:S(2)}) collective-permute-start(bf16[136,1024]{1,0:T(8,128)(2,1)S(1)} %get-tuple-element.87), channel_id=1, source_target_pairs={{0,3},{1,2},{2,1},{3,0},{4,7},{5,6},{6,5},{7,4},{8,11},{9,10},{10,... | collective-permute-start | bytes 835592 | tf_op jit(solution)/shard_map/ppermute | solution.py:586
  74.7 4.3 %collective-permute-done.13.refs_1_ = bf16[136,1024]{1,0:T(8,128)(2,1)S(1)} collective-permute-done((bf16[136,1024]{1,0:T(8,128)(2,1)S(1)}, bf16[136,1024]{1,0:T(8,128)(2,1)S(1)}, u32[]{:S(2)}, u32[]{:S(2)}) %collective-permute-start.13) | collective-permute-done | bytes 278560 | tf_op jit(solution)/shard_map/ppermute | solution.py:586
  79.0 2.4 %collective-permute-done.14.refs_2_ = bf16[136,1024]{1,0:T(8,128)(2,1)S(1)} collective-permute-done((bf16[136,1024]{1,0:T(8,128)(2,1)S(1)}, bf16[136,1024]{1,0:T(8,128)(2,1)S(1)}, u32[]{:S(2)}, u32[]{:S(2)}) %collective-permute-start.14) | collective-permute-done | bytes 278560 | tf_op jit(solution)/shard_map/ppermute | solution.py:586
  81.4 4.8 %collective-permute-done.15.refs_3_ = bf16[136,1024]{1,0:T(8,128)(2,1)S(1)} collective-permute-done((bf16[136,1024]{1,0:T(8,128)(2,1)S(1)}, bf16[136,1024]{1,0:T(8,128)(2,1)S(1)}, u32[]{:S(2)}, u32[]{:S(2)}) %collective-permute-start.15) | collective-permute-done | bytes 278560 | tf_op jit(solution)/shard_map/ppermute | solution.py:586
  86.2 1.5 %shard_map.122 = (bf16[128,4096]{1,0:T(8,128)(2,1)}, bf16[128,256]{1,0:T(8,128)(2,1)}, bf16[64,128]{1,0:T(8,128)(2,1)}) custom-call(bf16[136,1024]{1,0:T(8,128)(2,1)S(1)} %get-tuple-element.84.refs_0_, bf16[136,1024]{1,0:T(8,128)(2,1)S(1)} %collective-permute-done.13.refs_1_, ...), custom_call_target="tpu_custom_call", output_to_operand_aliasing={{0}: (4, {})} | custom-call | flops 2300000000 | bytes 1048576 | tf_op jit(solution)/shard_map/pallas_call | solution.py:677
  (35 shorter events, 7.7 us)
Async XLA Ops:
  2.3 11.6 %collective-permute-start.4 = (bf16[128,1408]{1,0:T(8,128)(2,1)S(1)}, bf16[128,1408]{1,0:T(8,128)(2,1)S(1)}, u32[]{:S(2)}, u32[]{:S(2)}) collective-permute-start(bf16[128,1408]{1,0:T(8,128)(2,1)S(1)} %get-tuple-element.54), channel_id=1, source_target_pairs={{0,1},{1,0},{2,3},{3,2},{4,5},{5,4},{6,7},{7,6},{8,9},{9,8},{10,11... | collective-permute-start | bytes 1081352 | tf_op jit(solution)/shard_map/ppermute | solution.py:586
  5.4 15.0 %collective-permute-start.5 = (bf16[128,1408]{1,0:T(8,128)(2,1)S(1)}, bf16[128,1408]{1,0:T(8,128)(2,1)S(1)}, u32[]{:S(2)}, u32[]{:S(2)}) collective-permute-start(bf16[128,1408]{1,0:T(8,128)(2,1)S(1)} %get-tuple-element.55), channel_id=1, source_target_pairs={{0,2},{1,3},{2,0},{3,1},{4,6},{5,7},{6,4},{7,5},{8,10},{9,11},{10,... | collective-permute-start | bytes 1081352 | tf_op jit(solution)/shard_map/ppermute | solution.py:586
  6.9 19.5 %collective-permute-start.6 = (bf16[128,1408]{1,0:T(8,128)(2,1)S(1)}, bf16[128,1408]{1,0:T(8,128)(2,1)S(1)}, u32[]{:S(2)}, u32[]{:S(2)}) collective-permute-start(bf16[128,1408]{1,0:T(8,128)(2,1)S(1)} %get-tuple-element.56), channel_id=1, source_target_pairs={{0,3},{1,2},{2,1},{3,0},{4,7},{5,6},{6,5},{7,4},{8,11},{9,10},{10,... | collective-permute-start | bytes 1081352 | tf_op jit(solution)/shard_map/ppermute | solution.py:586
  6.9 1.3 %collective-permute-start.7 = (bf16[16,1280]{1,0:T(8,128)(2,1)S(1)}, bf16[16,1280]{1,0:T(8,128)(2,1)S(1)}, u32[]{:S(2)}, u32[]{:S(2)}) collective-permute-start(bf16[16,1280]{1,0:T(8,128)(2,1)S(1)} %get-tuple-element.57), channel_id=1, source_target_pairs={{3,4},{11,12},{19,20},{27,28}} | collective-permute-start | bytes 122888 | tf_op jit(solution)/shard_map/ppermute | solution.py:620
  7.6 1.4 %collective-permute-start.8 = (bf16[16,1280]{1,0:T(8,128)(2,1)S(1)}, bf16[16,1280]{1,0:T(8,128)(2,1)S(1)}, u32[]{:S(2)}, u32[]{:S(2)}) collective-permute-start(bf16[16,1280]{1,0:T(8,128)(2,1)S(1)} %get-tuple-element.58), channel_id=1, source_target_pairs={{3,5},{11,13},{19,21},{27,29}} | collective-permute-start | bytes 122888 | tf_op jit(solution)/shard_map/ppermute | solution.py:620
  8.3 2.7 %collective-permute-start.9 = (bf16[16,1280]{1,0:T(8,128)(2,1)S(1)}, bf16[16,1280]{1,0:T(8,128)(2,1)S(1)}, u32[]{:S(2)}, u32[]{:S(2)}) collective-permute-start(bf16[16,1280]{1,0:T(8,128)(2,1)S(1)} %get-tuple-element.59), channel_id=1, source_target_pairs={{3,6},{11,14},{19,22},{27,30}} | collective-permute-start | bytes 122888 | tf_op jit(solution)/shard_map/ppermute | solution.py:620
  9.0 2.5 %collective-permute-start.10 = (bf16[16,1280]{1,0:T(8,128)(2,1)S(1)}, bf16[16,1280]{1,0:T(8,128)(2,1)S(1)}, u32[]{:S(2)}, u32[]{:S(2)}) collective-permute-start(bf16[16,1280]{1,0:T(8,128)(2,1)S(1)} %get-tuple-element.60), channel_id=1, source_target_pairs={{3,7},{11,15},{19,23},{27,31}} | collective-permute-start | bytes 122888 | tf_op jit(solution)/shard_map/ppermute | solution.py:620
  9.6 16.8 %copy-start.1 = (f32[1,4,4352]{2,1,0:T(4,128)S(1)}, f32[1,4,4352]{2,1,0:T(4,128)}, u32[]{:S(2)}) copy-start(f32[1,4,4352]{2,1,0:T(4,128)} %param.12) | copy-start | bytes 208900
  9.7 16.8 %copy-start.2 = (f32[1,4352]{1,0:T(1,128)S(1)}, f32[1,4352]{1,0:T(1,128)}, u32[]{:S(2)}) copy-start(f32[1,4352]{1,0:T(1,128)} %refs_9_.1) | copy-start | bytes 52228
  9.7 16.8 %copy-start.3 = (f32[1,64]{1,0:T(1,128)S(1)}, f32[1,64]{1,0:T(1,128)}, u32[]{:S(2)}) copy-start(f32[1,64]{1,0:T(1,128)} %refs_11_.2) | copy-start | bytes 772
  9.7 16.8 %copy-start.4 = (f32[1,64]{1,0:T(1,128)S(1)}, f32[1,64]{1,0:T(1,128)}, u32[]{:S(2)}) copy-start(f32[1,64]{1,0:T(1,128)} %refs_13_.3) | copy-start | bytes 772
  11.0 20.5 %collective-permute-start = (bf16[128,1024]{1,0:T(8,128)(2,1)S(1)}, bf16[128,1024]{1,0:T(8,128)(2,1)S(1)}, u32[]{:S(2)}, u32[]{:S(2)}) collective-permute-start(bf16[128,1024]{1,0:T(8,128)(2,1)S(1)} %get-tuple-element.49), channel_id=1, source_target_pairs={{8,0},{9,1},{10,2},{11,3},{12,4},{13,5},{14,6},{15,7},{16,8},{17,9... | collective-permute-start | bytes 786440 | tf_op jit(solution)/shard_map/ppermute | solution.py:594
  11.5 20.0 %collective-permute-start.1 = (bf16[128,1024]{1,0:T(8,128)(2,1)S(1)}, bf16[128,1024]{1,0:T(8,128)(2,1)S(1)}, u32[]{:S(2)}, u32[]{:S(2)}) collective-permute-start(bf16[128,1024]{1,0:T(8,128)(2,1)S(1)} %get-tuple-element.50), channel_id=1, source_target_pairs={{8,1},{9,0},{10,3},{11,2},{12,5},{13,4},{14,7},{15,6},{16,9},{17,8... | collective-permute-start | bytes 786440 | tf_op jit(solution)/shard_map/ppermute | solution.py:594
  14.0 17.6 %collective-permute-start.2 = (bf16[128,1024]{1,0:T(8,128)(2,1)S(1)}, bf16[128,1024]{1,0:T(8,128)(2,1)S(1)}, u32[]{:S(2)}, u32[]{:S(2)}) collective-permute-start(bf16[128,1024]{1,0:T(8,128)(2,1)S(1)} %get-tuple-element.51), channel_id=1, source_target_pairs={{8,2},{9,3},{10,0},{11,1},{12,6},{13,7},{14,4},{15,5},{16,10},{17,... | collective-permute-start | bytes 786440 | tf_op jit(solution)/shard_map/ppermute | solution.py:594
  20.4 15.0 %collective-permute-start.3 = (bf16[128,1024]{1,0:T(8,128)(2,1)S(1)}, bf16[128,1024]{1,0:T(8,128)(2,1)S(1)}, u32[]{:S(2)}, u32[]{:S(2)}) collective-permute-start(bf16[128,1024]{1,0:T(8,128)(2,1)S(1)} %get-tuple-element.52), channel_id=1, source_target_pairs={{8,3},{9,2},{10,1},{11,0},{12,7},{13,6},{14,5},{15,4},{16,11},{17,... | collective-permute-start | bytes 786440 | tf_op jit(solution)/shard_map/ppermute | solution.py:594
  26.5 8.9 %copy-start = (f32[1,64]{1,0:T(1,128)S(1)}, f32[1,64]{1,0:T(1,128)}, u32[]{:S(2)}) copy-start(f32[1,64]{1,0:T(1,128)} %refs_14_.3) | copy-start | bytes 772
  36.5 15.3 %collective-permute-start.12 = (f32[136,512]{1,0:T(8,128)S(1)}, f32[136,512]{1,0:T(8,128)S(1)}, u32[]{:S(2)}, u32[]{:S(2)}) collective-permute-start(f32[136,512]{1,0:T(8,128)S(1)} %get-tuple-element.77), channel_id=1, source_target_pairs={{0,4},{1,5},{2,6},{3,7},{4,0},{5,1},{6,2},{7,3},{8,12},{9,13},{10,... | collective-permute-start | bytes 835592 | tf_op jit(solution)/shard_map/ppermute | solution.py:586
  48.4 17.0 %collective-permute-start.11 = (f32[144,512]{1,0:T(8,128)S(1)}, f32[144,512]{1,0:T(8,128)S(1)}, u32[]{:S(2)}, u32[]{:S(2)}) collective-permute-start(f32[144,512]{1,0:T(8,128)S(1)} %get-tuple-element.72), channel_id=1, source_target_pairs={{0,4},{1,5},{2,6},{3,7},{4,0},{5,1},{6,2},{7,3},{8,12},{9,13},{10,... | collective-permute-start | bytes 884744 | tf_op jit(solution)/shard_map/ppermute | solution.py:586
  56.3 15.5 %collective-permute-start.16 = (bf16[128,512]{1,0:T(8,128)(2,1)S(1)}, bf16[128,512]{1,0:T(8,128)(2,1)S(1)}, u32[]{:S(2)}, u32[]{:S(2)}) collective-permute-start(bf16[128,512]{1,0:T(8,128)(2,1)S(1)} %get-tuple-element.89), channel_id=1, source_target_pairs={{0,1},{1,0},{2,3},{3,2},{4,5},{5,4},{6,7},{7,6},{8,9},{9,8},{10,11... | collective-permute-start | bytes 393224 | tf_op jit(solution)/shard_map/ppermute | solution.py:586
  58.1 15.7 %collective-permute-start.17 = (bf16[128,512]{1,0:T(8,128)(2,1)S(1)}, bf16[128,512]{1,0:T(8,128)(2,1)S(1)}, u32[]{:S(2)}, u32[]{:S(2)}) collective-permute-start(bf16[128,512]{1,0:T(8,128)(2,1)S(1)} %get-tuple-element.90), channel_id=1, source_target_pairs={{0,2},{1,3},{2,0},{3,1},{4,6},{5,7},{6,4},{7,5},{8,10},{9,11},{10,... | collective-permute-start | bytes 393224 | tf_op jit(solution)/shard_map/ppermute | solution.py:586
  58.1 15.7 %collective-permute-start.18 = (bf16[128,512]{1,0:T(8,128)(2,1)S(1)}, bf16[128,512]{1,0:T(8,128)(2,1)S(1)}, u32[]{:S(2)}, u32[]{:S(2)}) collective-permute-start(bf16[128,512]{1,0:T(8,128)(2,1)S(1)} %get-tuple-element.91), channel_id=1, source_target_pairs={{0,3},{1,2},{2,1},{3,0},{4,7},{5,6},{6,5},{7,4},{8,11},{9,10},{10,... | collective-permute-start | bytes 393224 | tf_op jit(solution)/shard_map/ppermute | solution.py:586
  70.3 8.7 %collective-permute-start.13 = (bf16[136,1024]{1,0:T(8,128)(2,1)S(1)}, bf16[136,1024]{1,0:T(8,128)(2,1)S(1)}, u32[]{:S(2)}, u32[]{:S(2)}) collective-permute-start(bf16[136,1024]{1,0:T(8,128)(2,1)S(1)} %get-tuple-element.85), channel_id=1, source_target_pairs={{0,1},{1,0},{2,3},{3,2},{4,5},{5,4},{6,7},{7,6},{8,9},{9,8},{10,11... | collective-permute-start | bytes 835592 | tf_op jit(solution)/shard_map/ppermute | solution.py:586
  71.8 9.6 %collective-permute-start.14 = (bf16[136,1024]{1,0:T(8,128)(2,1)S(1)}, bf16[136,1024]{1,0:T(8,128)(2,1)S(1)}, u32[]{:S(2)}, u32[]{:S(2)}) collective-permute-start(bf16[136,1024]{1,0:T(8,128)(2,1)S(1)} %get-tuple-element.86), channel_id=1, source_target_pairs={{0,2},{1,3},{2,0},{3,1},{4,6},{5,7},{6,4},{7,5},{8,10},{9,11},{10,... | collective-permute-start | bytes 835592 | tf_op jit(solution)/shard_map/ppermute | solution.py:586
  71.8 14.3 %collective-permute-start.15 = (bf16[136,1024]{1,0:T(8,128)(2,1)S(1)}, bf16[136,1024]{1,0:T(8,128)(2,1)S(1)}, u32[]{:S(2)}, u32[]{:S(2)}) collective-permute-start(bf16[136,1024]{1,0:T(8,128)(2,1)S(1)} %get-tuple-element.87), channel_id=1, source_target_pairs={{0,3},{1,2},{2,1},{3,0},{4,7},{5,6},{6,5},{7,4},{8,11},{9,10},{10,... | collective-permute-start | bytes 835592 | tf_op jit(solution)/shard_map/ppermute | solution.py:586

commit v7 on v6

--- a/solution.py
+++ b/solution.py
@@ -93,6 +93,11 @@
         self.blocks = self.half
         self.spans = -(-self.heads // PAD)
         self.tokens = self.half * BLOCK
+        self.lots = (self.all + self.maps) // LANES
+        self.below = PAD * -(-(heads // PAD) // self.lots)
+
+    def lot(self, n):
+        return slice(BLOCK + n // self.lots * PAD, BLOCK + (n // self.lots + 1) * PAD), n % self.lots * LANES
 
 
 class Stage:
@@ -169,10 +174,11 @@
     pairs = []
     for k in range(plan.half):
         start = pl.multiple_of(jnp.bitwise_xor(own, k) * whole, LANES)
-        pairs.append((f_ref.at[:, pl.ds(start, whole)], pays[k].at[:, pl.ds(0, whole)]))
-        pairs.append((m_ref, pays[k].at[:, pl.ds(whole, plan.maps)]))
-        for row in range(0, BLOCK, heads):
-            pairs.append((s_ref, pays[k].at[pl.ds(row, heads), pl.ds(whole + plan.maps, LANES)]))
+        pairs.append((f_ref.at[:, pl.ds(start, whole)], pays[k].at[pl.ds(0, BLOCK), pl.ds(0, whole)]))
+        pairs.append((m_ref, pays[k].at[pl.ds(0, BLOCK), pl.ds(whole, plan.maps)]))
+        for n in range(heads // PAD):
+            rows, lane = plan.lot(n)
+            pairs.append((s_ref.at[pl.ds(n * PAD, PAD), :], pays[k].at[rows, pl.ds(lane, LANES)]))
         tail = pl.ds(BLOCK - 16, 16)
         pairs.append((f_ref.at[tail, pl.ds(k * whole, whole)], edges[k].at[:, pl.ds(0, whole)]))
         pairs.append((m_ref.at[tail, :], edges[k].at[:, pl.ds(whole, plan.maps)]))
@@ -203,8 +209,10 @@
     sraw[...] = jnp.zeros_like(sraw)
     for k in range(half):
         block = jnp.bitwise_xor(own, k) * BLOCK
-        raw[pl.ds(pl.multiple_of(block + PAD, 8), BLOCK), :] = pays[k][:, :conv].astype(F32)
-        sraw[pl.ds(pl.multiple_of(block, 8), BLOCK), 0:heads] = pays[k][0:heads, conv:].astype(F32).T
+        raw[pl.ds(pl.multiple_of(block + PAD, 8), BLOCK), :] = pays[k][0:BLOCK, :].astype(F32)
+        lots = [plan.lot(n) for n in range(heads // PAD)]
+        turned = jnp.concatenate([pays[k][rows, lane : lane + LANES].astype(F32) for rows, lane in lots], axis=0)
+        sraw[pl.ds(pl.multiple_of(block, 8), BLOCK), 0:heads] = turned.T
     rates, offsets = head_rows(plan, prm, [-jnp.exp(dl_ref[...]), sb_ref[...]], own)
     shift = lax.rem(LANES - own * plan.heads, LANES)
     lower = (iota((BLOCK, BLOCK), 0) >= iota((BLOCK, BLOCK), 1)).astype(F32)
@@ -603,8 +611,8 @@
     packed = call(
         pack_kernel,
         plan,
-        [struct(BLOCK, conv + LANES, dtype=BF16)] * half + [struct(16, conv, dtype=BF16)] * half,
-        [pltpu.SemaphoreType.DMA((half * (4 + BLOCK // heads),))],
+        [struct(BLOCK + plan.below, conv, dtype=BF16)] * half + [struct(16, conv, dtype=BF16)] * half,
+        [pltpu.SemaphoreType.DMA((half * (4 + heads // PAD),))],
         work=3.0,
         in_specs=[far] * 3,
     )(hold(features[0]), hold(state_maps[0]), hold(step_raw[0].T))

time: 88 us -> 88.1 us (level)
  no operation moved by 1% of the time
where the time goes in v7:
time: 88.1 us; the launch traced here: 87.9 us
  Pallas kernels  31 us (35%)
  starting transfers between devices  28.4 us (32%)
  waiting for transfers between devices  27.5 us (31%)
  between operations  1.01 us (1%)
    ppermute x11, waiting for transfers between devices, partner(): return lax.ppermute(array, 'ctx', [(i, i ^ k) for i in range(devices)])  23.6 us
    ppermute x11, starting transfers between devices, partner(): return lax.ppermute(array, 'ctx', [(i, i ^ k) for i in range(devices)])  16.3 us
    ppermute x4, starting transfers between devices, shifted(): return lax.ppermute(array, ('pipe', 'ctx'), route)  9.44 us
    pallas_call x2, Pallas kernels, per_device(): result = call(final_kernel, stage, outs, scratch, work=5.8)(*args)  9.39 us
    pallas_call x2, Pallas kernels, per_device(): call(within_kernel, other, outs, work=2.0)(*args)  8.69 us
    pallas_call x1, Pallas kernels, per_device(): call(forward_kernel, plan, [near(tokens, plan.all), near(tokens, plan.all...  5.02 us
    ppermute x4, waiting for transfers between devices, shifted(): return lax.ppermute(array, ('pipe', 'ctx'), route)  3.85 us
    ppermute x4, starting transfers between devices, per_device(): lax.ppermute(e, 'ctx', [(half - 1, half + k)])  2.64 us
  transfers between devices with their start and end apart: 19, of which 7 were waited for; matrix products, arithmetic and copies ran while one was open for 0% of the time, Pallas kernels for 30%

profile of v7, /device:TPU:0, one launch (start us, length us, event | category | flops | bytes accessed | tf_op | source)
XLA Modules:
  0.0 87.9 jit_solution(67213787216389518)
XLA Ops:
  0.6 2.0 %shard_map.113 = (bf16[136,1280]{1,0:T(8,128)(2,1)S(1)}, bf16[136,1280]{1,0:T(8,128)(2,1)S(1)}, bf16[136,1280]{1,0:T(8,128)(2,1)S(1)}, bf16[136,1280]{1,0:T(8,12...) custom-call(bf16[128,4096]{1,0:T(8,128)(2,1)} %bitcast.15, ...), custom_call_target="tpu_custom_call" | custom-call | flops 3449999872 | bytes 1048576 | tf_op jit(solution)/shard_map/pallas_call | solution.py:611
  2.6 3.0 %collective-permute-start.4 = (bf16[136,1280]{1,0:T(8,128)(2,1)S(1)}, bf16[136,1280]{1,0:T(8,128)(2,1)S(1)}, u32[]{:S(2)}, u32[]{:S(2)}) collective-permute-start(bf16[136,1280]{1,0:T(8,128)(2,1)S(1)} %get-tuple-element.54), channel_id=1, source_target_pairs={{0,1},{1,0},{2,3},{3,2},{4,5},{5,4},{6,7},{7,6},{8,9},{9,8},{10,11... | collective-permute-start | bytes 1044488 | tf_op jit(solution)/shard_map/ppermute | solution.py:594
  5.6 1.6 %collective-permute-start.5 = (bf16[136,1280]{1,0:T(8,128)(2,1)S(1)}, bf16[136,1280]{1,0:T(8,128)(2,1)S(1)}, u32[]{:S(2)}, u32[]{:S(2)}) collective-permute-start(bf16[136,1280]{1,0:T(8,128)(2,1)S(1)} %get-tuple-element.55), channel_id=1, source_target_pairs={{0,2},{1,3},{2,0},{3,1},{4,6},{5,7},{6,4},{7,5},{8,10},{9,11},{10,... | collective-permute-start | bytes 1044488 | tf_op jit(solution)/shard_map/ppermute | solution.py:594
  9.9 1.3 %shard_map.112 = (bf16[128,1024]{1,0:T(8,128)(2,1)S(1)}, bf16[128,1024]{1,0:T(8,128)(2,1)S(1)}, bf16[128,1024]{1,0:T(8,128)(2,1)S(1)}, bf16[128,1024]{1,0:T(8,128)(2,1)S(1)}) custom-call(bf16[128,4096]{1,0:T(8,128)(2,1)} %bitcast.16), custom_call_target="tpu_custom_call" | custom-call | flops 2529999872 | bytes 1048576 | tf_op jit(solution)/shard_map/pallas_call | solution.py:619
  11.8 2.5 %collective-permute-start.1 = (bf16[128,1024]{1,0:T(8,128)(2,1)S(1)}, bf16[128,1024]{1,0:T(8,128)(2,1)S(1)}, u32[]{:S(2)}, u32[]{:S(2)}) collective-permute-start(bf16[128,1024]{1,0:T(8,128)(2,1)S(1)} %get-tuple-element.50), channel_id=1, source_target_pairs={{8,1},{9,0},{10,3},{11,2},{12,5},{13,4},{14,7},{15,6},{16,9},{17,8... | collective-permute-start | bytes 786440 | tf_op jit(solution)/shard_map/ppermute | solution.py:602
  14.2 6.4 %collective-permute-start.2 = (bf16[128,1024]{1,0:T(8,128)(2,1)S(1)}, bf16[128,1024]{1,0:T(8,128)(2,1)S(1)}, u32[]{:S(2)}, u32[]{:S(2)}) collective-permute-start(bf16[128,1024]{1,0:T(8,128)(2,1)S(1)} %get-tuple-element.51), channel_id=1, source_target_pairs={{8,2},{9,3},{10,0},{11,1},{12,6},{13,7},{14,4},{15,5},{16,10},{17,... | collective-permute-start | bytes 786440 | tf_op jit(solution)/shard_map/ppermute | solution.py:602
  20.7 5.0 %collective-permute-done.6.refs_3_ = bf16[136,1280]{1,0:T(8,128)(2,1)S(1)} collective-permute-done((bf16[136,1280]{1,0:T(8,128)(2,1)S(1)}, bf16[136,1280]{1,0:T(8,128)(2,1)S(1)}, u32[]{:S(2)}, u32[]{:S(2)}) %collective-permute-start.6) | collective-permute-done | bytes 348192 | tf_op jit(solution)/shard_map/ppermute | solution.py:594
  25.7 5.0 %shard_map.114 = (f32[512,1024]{1,0:T(8,128)S(1)}, f32[512,1024]{1,0:T(8,128)S(1)}, f32[640,1024]{1,0:T(8,128)S(1)}, f32[512,256]{1,0:T(8,128)S(1)}, f32[512,256...) custom-call(bf16[136,1280]{1,0:T(8,128)(2,1)S(1)} %get-tuple-element.53.refs_0_, ...), custom_call_target="tpu_custom_call" | custom-call | flops 5750000128 | bytes 1048576 | tf_op jit(solution)/shard_map/pallas_call | solution.py:632
  30.7 3.8 %collective-permute-done.3.refs_3_ = bf16[128,1024]{1,0:T(8,128)(2,1)S(1)} collective-permute-done((bf16[128,1024]{1,0:T(8,128)(2,1)S(1)}, bf16[128,1024]{1,0:T(8,128)(2,1)S(1)}, u32[]{:S(2)}, u32[]{:S(2)}) %collective-permute-start.3) | collective-permute-done | bytes 262176 | tf_op jit(solution)/shard_map/ppermute | solution.py:602
  35.7 2.7 %collective-permute-start.12 = (f32[136,512]{1,0:T(8,128)S(1)}, f32[136,512]{1,0:T(8,128)S(1)}, u32[]{:S(2)}, u32[]{:S(2)}) collective-permute-start(f32[136,512]{1,0:T(8,128)S(1)} %get-tuple-element.77), channel_id=1, source_target_pairs={{0,4},{1,5},{2,6},{3,7},{4,0},{5,1},{6,2},{7,3},{8,12},{9,13},{10,... | collective-permute-start | bytes 835592 | tf_op jit(solution)/shard_map/ppermute | solution.py:594
  38.4 4.3 %shard_map.116 = (f32[512,512]{1,0:T(8,128)S(1)}, f32[512,512]{1,0:T(8,128)S(1)}, f32[512,128]{1,0:T(8,128)S(1)}) custom-call(f32[512,1024]{1,0:T(8,128)S(1)} %get-tuple-element.64.refs_7_.refs_0_.refs_6_.refs_1_, f32[512,256]{1,0:T(8,128)S(1)} %get-tuple-element.61.refs_4_.refs_1_.refs_3_.refs_2_, ...), custom_call_target="tpu_custom_call" | custom-call | flops 2300000000 | bytes 1048576 | tf_op jit(solution)/shard_map/pallas_call | solution.py:656
  42.7 4.3 %shard_map.117 = (f32[512,512]{1,0:T(8,128)S(1)}, f32[512,512]{1,0:T(8,128)S(1)}, f32[512,128]{1,0:T(8,128)S(1)}) custom-call(f32[512,1024]{1,0:T(8,128)S(1)} %get-tuple-element.64.refs_7_.refs_0_.refs_6_.refs_1_, f32[512,256]{1,0:T(8,128)S(1)} %get-tuple-element.61.refs_4_.refs_1_.refs_3_.refs_2_, ...), custom_call_target="tpu_custom_call" | custom-call | flops 2300000000 | bytes 1048576 | tf_op jit(solution)/shard_map/pallas_call | solution.py:656
  47.1 1.3 %shard_map.118 = (f32[640,512]{1,0:T(8,128)S(1)}, f32[144,512]{1,0:T(8,128)S(1)}) custom-call(bf16[512,1024]{1,0:T(8,128)(2,1)S(1)} %get-tuple-element.68.refs_4_.refs_0_.refs_9_, f32[16,256]{1,0:T(8,128)S(1)} %get-tuple-element.69.refs_1_, f32[512,128]{1,0:T(8,128)S(1)} %get-tuple-element.71.refs_2_.refs_15_, ...), custom_call_target="tpu_custom_call" | custom-call | flops 2415000064 | bytes 1048576 | tf_op jit(solution)/shard_map/pallas_call | solution.py:649
  48.4 1.2 %collective-permute-start.11 = (f32[144,512]{1,0:T(8,128)S(1)}, f32[144,512]{1,0:T(8,128)S(1)}, u32[]{:S(2)}, u32[]{:S(2)}) collective-permute-start(f32[144,512]{1,0:T(8,128)S(1)} %get-tuple-element.72), channel_id=1, source_target_pairs={{0,4},{1,5},{2,6},{3,7},{4,0},{5,1},{6,2},{7,3},{8,12},{9,13},{10,... | collective-permute-start | bytes 884744 | tf_op jit(solution)/shard_map/ppermute | solution.py:594
  50.8 4.5 %shard_map.119 = (bf16[128,512]{1,0:T(8,128)(2,1)S(1)}, bf16[128,512]{1,0:T(8,128)(2,1)S(1)}, bf16[128,512]{1,0:T(8,128)(2,1)S(1)}, bf16[128,512]{1,0:T(8,128)(2...) custom-call(f32[136,512]{1,0:T(8,128)S(1)} %collective-permute-done.12.refs_0_, ...), custom_call_target="tpu_custom_call" | custom-call | flops 6670000128 | bytes 1048576 | tf_op jit(solution)/shard_map/pallas_call | solution.py:676
  55.3 2.7 %collective-permute-start.16 = (bf16[128,512]{1,0:T(8,128)(2,1)S(1)}, bf16[128,512]{1,0:T(8,128)(2,1)S(1)}, u32[]{:S(2)}, u32[]{:S(2)}) collective-permute-start(bf16[128,512]{1,0:T(8,128)(2,1)S(1)} %get-tuple-element.89), channel_id=1, source_target_pairs={{0,1},{1,0},{2,3},{3,2},{4,5},{5,4},{6,7},{7,6},{8,9},{9,8},{10,11... | collective-permute-start | bytes 393224 | tf_op jit(solution)/shard_map/ppermute | solution.py:594
  58.1 1.5 %collective-permute-start.18 = (bf16[128,512]{1,0:T(8,128)(2,1)S(1)}, bf16[128,512]{1,0:T(8,128)(2,1)S(1)}, u32[]{:S(2)}, u32[]{:S(2)}) collective-permute-start(bf16[128,512]{1,0:T(8,128)(2,1)S(1)} %get-tuple-element.91), channel_id=1, source_target_pairs={{0,3},{1,2},{2,1},{3,0},{4,7},{5,6},{6,5},{7,4},{8,11},{9,10},{10,... | collective-permute-start | bytes 393224 | tf_op jit(solution)/shard_map/ppermute | solution.py:594
  59.6 6.0 %collective-permute-done.11.refs_0_ = f32[144,512]{1,0:T(8,128)S(1)} collective-permute-done((f32[144,512]{1,0:T(8,128)S(1)}, f32[144,512]{1,0:T(8,128)S(1)}, u32[]{:S(2)}, u32[]{:S(2)}) %collective-permute-start.11) | collective-permute-done | bytes 294944 | tf_op jit(solution)/shard_map/ppermute | solution.py:594
  65.6 4.9 %shard_map.120 = (bf16[136,1024]{1,0:T(8,128)(2,1)S(1)}, bf16[136,1024]{1,0:T(8,128)(2,1)S(1)}, bf16[136,1024]{1,0:T(8,128)(2,1)S(1)}, bf16[136,1024]{1,0:T(8,128)(2,1)S(1)}) custom-call(f32[144,512]{1,0:T(8,128)S(1)} %collective-permute-done.11.refs_0_, f32[512,1024]{1,0:T(8,128)S(1)} %get-tuple-element.64.refs_7_.refs_0_.refs_6_.refs_1_, ...), custom_call_target="tpu_custom_call" | custom-call | flops 6670000128 | bytes 1048576 | tf_op jit(solution)/shard_map/pallas_call | solution.py:676
  71.6 2.5 %collective-permute-start.15 = (bf16[136,1024]{1,0:T(8,128)(2,1)S(1)}, bf16[136,1024]{1,0:T(8,128)(2,1)S(1)}, u32[]{:S(2)}, u32[]{:S(2)}) collective-permute-start(bf16[136,1024]{1,0:T(8,128)(2,1)S(1)} %get-tuple-element.87), channel_id=1, source_target_pairs={{0,3},{1,2},{2,1},{3,0},{4,7},{5,6},{6,5},{7,4},{8,11},{9,10},{10,... | collective-permute-start | bytes 835592 | tf_op jit(solution)/shard_map/ppermute | solution.py:594
  74.9 4.3 %collective-permute-done.13.refs_1_ = bf16[136,1024]{1,0:T(8,128)(2,1)S(1)} collective-permute-done((bf16[136,1024]{1,0:T(8,128)(2,1)S(1)}, bf16[136,1024]{1,0:T(8,128)(2,1)S(1)}, u32[]{:S(2)}, u32[]{:S(2)}) %collective-permute-start.13) | collective-permute-done | bytes 278560 | tf_op jit(solution)/shard_map/ppermute | solution.py:594
  79.2 1.9 %collective-permute-done.14.refs_2_ = bf16[136,1024]{1,0:T(8,128)(2,1)S(1)} collective-permute-done((bf16[136,1024]{1,0:T(8,128)(2,1)S(1)}, bf16[136,1024]{1,0:T(8,128)(2,1)S(1)}, u32[]{:S(2)}, u32[]{:S(2)}) %collective-permute-start.14) | collective-permute-done | bytes 278560 | tf_op jit(solution)/shard_map/ppermute | solution.py:594
  81.1 5.2 %collective-permute-done.15.refs_3_ = bf16[136,1024]{1,0:T(8,128)(2,1)S(1)} collective-permute-done((bf16[136,1024]{1,0:T(8,128)(2,1)S(1)}, bf16[136,1024]{1,0:T(8,128)(2,1)S(1)}, u32[]{:S(2)}, u32[]{:S(2)}) %collective-permute-start.15) | collective-permute-done | bytes 278560 | tf_op jit(solution)/shard_map/ppermute | solution.py:594
  86.3 1.5 %shard_map.122 = (bf16[128,4096]{1,0:T(8,128)(2,1)}, bf16[128,256]{1,0:T(8,128)(2,1)}, bf16[64,128]{1,0:T(8,128)(2,1)}) custom-call(bf16[136,1024]{1,0:T(8,128)(2,1)S(1)} %get-tuple-element.84.refs_0_, bf16[136,1024]{1,0:T(8,128)(2,1)S(1)} %collective-permute-done.13.refs_1_, ...), custom_call_target="tpu_custom_call", output_to_operand_aliasing={{0}: (4, {})} | custom-call | flops 2300000000 | bytes 1048576 | tf_op jit(solution)/shard_map/pallas_call | solution.py:685
  (35 shorter events, 7.5 us)
Async XLA Ops:
  2.6 11.6 %collective-permute-start.4 = (bf16[136,1280]{1,0:T(8,128)(2,1)S(1)}, bf16[136,1280]{1,0:T(8,128)(2,1)S(1)}, u32[]{:S(2)}, u32[]{:S(2)}) collective-permute-start(bf16[136,1280]{1,0:T(8,128)(2,1)S(1)} %get-tuple-element.54), channel_id=1, source_target_pairs={{0,1},{1,0},{2,3},{3,2},{4,5},{5,4},{6,7},{7,6},{8,9},{9,8},{10,11... | collective-permute-start | bytes 1044488 | tf_op jit(solution)/shard_map/ppermute | solution.py:594
  5.6 15.1 %collective-permute-start.5 = (bf16[136,1280]{1,0:T(8,128)(2,1)S(1)}, bf16[136,1280]{1,0:T(8,128)(2,1)S(1)}, u32[]{:S(2)}, u32[]{:S(2)}) collective-permute-start(bf16[136,1280]{1,0:T(8,128)(2,1)S(1)} %get-tuple-element.55), channel_id=1, source_target_pairs={{0,2},{1,3},{2,0},{3,1},{4,6},{5,7},{6,4},{7,5},{8,10},{9,11},{10,... | collective-permute-start | bytes 1044488 | tf_op jit(solution)/shard_map/ppermute | solution.py:594
  7.2 18.4 %collective-permute-start.6 = (bf16[136,1280]{1,0:T(8,128)(2,1)S(1)}, bf16[136,1280]{1,0:T(8,128)(2,1)S(1)}, u32[]{:S(2)}, u32[]{:S(2)}) collective-permute-start(bf16[136,1280]{1,0:T(8,128)(2,1)S(1)} %get-tuple-element.56), channel_id=1, source_target_pairs={{0,3},{1,2},{2,1},{3,0},{4,7},{5,6},{6,5},{7,4},{8,11},{9,10},{10,... | collective-permute-start | bytes 1044488 | tf_op jit(solution)/shard_map/ppermute | solution.py:594
  7.2 1.3 %collective-permute-start.7 = (bf16[16,1280]{1,0:T(8,128)(2,1)S(1)}, bf16[16,1280]{1,0:T(8,128)(2,1)S(1)}, u32[]{:S(2)}, u32[]{:S(2)}) collective-permute-start(bf16[16,1280]{1,0:T(8,128)(2,1)S(1)} %get-tuple-element.57), channel_id=1, source_target_pairs={{3,4},{11,12},{19,20},{27,28}} | collective-permute-start | bytes 122888 | tf_op jit(solution)/shard_map/ppermute | solution.py:628
  7.9 1.4 %collective-permute-start.8 = (bf16[16,1280]{1,0:T(8,128)(2,1)S(1)}, bf16[16,1280]{1,0:T(8,128)(2,1)S(1)}, u32[]{:S(2)}, u32[]{:S(2)}) collective-permute-start(bf16[16,1280]{1,0:T(8,128)(2,1)S(1)} %get-tuple-element.58), channel_id=1, source_target_pairs={{3,5},{11,13},{19,21},{27,29}} | collective-permute-start | bytes 122888 | tf_op jit(solution)/shard_map/ppermute | solution.py:628
  8.5 2.7 %collective-permute-start.9 = (bf16[16,1280]{1,0:T(8,128)(2,1)S(1)}, bf16[16,1280]{1,0:T(8,128)(2,1)S(1)}, u32[]{:S(2)}, u32[]{:S(2)}) collective-permute-start(bf16[16,1280]{1,0:T(8,128)(2,1)S(1)} %get-tuple-element.59), channel_id=1, source_target_pairs={{3,6},{11,14},{19,22},{27,30}} | collective-permute-start | bytes 122888 | tf_op jit(solution)/shard_map/ppermute | solution.py:628
  9.2 2.5 %collective-permute-start.10 = (bf16[16,1280]{1,0:T(8,128)(2,1)S(1)}, bf16[16,1280]{1,0:T(8,128)(2,1)S(1)}, u32[]{:S(2)}, u32[]{:S(2)}) collective-permute-start(bf16[16,1280]{1,0:T(8,128)(2,1)S(1)} %get-tuple-element.60), channel_id=1, source_target_pairs={{3,7},{11,15},{19,23},{27,31}} | collective-permute-start | bytes 122888 | tf_op jit(solution)/shard_map/ppermute | solution.py:628
  9.9 15.7 %copy-start.1 = (f32[1,4,4352]{2,1,0:T(4,128)S(1)}, f32[1,4,4352]{2,1,0:T(4,128)}, u32[]{:S(2)}) copy-start(f32[1,4,4352]{2,1,0:T(4,128)} %param.12) | copy-start | bytes 208900
  9.9 15.7 %copy-start.2 = (f32[1,4352]{1,0:T(1,128)S(1)}, f32[1,4352]{1,0:T(1,128)}, u32[]{:S(2)}) copy-start(f32[1,4352]{1,0:T(1,128)} %refs_9_.1) | copy-start | bytes 52228
  9.9 15.7 %copy-start.3 = (f32[1,64]{1,0:T(1,128)S(1)}, f32[1,64]{1,0:T(1,128)}, u32[]{:S(2)}) copy-start(f32[1,64]{1,0:T(1,128)} %refs_11_.2) | copy-start | bytes 772
  9.9 15.7 %copy-start.4 = (f32[1,64]{1,0:T(1,128)S(1)}, f32[1,64]{1,0:T(1,128)}, u32[]{:S(2)}) copy-start(f32[1,64]{1,0:T(1,128)} %refs_13_.3) | copy-start | bytes 772
  11.2 19.5 %collective-permute-start = (bf16[128,1024]{1,0:T(8,128)(2,1)S(1)}, bf16[128,1024]{1,0:T(8,128)(2,1)S(1)}, u32[]{:S(2)}, u32[]{:S(2)}) collective-permute-start(bf16[128,1024]{1,0:T(8,128)(2,1)S(1)} %get-tuple-element.49), channel_id=1, source_target_pairs={{8,0},{9,1},{10,2},{11,3},{12,4},{13,5},{14,6},{15,7},{16,8},{17,9... | collective-permute-start | bytes 786440 | tf_op jit(solution)/shard_map/ppermute | solution.py:602
  11.8 19.0 %collective-permute-start.1 = (bf16[128,1024]{1,0:T(8,128)(2,1)S(1)}, bf16[128,1024]{1,0:T(8,128)(2,1)S(1)}, u32[]{:S(2)}, u32[]{:S(2)}) collective-permute-start(bf16[128,1024]{1,0:T(8,128)(2,1)S(1)} %get-tuple-element.50), channel_id=1, source_target_pairs={{8,1},{9,0},{10,3},{11,2},{12,5},{13,4},{14,7},{15,6},{16,9},{17,8... | collective-permute-start | bytes 786440 | tf_op jit(solution)/shard_map/ppermute | solution.py:602
  14.2 16.5 %collective-permute-start.2 = (bf16[128,1024]{1,0:T(8,128)(2,1)S(1)}, bf16[128,1024]{1,0:T(8,128)(2,1)S(1)}, u32[]{:S(2)}, u32[]{:S(2)}) collective-permute-start(bf16[128,1024]{1,0:T(8,128)(2,1)S(1)} %get-tuple-element.51), channel_id=1, source_target_pairs={{8,2},{9,3},{10,0},{11,1},{12,6},{13,7},{14,4},{15,5},{16,10},{17,... | collective-permute-start | bytes 786440 | tf_op jit(solution)/shard_map/ppermute | solution.py:602
  20.7 13.9 %collective-permute-start.3 = (bf16[128,1024]{1,0:T(8,128)(2,1)S(1)}, bf16[128,1024]{1,0:T(8,128)(2,1)S(1)}, u32[]{:S(2)}, u32[]{:S(2)}) collective-permute-start(bf16[128,1024]{1,0:T(8,128)(2,1)S(1)} %get-tuple-element.52), channel_id=1, source_target_pairs={{8,3},{9,2},{10,1},{11,0},{12,7},{13,6},{14,5},{15,4},{16,11},{17,... | collective-permute-start | bytes 786440 | tf_op jit(solution)/shard_map/ppermute | solution.py:602
  25.7 8.9 %copy-start = (f32[1,64]{1,0:T(1,128)S(1)}, f32[1,64]{1,0:T(1,128)}, u32[]{:S(2)}) copy-start(f32[1,64]{1,0:T(1,128)} %refs_14_.3) | copy-start | bytes 772
  35.7 15.1 %collective-permute-start.12 = (f32[136,512]{1,0:T(8,128)S(1)}, f32[136,512]{1,0:T(8,128)S(1)}, u32[]{:S(2)}, u32[]{:S(2)}) collective-permute-start(f32[136,512]{1,0:T(8,128)S(1)} %get-tuple-element.77), channel_id=1, source_target_pairs={{0,4},{1,5},{2,6},{3,7},{4,0},{5,1},{6,2},{7,3},{8,12},{9,13},{10,... | collective-permute-start | bytes 835592 | tf_op jit(solution)/shard_map/ppermute | solution.py:594
  48.4 17.2 %collective-permute-start.11 = (f32[144,512]{1,0:T(8,128)S(1)}, f32[144,512]{1,0:T(8,128)S(1)}, u32[]{:S(2)}, u32[]{:S(2)}) collective-permute-start(f32[144,512]{1,0:T(8,128)S(1)} %get-tuple-element.72), channel_id=1, source_target_pairs={{0,4},{1,5},{2,6},{3,7},{4,0},{5,1},{6,2},{7,3},{8,12},{9,13},{10,... | collective-permute-start | bytes 884744 | tf_op jit(solution)/shard_map/ppermute | solution.py:594
  55.3 16.2 %collective-permute-start.16 = (bf16[128,512]{1,0:T(8,128)(2,1)S(1)}, bf16[128,512]{1,0:T(8,128)(2,1)S(1)}, u32[]{:S(2)}, u32[]{:S(2)}) collective-permute-start(bf16[128,512]{1,0:T(8,128)(2,1)S(1)} %get-tuple-element.89), channel_id=1, source_target_pairs={{0,1},{1,0},{2,3},{3,2},{4,5},{5,4},{6,7},{7,6},{8,9},{9,8},{10,11... | collective-permute-start | bytes 393224 | tf_op jit(solution)/shard_map/ppermute | solution.py:594
  58.1 16.0 %collective-permute-start.17 = (bf16[128,512]{1,0:T(8,128)(2,1)S(1)}, bf16[128,512]{1,0:T(8,128)(2,1)S(1)}, u32[]{:S(2)}, u32[]{:S(2)}) collective-permute-start(bf16[128,512]{1,0:T(8,128)(2,1)S(1)} %get-tuple-element.90), channel_id=1, source_target_pairs={{0,2},{1,3},{2,0},{3,1},{4,6},{5,7},{6,4},{7,5},{8,10},{9,11},{10,... | collective-permute-start | bytes 393224 | tf_op jit(solution)/shard_map/ppermute | solution.py:594
  58.1 16.0 %collective-permute-start.18 = (bf16[128,512]{1,0:T(8,128)(2,1)S(1)}, bf16[128,512]{1,0:T(8,128)(2,1)S(1)}, u32[]{:S(2)}, u32[]{:S(2)}) collective-permute-start(bf16[128,512]{1,0:T(8,128)(2,1)S(1)} %get-tuple-element.91), channel_id=1, source_target_pairs={{0,3},{1,2},{2,1},{3,0},{4,7},{5,6},{6,5},{7,4},{8,11},{9,10},{10,... | collective-permute-start | bytes 393224 | tf_op jit(solution)/shard_map/ppermute | solution.py:594
  70.5 8.7 %collective-permute-start.13 = (bf16[136,1024]{1,0:T(8,128)(2,1)S(1)}, bf16[136,1024]{1,0:T(8,128)(2,1)S(1)}, u32[]{:S(2)}, u32[]{:S(2)}) collective-permute-start(bf16[136,1024]{1,0:T(8,128)(2,1)S(1)} %get-tuple-element.85), channel_id=1, source_target_pairs={{0,1},{1,0},{2,3},{3,2},{4,5},{5,4},{6,7},{7,6},{8,9},{9,8},{10,11... | collective-permute-start | bytes 835592 | tf_op jit(solution)/shard_map/ppermute | solution.py:594
  71.6 9.6 %collective-permute-start.14 = (bf16[136,1024]{1,0:T(8,128)(2,1)S(1)}, bf16[136,1024]{1,0:T(8,128)(2,1)S(1)}, u32[]{:S(2)}, u32[]{:S(2)}) collective-permute-start(bf16[136,1024]{1,0:T(8,128)(2,1)S(1)} %get-tuple-element.86), channel_id=1, source_target_pairs={{0,2},{1,3},{2,0},{3,1},{4,6},{5,7},{6,4},{7,5},{8,10},{9,11},{10,... | collective-permute-start | bytes 835592 | tf_op jit(solution)/shard_map/ppermute | solution.py:594
  71.6 14.7 %collective-permute-start.15 = (bf16[136,1024]{1,0:T(8,128)(2,1)S(1)}, bf16[136,1024]{1,0:T(8,128)(2,1)S(1)}, u32[]{:S(2)}, u32[]{:S(2)}) collective-permute-start(bf16[136,1024]{1,0:T(8,128)(2,1)S(1)} %get-tuple-element.87), channel_id=1, source_target_pairs={{0,3},{1,2},{2,1},{3,0},{4,7},{5,6},{6,5},{7,4},{8,11},{9,10},{10,... | collective-permute-start | bytes 835592 | tf_op jit(solution)/shard_map/ppermute | solution.py:594
